TPU v7x, 32 devices: a whole 2x2x4 slice. The times are simulated.
32 devices in a mesh: freq: 4 (over z), tm: 4 (over y, x), grp: 2 (over core).
Axes of the slice: x: 2, y: 2, z: 4, core: 2. Of those that a mesh axis runs over, the one named last changes fastest.
Arguments:
- inputs: bfloat16 [10, 1280, 768], P('grp', ('freq', 'tm')), may hold values from -6 to 6
- gain_one: float32 [768], replicated, may hold values from 0.5 to 1.5
- shift_one: float32 [768], replicated, may hold values from -1.8 to 1.8
- w_qkv: bfloat16 [768, 2304], replicated, may hold values from -0.21875 to 0.21875
- bias_query: float32 [768], replicated, may hold values from -1.8 to 1.8
- bias_value: float32 [768], replicated, may hold values from -0.18 to 0.18
- w_out: bfloat16 [768, 768], replicated, may hold values from -4 to 4
- bias_out: float32 [768], replicated, may hold values from -0.6 to 0.6
- gain_two: float32 [768], replicated, may hold values from 0.5 to 1.5
- shift_two: float32 [768], replicated, may hold values from -1.8 to 1.8
- w_up: bfloat16 [768, 3072], replicated, may hold values from -0.21875 to 0.21875
- bias_up: float32 [3072], replicated, may hold values from -1.8 to 1.8
- w_down: bfloat16 [3072, 768], replicated, may hold values from -0.109375 to 0.109375
- bias_down: float32 [768], replicated, may hold values from -0.6 to 0.6
- cotangent: bfloat16 [10, 1280, 768], P('grp', ('freq', 'tm')), may hold values from -6 to 6
Outputs:
- block_out: float32 [10, 1280, 768], P('grp', ('freq', 'tm'))
- grad_inputs: float32 [10, 1280, 768], P('grp', ('freq', 'tm'))
- grad_gain_one: float32 [768], P(('freq', 'tm', 'grp'))
- grad_shift_one: float32 [768], P(('freq', 'tm', 'grp'))
- grad_w_qkv: float32 [768, 2304], P(('freq', 'tm', 'grp'))
- grad_bias_query: float32 [768], P(('freq', 'tm', 'grp'))
- grad_bias_value: float32 [768], P(('freq', 'tm', 'grp'))
- grad_w_out: float32 [768, 768], P(('freq', 'tm', 'grp'))
- grad_bias_out: float32 [768], P(('freq', 'tm', 'grp'))
- grad_gain_two: float32 [768], P(('freq', 'tm', 'grp'))
- grad_shift_two: float32 [768], P(('freq', 'tm', 'grp'))
- grad_w_up: float32 [768, 3072], P(('freq', 'tm', 'grp'))
- grad_bias_up: float32 [3072], P(('freq', 'tm', 'grp'))
- grad_w_down: float32 [3072, 768], P(('freq', 'tm', 'grp'))
- grad_bias_down: float32 [768], P(('freq', 'tm', 'grp'))
All inputs are finite; a program needn't handle non-finite values.
Results may differ from a plain program's by a relative error of at most 0.019.
Values may be sent and summed in bfloat16 or wider, within the bound.
No kernel may reach another device: no remote copies, remote signals or barrier semaphores. Data moves between devices by JAX's collectives and lax.ppermute only.
A program may use at most 256 MiB of HBM per device.

v0:
```python
import jax
import jax.numpy as jnp
from jax import lax
from jax.sharding import PartitionSpec as P

HD = 64


NORM_EPS = 1e-06


def layer_norm(tensor, gain_vec, shift_vec):
    row_mean = jnp.mean(tensor, axis=-1, keepdims=True)
    centered = tensor - row_mean
    variance = jnp.mean(centered * centered, axis=-1, keepdims=True)
    return centered * lax.rsqrt(variance + NORM_EPS) * gain_vec + shift_vec


def gelu_exact(tensor):
    return jax.nn.gelu(tensor, approximate=False)


def row_contract(left, right):
    return lax.dot_general(
        left, right, (((0,), (0,)), ((), ())), preferred_element_type=jnp.float32
    )


def col_contract(left, right):
    return lax.dot_general(
        left, right, (((1,), (1,)), ((), ())), preferred_element_type=jnp.float32
    )


def pair_split(tensor):
    clip_count, row_count, model_width = tensor.shape
    return tensor.reshape(clip_count, row_count, model_width // (2 * HD), 2 * HD).transpose(
        2, 0, 1, 3
    )


def pair_join(tensor):
    pair_count, clip_count, row_count, lane_count = tensor.shape
    return tensor.transpose(1, 2, 0, 3).reshape(clip_count, row_count, pair_count * lane_count)


def head_view(tensor):
    clip_count, row_count, lane_count = tensor.shape
    return tensor.reshape(clip_count, row_count, lane_count // HD, HD)


def mixed_product(spec, left, right):
    return jnp.einsum(spec, left, right, preferred_element_type=jnp.float32)


def attend_pair(operands):
    query_blk, key_blk, value_blk = operands
    head_scale = HD ** (-0.5)
    scores = mixed_product("cqhe,ckhe->chqk", head_view(query_blk), head_view(key_blk)) * head_scale
    row_max = jnp.max(scores, axis=-1, keepdims=True)
    log_total = row_max + jnp.log(jnp.sum(jnp.exp(scores - row_max), axis=-1, keepdims=True))
    weights = jnp.exp(scores - log_total).astype(jnp.bfloat16)
    mixed_heads = mixed_product("chqk,ckhe->cqhe", weights, head_view(value_blk))
    return (mixed_heads.reshape(query_blk.shape), log_total[..., 0])


def full_side(operands):
    query_blk, key_blk, value_blk, grad_blk, log_total = operands
    head_scale = HD ** (-0.5)
    scores = mixed_product("cqhe,ckhe->chqk", head_view(query_blk), head_view(key_blk)) * head_scale
    prob_full = jnp.exp(scores - log_total[..., None])
    grad_probs = mixed_product("cqhe,ckhe->chqk", head_view(grad_blk), head_view(value_blk))
    inner_prod = jnp.sum(prob_full * grad_probs, axis=-1)
    grad_scores = (prob_full * (grad_probs - inner_prod[..., None])).astype(jnp.bfloat16)
    grad_query = mixed_product("chqk,ckhe->cqhe", grad_scores, head_view(key_blk)) * head_scale
    grad_key = mixed_product("chqk,cqhe->ckhe", grad_scores, head_view(query_blk)) * head_scale
    grad_value = mixed_product(
        "chqk,cqhe->ckhe", prob_full.astype(jnp.bfloat16), head_view(grad_blk)
    )
    return (
        grad_query.reshape(query_blk.shape),
        grad_key.reshape(key_blk.shape),
        grad_value.reshape(key_blk.shape),
    )


def local(
    inputs,
    gain_one,
    shift_one,
    w_qkv,
    bias_query,
    bias_value,
    w_out,
    bias_out,
    gain_two,
    shift_two,
    w_up,
    bias_up,
    w_down,
    bias_down,
    cotangent,
):
    clip_count, row_count, model_width = inputs.shape
    flat_rows = clip_count * row_count
    local_shape = (clip_count, row_count, model_width)
    resid_in = inputs.astype(jnp.float32).reshape(flat_rows, model_width)
    normed_full, norm_back_one = jax.vjp(layer_norm, resid_in, gain_one, shift_one)
    normed_one = normed_full.astype(jnp.bfloat16)
    projected = jnp.dot(normed_one, w_qkv, preferred_element_type=jnp.float32)
    queries = (projected[:, :model_width] + bias_query).astype(jnp.bfloat16).reshape(local_shape)
    key_own = projected[:, model_width : 2 * model_width].astype(jnp.bfloat16).reshape(local_shape)
    value_own = (
        (projected[:, 2 * model_width :] + bias_value).astype(jnp.bfloat16).reshape(local_shape)
    )
    all_keys, all_values = (
        lax.all_gather(key_own, ("freq", "tm"), axis=1, tiled=True),
        lax.all_gather(value_own, ("freq", "tm"), axis=1, tiled=True),
    )
    query_pairs = pair_split(queries)
    key_pairs = pair_split(all_keys)
    value_pairs = pair_split(all_values)
    mixed_pairs, log_pairs = lax.map(attend_pair, (query_pairs, key_pairs, value_pairs))
    attended = pair_join(mixed_pairs).astype(jnp.bfloat16).reshape(flat_rows, model_width)
    resid_mid = resid_in + jnp.dot(attended, w_out, preferred_element_type=jnp.float32) + bias_out
    normed_mid, norm_back_two = jax.vjp(layer_norm, resid_mid, gain_two, shift_two)
    normed_two = normed_mid.astype(jnp.bfloat16)
    hidden_pre = jnp.dot(normed_two, w_up, preferred_element_type=jnp.float32) + bias_up
    activated, gelu_back = jax.vjp(gelu_exact, hidden_pre)
    activated_low = activated.astype(jnp.bfloat16)
    block_out = (
        resid_mid + jnp.dot(activated_low, w_down, preferred_element_type=jnp.float32) + bias_down
    )
    grad_out = cotangent.reshape(flat_rows, model_width)
    grad_w_down = row_contract(activated_low, grad_out)
    grad_bias_down = jnp.sum(grad_out.astype(jnp.float32), axis=0)
    grad_act = col_contract(grad_out, w_down)
    grad_pre = gelu_back(grad_act)[0].astype(jnp.bfloat16)
    grad_w_up = row_contract(normed_two, grad_pre)
    grad_bias_up = jnp.sum(grad_pre.astype(jnp.float32), axis=0)
    grad_norm_two = col_contract(grad_pre, w_up)
    grad_mid_part, grad_gain_two, grad_shift_two = norm_back_two(grad_norm_two)
    grad_mid = grad_out.astype(jnp.float32) + grad_mid_part
    grad_branch = grad_mid.astype(jnp.bfloat16)
    grad_w_out = row_contract(attended, grad_branch)
    grad_bias_out = jnp.sum(grad_branch.astype(jnp.float32), axis=0)
    grad_attended = col_contract(grad_branch, w_out).astype(jnp.bfloat16).reshape(local_shape)
    grad_pairs = pair_split(grad_attended)
    gq_pairs, gk_pairs, gv_pairs = lax.map(
        full_side, (query_pairs, key_pairs, value_pairs, grad_pairs, log_pairs)
    )
    grad_key_sum, grad_value_sum = (
        lax.psum_scatter(
            pair_join(gk_pairs).astype(jnp.bfloat16),
            ("freq", "tm"),
            scatter_dimension=1,
            tiled=True,
        ).astype(jnp.float32),
        lax.psum_scatter(
            pair_join(gv_pairs).astype(jnp.bfloat16),
            ("freq", "tm"),
            scatter_dimension=1,
            tiled=True,
        ).astype(jnp.float32),
    )
    grad_queries = pair_join(gq_pairs).astype(jnp.bfloat16).reshape(flat_rows, model_width)
    grad_keys = grad_key_sum.astype(jnp.bfloat16).reshape(flat_rows, model_width)
    grad_values = grad_value_sum.astype(jnp.bfloat16).reshape(flat_rows, model_width)
    grad_proj = jnp.concatenate([grad_queries, grad_keys, grad_values], axis=1)
    grad_w_qkv = row_contract(normed_one, grad_proj)
    grad_bias_query = jnp.sum(grad_queries.astype(jnp.float32), axis=0)
    grad_bias_value = jnp.sum(grad_values.astype(jnp.float32), axis=0)
    grad_norm_one = col_contract(grad_proj, w_qkv)
    grad_in_part, grad_gain_one, grad_shift_one = norm_back_one(grad_norm_one)
    grad_inputs = grad_mid + grad_in_part
    summed = (
        lax.psum_scatter(grad_gain_one, ("freq", "tm", "grp"), scatter_dimension=0, tiled=True),
        lax.psum_scatter(grad_shift_one, ("freq", "tm", "grp"), scatter_dimension=0, tiled=True),
        lax.psum_scatter(grad_w_qkv, ("freq", "tm", "grp"), scatter_dimension=0, tiled=True),
        lax.psum_scatter(grad_bias_query, ("freq", "tm", "grp"), scatter_dimension=0, tiled=True),
        lax.psum_scatter(grad_bias_value, ("freq", "tm", "grp"), scatter_dimension=0, tiled=True),
        lax.psum_scatter(grad_w_out, ("freq", "tm", "grp"), scatter_dimension=0, tiled=True),
        lax.psum_scatter(grad_bias_out, ("freq", "tm", "grp"), scatter_dimension=0, tiled=True),
        lax.psum_scatter(grad_gain_two, ("freq", "tm", "grp"), scatter_dimension=0, tiled=True),
        lax.psum_scatter(grad_shift_two, ("freq", "tm", "grp"), scatter_dimension=0, tiled=True),
        lax.psum_scatter(grad_w_up, ("freq", "tm", "grp"), scatter_dimension=0, tiled=True),
        lax.psum_scatter(grad_bias_up, ("freq", "tm", "grp"), scatter_dimension=0, tiled=True),
        lax.psum_scatter(grad_w_down, ("freq", "tm", "grp"), scatter_dimension=0, tiled=True),
        lax.psum_scatter(grad_bias_down, ("freq", "tm", "grp"), scatter_dimension=0, tiled=True),
    )
    return (
        block_out.reshape(local_shape),
        grad_inputs.reshape(local_shape),
        summed[0],
        summed[1],
        summed[2],
        summed[3],
        summed[4],
        summed[5],
        summed[6],
        summed[7],
        summed[8],
        summed[9],
        summed[10],
        summed[11],
        summed[12],
    )


def solution(mesh):
    placed = (
        P("grp", ("freq", "tm"), None),
        P(),
        P(),
        P(),
        P(),
        P(),
        P(),
        P(),
        P(),
        P(),
        P(),
        P(),
        P(),
        P(),
        P("grp", ("freq", "tm"), None),
    )
    return jax.shard_map(
        local,
        mesh=mesh,
        in_specs=placed,
        out_specs=(
            P("grp", ("freq", "tm"), None),
            P("grp", ("freq", "tm"), None),
            P(("freq", "tm", "grp")),
            P(("freq", "tm", "grp")),
            P(("freq", "tm", "grp"), None),
            P(("freq", "tm", "grp")),
            P(("freq", "tm", "grp")),
            P(("freq", "tm", "grp"), None),
            P(("freq", "tm", "grp")),
            P(("freq", "tm", "grp")),
            P(("freq", "tm", "grp")),
            P(("freq", "tm", "grp"), None),
            P(("freq", "tm", "grp")),
            P(("freq", "tm", "grp"), None),
            P(("freq", "tm", "grp")),
        ),
        check_vma=False,
    )
```

profile of v0, /device:TPU:0, one launch (start us, length us, event | category | flops | bytes accessed | tf_op | source)
XLA Modules:
  0.0 1359.0 jit_solution(13765371813833233255)
XLA Ops:
  17.2 2.9 fusion.14
  25.3 120.8 %all-gather.5.cloned.1.call-done = bf16[5,1280,768]{2,1,0:T(8,128)(2,1)} async-done(((bf16[5,80,768]{2,1,0:T(8,128)(2,1)}), bf16[5,1280,768]{2,1,0:T(8,128)(2,1)}) %all-gather.5.cloned.1.call-update) | async-done | bytes 9830416 | tf_op jit(solution)/shard_map/all_gather | solution.py:117
  146.1 13.9 %copy.48 = bf16[5,1280,768]{1,2,0:T(8,128)(2,1)} copy(bf16[5,1280,768]{2,1,0:T(8,128)(2,1)} %all-gather.5.cloned.1.call-done) | data formatting | bytes 19660800 | tf_op jit(solution)/shard_map/all_gather | solution.py:117
  160.0 8.7 copy.51
  168.6 104.3 %all-gather.3.cloned.1.call-done = bf16[5,1280,768]{2,1,0:T(8,128)(2,1)} async-done(((bf16[5,80,768]{2,1,0:T(8,128)(2,1)}), bf16[5,1280,768]{2,1,0:T(8,128)(2,1)}) %all-gather.3.cloned.1.call-update) | async-done | bytes 9830416 | tf_op jit(solution)/shard_map/all_gather | solution.py:118
  273.0 13.8 %copy.47 = bf16[5,1280,768]{1,2,0:T(8,128)(2,1)} copy(bf16[5,1280,768]{2,1,0:T(8,128)(2,1)} %all-gather.3.cloned.1.call-done) | data formatting | bytes 19660800 | tf_op jit(solution)/shard_map/all_gather | solution.py:118
  286.8 8.6 copy.49
  296.6 40.7 %while.26 = (s32[]{:T(128)}, bf16[6,5,80,128]{2,3,1,0:T(8,128)(2,1)}, f32[6,5,2,80]{3,2,1,0:T(2,128)}, bf16[6,5,1280,128]{2,3,1,0:T(8,128)(2,1)}, bf16[6,5,80,12...) while((s32[]{:T(128)}, bf16[6,5,80,128]{2,3,1,0:T(8,128)(2,1)}, ...), condition=%wide.region_5.6_spmd, body=%wide.region_2.5_spmd.sunk | while | flops 268287200 | bytes 22821860 | solution.py:123
  342.7 4.7 fusion.28
  347.5 16.0 %convert_reduce_fusion = (f32[3072]{0:T(1024)}, bf16[400,3072]{1,0:T(8,128)(2,1)S(1)}, f32[400,3072]{1,0:T(8,128)}) fusion(f32[400,3072]{1,0:T(8,128)S(1)} %fusion.28, f32[3072]{0:T(1024)S(1)} %copy-done.20, bf16[400,768]{1,0:T(8,128)(2,1)S(1)} %bitcast.197, bf16[3072,768]{1,0:T(8,128)(2,1)S(1)} %bitcast.219), kind=kOutput, calls=%fused_computation.30 | convolution fusion | flops 1979593728 | bytes 17645568 | tf_op jit(solution)/shard_map/dot_general | solution.py:30
  363.5 2.9 multiply_reduce_fusion.1
  377.3 77.4 %while.27 = (s32[]{:T(128)}, bf16[6,5,80,128]{2,3,1,0:T(8,128)(2,1)}, bf16[6,5,1280,128]{2,3,0,1:T(8,128)(2,1)}, bf16[6,5,1280,128]{2,3,0,1:T(8,128)(2,1)}, bf16...) while((s32[]{:T(128)}, ...), condition=%wide.region_12.13_spmd, body=%wide.region_10.12_spmd.sunk | while | flops 665292032 | bytes 53223176 | solution.py:149
  454.7 19.6 %copy.62 = bf16[5,1280,768]{2,0,1:T(8,128)(2,1)} copy(bf16[5,1280,768]{1,2,0:T(8,128)(2,1)} %bitcast.192) | data formatting | bytes 19660800
  474.4 12.5 copy.91
  487.0 19.7 %copy.64 = bf16[5,1280,768]{2,0,1:T(8,128)(2,1)} copy(bf16[5,1280,768]{1,2,0:T(8,128)(2,1)} %bitcast.191) | data formatting | bytes 19660800
  506.7 12.8 copy.92
  519.6 3.6 fusion.19
  523.4 8.7 fusion.27
  532.2 5.3 multiply_convert_fusion.1
  539.0 5.1 fusion.37
  548.7 110.9 %reduce-scatter.19.cloned.1.call-done = bf16[80,3840]{1,0:T(8,128)(2,1)} async-done(((bf16[1280,3840]{1,0:T(8,128)(2,1)}), bf16[80,3840]{1,0:T(8,128)(2,1)}) %reduce-scatter.19.cloned.1.call-update) | async-done | bytes 614416
  664.3 175.4 %reduce-scatter.21.cloned.1.call-done = bf16[80,3840]{1,0:T(8,128)(2,1)} async-done(((bf16[1280,3840]{1,0:T(8,128)(2,1)}), bf16[80,3840]{1,0:T(8,128)(2,1)}) %reduce-scatter.21.cloned.1.call-update) | async-done | bytes 614416
  844.3 6.3 fusion.17
  854.6 6.6 fusion.13
  865.7 5.4 fusion.29
  871.1 41.3 %all-reduce.9 = (f32[768]{0:T(1024)}, f32[768]{0:T(1024)}, f32[768]{0:T(1024)}, f32[768]{0:T(1024)}, f32[768]{0:T(1024)}, /*index=5*/f32[768]{0:T(1024)}, f32[768]{0:T(1024)}, f32[3072]{0:T(1024)}, f32[768]{0:T(1024)}) all-reduce(f32[768]{0:T(1024)} %get-tuple-element.137, ...), channel_id=4, replica_groups=mesh['freq'=4,'tm'=4,'grp'=2] {'freq','tm','grp'}, use_global_device_ids=true, to_apply=%region_18.19.clone | all-reduce | flops 9216 | bytes 73728
  924.3 2.8 add_add_fusion
  928.6 3.1 add_add_fusion.2
  931.8 12.0 reduce-scatter.13.cloned.1.call-done
  943.8 141.9 %reduce-scatter.15.cloned.1.call-done = f32[24,3072]{1,0:T(8,128)} async-done(((f32[768,3072]{1,0:T(8,128)}), f32[24,3072]{1,0:T(8,128)}) %reduce-scatter.15.cloned.1.call-update) | async-done | bytes 294928 | tf_op jit(solution)/shard_map/reduce_scatter | solution.py:186
  1085.6 141.2 %reduce-scatter.17.cloned.1.call-done = f32[96,768]{1,0:T(8,128)} async-done(((f32[3072,768]{1,0:T(8,128)}), f32[96,768]{1,0:T(8,128)}) %reduce-scatter.17.cloned.1.call-update) | async-done | bytes 294928 | tf_op jit(solution)/shard_map/reduce_scatter | solution.py:188
  1226.9 125.1 %reduce-scatter.11.cloned.1.call-done = f32[24,2304]{1,0:T(8,128)} async-done(((f32[768,2304]{1,0:T(8,128)}), f32[24,2304]{1,0:T(8,128)}) %reduce-scatter.11.cloned.1.call-update) | async-done | bytes 221200 | tf_op jit(solution)/shard_map/reduce_scatter | solution.py:179
  (257 shorter events, 187.7 us)
Async XLA Ops:
  7.2 5.5 copy-start
  7.2 138.9 %all-gather.5.cloned.1.call-start = ((), (), s32[]{:S(2)}) async-start(), calls=%async_computation.7 | async-start | bytes 10444800 | tf_op jit(solution)/shard_map/all_gather | solution.py:117
  8.7 5.6 copy-start.15
  10.2 4.1 copy-start.13
  12.7 4.5 copy-start.22
  12.7 4.5 copy-start.23
  17.2 255.8 %all-gather.3.cloned.1.call-start = ((), (), s32[]{:S(2)}) async-start(), calls=%async_computation.6 | async-start | bytes 10444800 | tf_op jit(solution)/shard_map/all_gather | solution.py:118
  20.2 639.5 %reduce-scatter.19.cloned.1.call-start = ((), (), s32[]{:S(2)}) async-start(), calls=%async_computation.12 | async-start | bytes 10444800
  296.5 43.2 %copy-start.26 = (f32[768]{0:T(1024)S(1)}, f32[768]{0:T(1024)}, u32[]{:S(2)}) copy-start(f32[768]{0:T(1024)} %param.26) | copy-start | bytes 9220
  339.7 2.9 copy-start.27
  339.7 7.7 slice-start.2
  342.3 24.1 %copy-start.5 = (f32[400,768]{1,0:T(8,128)}, f32[400,768]{1,0:T(8,128)S(1)}, u32[]{:S(2)}) copy-start(f32[400,768]{1,0:T(8,128)S(1)} %get-tuple-element.199) | copy-start | bytes 3686404
  342.7 23.8 %copy-start.21 = (f32[400]{0:T(512)}, f32[400]{0:T(512)S(1)}, u32[]{:S(2)}) copy-start(f32[400]{0:T(512)S(1)} %fusion.24) | copy-start | bytes 4804
  342.7 4.7 copy-start.2
  342.7 4.7 copy-start.20
  342.7 4.7 slice-start.3
  342.7 20.8 %slice-start = ((s8[4718592]{0:T(1024)(128)(4,1)}), s8[4194304]{0:T(1024)(128)(4,1)S(1)}, s32[]{:S(2)}) async-start(s8[4718592]{0:T(1024)(128)(4,1)} %bitcast.216), calls=%async_computation.14 | async-start | bytes 8388608
  347.4 16.1 %copy-start.4 = (f32[400,3072]{1,0:T(8,128)}, f32[400,3072]{1,0:T(8,128)S(1)}, u32[]{:S(2)}) copy-start(f32[400,3072]{1,0:T(8,128)S(1)} %fusion.28) | copy-start | bytes 14745604
  347.4 16.0 %slice-start.1 = ((s8[4718592]{0:T(1024)(128)(4,1)}), s8[524288]{0:T(1024)(128)(4,1)S(1)}, s32[]{:S(2)}) async-start(s8[4718592]{0:T(1024)(128)(4,1)} %bitcast.216), calls=%async_computation.15 | async-start | bytes 1048576
  366.4 3.4 copy-start.25
  486.9 352.8 %reduce-scatter.21.cloned.1.call-start = ((), (), s32[]{:S(2)}) async-start(), calls=%async_computation.13 | async-start | bytes 10444800
  519.5 424.2 %reduce-scatter.13.cloned.1.call-start = ((), (), s32[]{:S(2)}) async-start(), calls=%async_computation.9 | async-start | bytes 2433024 | tf_op jit(solution)/shard_map/reduce_scatter | solution.py:182
  523.2 562.4 %reduce-scatter.15.cloned.1.call-start = ((), (), s32[]{:S(2)}) async-start(), calls=%async_computation.10 | async-start | bytes 9732096 | tf_op jit(solution)/shard_map/reduce_scatter | solution.py:186
  532.2 694.7 %reduce-scatter.17.cloned.1.call-start = ((), (), s32[]{:S(2)}) async-start(), calls=%async_computation.11 | async-start | bytes 9732096 | tf_op jit(solution)/shard_map/reduce_scatter | solution.py:188
  532.2 6.8 copy-start.3
  544.1 807.9 %reduce-scatter.11.cloned.1.call-start = ((), (), s32[]{:S(2)}) async-start(), calls=%async_computation.8 | async-start | bytes 7299072 | tf_op jit(solution)/shard_map/reduce_scatter | solution.py:179
  850.7 3.9 copy-start.28
  854.6 11.1 copy-start.16
  854.6 11.1 copy-start.18
  854.6 11.1 copy-start.19
  865.7 58.0 %copy-start.14 = (f32[400]{0:T(512)S(1)}, f32[400]{0:T(512)}, u32[]{:S(2)}) copy-start(f32[400]{0:T(512)} %copy-done.13) | copy-start | bytes 4804
  871.1 57.6 %copy-start.12 = (f32[400]{0:T(512)S(1)}, f32[400]{0:T(512)}, u32[]{:S(2)}) copy-start(f32[400]{0:T(512)} %copy-done.11) | copy-start | bytes 4804
  (10 other events, 18.0 us)
Sparse Core Ops, SparseCore 0:
  17.3 128.7 all-gather.4
  148.7 124.1 all-gather.2
  487.0 172.5 reduce-scatter.18
  666.2 173.4 reduce-scatter.20
  845.4 98.2 reduce-scatter.12
  951.1 134.4 reduce-scatter.14
  1092.1 134.7 reduce-scatter.16
  1234.1 117.8 reduce-scatter.10
where the time goes:
time: 1370 us; the launch traced here: 1360 us
  waiting for transfers between devices  932 us (68%)
  local copies, waits for them, and re-layouts  230 us (17%)
  matrix products  99.4 us (7%)
  blocking collectives  41.3 us (3%)
  other arithmetic  40.1 us (3%)
  between operations  14.8 us (1%)
    unnamed x10, waiting for transfers between devices  287 us
    reduce_scatter x1, waiting for transfers between devices, local(): lax.psum_scatter(grad_w_up, ('freq', 'tm', 'grp'), scatter_dimension=0, t...  142 us
    reduce_scatter x1, waiting for transfers between devices, local(): lax.psum_scatter(grad_w_down, ('freq', 'tm', 'grp'), scatter_dimension=0,...  141 us
    reduce_scatter x1, waiting for transfers between devices, local(): lax.psum_scatter(grad_w_qkv, ('freq', 'tm', 'grp'), scatter_dimension=0,...  125 us
    all_gather x1, waiting for transfers between devices, local(): lax.all_gather(key_own, ('freq', 'tm'), axis=1, tiled=True)  121 us
    all_gather x1, waiting for transfers between devices, local(): lax.all_gather(value_own, ('freq', 'tm'), axis=1, tiled=True)  104 us
    unnamed x85, local copies, waits for them, and re-layouts  91.7 us
    dynamic_slice x36, local copies, waits for them, and re-layouts, local(): lax.map(attend_pair, (query_pairs, key_pairs, value_pairs))  48.1 us
  transfers between devices with their start and end apart: 8, of which 8 were waited for; matrix products, arithmetic and copies ran while one was open for 11% of the time, Pallas kernels for 0%

commit v1 on v0

v1 whole, which is shorter than its diff:
```python
import functools

import jax
import jax.numpy as jnp
from jax import lax
from jax.experimental import pallas as pl
from jax.experimental.pallas import tpu as pltpu
from jax.sharding import PartitionSpec as P

HD = 64
NORM_EPS = 1e-06
BF = jnp.bfloat16
F32 = jnp.float32
ALL = ("freq", "tm", "grp")
VMEM_LIMIT = 60 * 1024 * 1024


def nn(a, b):
    return lax.dot_general(a, b, (((1,), (0,)), ((), ())), preferred_element_type=F32)


def nt_dot(a, b):
    return lax.dot_general(a, b, (((1,), (1,)), ((), ())), preferred_element_type=F32)


def tn_dot(a, b):
    return lax.dot_general(a, b, (((0,), (0,)), ((), ())), preferred_element_type=F32)


def normalize(x):
    mean = jnp.mean(x, axis=-1, keepdims=True)
    centered = x - mean
    var = jnp.mean(centered * centered, axis=-1, keepdims=True)
    rstd = lax.rsqrt(var + NORM_EPS)
    return centered * rstd, rstd


def norm_back(e, n, rstd, gain):
    eg = e * gain
    return rstd * (
        eg - jnp.mean(eg, axis=-1, keepdims=True) - n * jnp.mean(eg * n, axis=-1, keepdims=True)
    )


def colsum(x):
    return jnp.sum(x, axis=0, keepdims=True)


def low_lanes(rows):
    return lax.broadcasted_iota(jnp.int32, (rows, 2 * HD), 1) < HD


def swap_halves(x):
    return pltpu.roll(x, HD, 1)


def slot_of(head, nf, nt):
    per = -(-(12) // nf)
    return (head // per) * nt + head % per


def params(count=1):
    return pltpu.CompilerParams(
        dimension_semantics=("arbitrary",) * count, vmem_limit_bytes=VMEM_LIMIT
    )


def full(shape):
    return pl.BlockSpec(shape, lambda *_: (0,) * len(shape))


def cost(flops, nbytes):
    return pl.CostEstimate(flops=int(flops), bytes_accessed=int(nbytes), transcendentals=0)


def ln_kernel(x_ref, g_ref, s_ref, n_ref):
    n, _ = normalize(x_ref[...].astype(F32))
    n_ref[...] = (n * g_ref[...] + s_ref[...]).astype(BF)


def ln_call(x, gain, shift):
    return pl.pallas_call(
        ln_kernel,
        out_shape=jax.ShapeDtypeStruct(x.shape, BF),
        compiler_params=pltpu.CompilerParams(vmem_limit_bytes=VMEM_LIMIT),
        cost_estimate=cost(x.size * 10, x.size * 4),
        name="ln_one",
    )(x, gain, shift)


def q5_kernel(nf, nt, x_ref, g_ref, s_ref, w_ref, bq_ref, bv_ref, n_ref, pack_ref):
    rows, width = x_ref.shape
    half = rows // 2
    hat, _ = normalize(x_ref[...].astype(F32))
    n = (hat * g_ref[...] + s_ref[...]).astype(BF)
    n_ref[...] = n
    low = low_lanes(half)
    pack_ref[...] = jnp.zeros_like(pack_ref)
    for part in range(3):
        proj = nn(n, w_ref[:, part * width : (part + 1) * width])
        if part == 0:
            proj = (proj + bq_ref[...]) * (HD**-0.5)
        if part == 2:
            proj = proj + bv_ref[...]
        for pair in range(width // (2 * HD)):
            blk = proj[:, pair * 2 * HD : (pair + 1) * 2 * HD]
            top, bot = blk[:half], blk[half:]
            even = jnp.where(low, top, swap_halves(bot))
            odd = jnp.where(low, swap_halves(top), bot)
            lanes = slice(part * 2 * HD, (part + 1) * 2 * HD)
            pack_ref[slot_of(2 * pair, nf, nt), :, lanes] = even.astype(BF)
            pack_ref[slot_of(2 * pair + 1, nf, nt), :, lanes] = odd.astype(BF)


def q5_call(nf, nt, x, gain, shift, w, bq, bv):
    rows, width = x.shape
    return pl.pallas_call(
        functools.partial(q5_kernel, nf, nt),
        out_shape=(
            jax.ShapeDtypeStruct((rows, width), BF),
            jax.ShapeDtypeStruct((nf * nt, rows // 2, 6 * HD), BF),
        ),
        compiler_params=pltpu.CompilerParams(vmem_limit_bytes=VMEM_LIMIT),
        cost_estimate=cost(2 * rows * w.size, w.size * 2),
        name="q_shared",
    )(x, gain, shift, w, bq, bv)


def spread(x):
    rows = x.shape[0]
    low = low_lanes(rows)
    zero = jnp.zeros_like(x)
    return jnp.concatenate([jnp.where(low, x, zero), jnp.where(low, swap_halves(x), zero)], axis=0)


def unspread(x):
    half = x.shape[0] // 2
    return x[:half] + swap_halves(x[half:])


def softmax_block(q, k, v):
    s = nt_dot(q, k)
    m = jnp.max(s, axis=-1, keepdims=True)
    e = jnp.exp(s - m)
    total = jnp.sum(e, axis=-1, keepdims=True)
    e = e.astype(BF)
    rinv = 1.0 / total
    return e, nn(e, v) * rinv, rinv


def attn5_fwd_kernel(steps, x_ref, o_ref, r_ref, ob_ref, e_ref, qf, kf, vf, of, rf):
    for part, dst in enumerate((qf, kf, vf)):
        blk = x_ref[:, part * 2 * HD : (part + 1) * 2 * HD].astype(F32)
        dst[...] = spread(blk).astype(BF)
    rows = qf.shape[0] // steps
    low = low_lanes(rows)

    def body(i, carry):
        at = pl.ds(pl.multiple_of(i * rows, rows), rows)
        e, o, rinv = softmax_block(qf[at, :], kf[...], vf[...])
        e_ref[at, :] = e
        of[at, :] = o
        rf[at, :] = jnp.where(low, jnp.broadcast_to(rinv, (rows, 2 * HD)), 0.0)
        return carry

    lax.fori_loop(0, steps, body, 0)
    packed = unspread(of[...])
    o_ref[...] = packed
    ob_ref[...] = packed.astype(BF)
    r_ref[...] = unspread(rf[...])


def attn5_fwd_call(x):
    rows = x.shape[0]
    toks = 2 * rows
    return pl.pallas_call(
        functools.partial(attn5_fwd_kernel, 4),
        out_shape=(
            jax.ShapeDtypeStruct((rows, 2 * HD), F32),
            jax.ShapeDtypeStruct((rows, 2 * HD), F32),
            jax.ShapeDtypeStruct((rows, 2 * HD), BF),
            jax.ShapeDtypeStruct((toks, toks), BF),
        ),
        scratch_shapes=[pltpu.VMEM((toks, 2 * HD), BF)] * 3 + [pltpu.VMEM((toks, 2 * HD), F32)] * 2,
        compiler_params=pltpu.CompilerParams(vmem_limit_bytes=VMEM_LIMIT),
        cost_estimate=cost(4 * 4 * toks * toks * 2 * HD, toks * toks * 2),
        name="attn_shared_fwd",
    )(x)


def attn5_bwd_kernel(
    steps, x_ref, ga_ref, o_ref, r_ref, e_ref, out_ref, qf, kf, vf, gf, inn, dq, dk, dv
):
    for part, dst in enumerate((qf, kf, vf)):
        blk = x_ref[:, part * 2 * HD : (part + 1) * 2 * HD].astype(F32)
        dst[...] = spread(blk).astype(BF)
    g = ga_ref[...].astype(F32) * r_ref[...]
    gs = spread(g)
    gf[...] = gs.astype(BF)
    inn[...] = jnp.sum(gs * spread(o_ref[...]), axis=-1, keepdims=True)
    rows = qf.shape[0] // steps
    dk[...] = jnp.zeros_like(dk)
    dv[...] = jnp.zeros_like(dv)

    def body(i, carry):
        at = pl.ds(pl.multiple_of(i * rows, rows), rows)
        e = e_ref[at, :]
        gb = gf[at, :]
        dp = nt_dot(gb, vf[...])
        ds = (e.astype(F32) * (dp - inn[at, :])).astype(BF)
        dq[at, :] = nn(ds, kf[...]) * (HD**-0.5)
        dk[...] += tn_dot(ds, qf[at, :])
        dv[...] += tn_dot(e, gb)
        return carry

    lax.fori_loop(0, steps, body, 0)
    for part, src in enumerate((dq, dk, dv)):
        out_ref[:, part * 2 * HD : (part + 1) * 2 * HD] = unspread(src[...]).astype(BF)


def attn5_bwd_call(x, ga, o, r, e):
    rows = x.shape[0]
    toks = 2 * rows
    return pl.pallas_call(
        functools.partial(attn5_bwd_kernel, 4),
        out_shape=jax.ShapeDtypeStruct((rows, 6 * HD), BF),
        scratch_shapes=[pltpu.VMEM((toks, 2 * HD), BF)] * 4
        + [pltpu.VMEM((toks, 1), F32)]
        + [pltpu.VMEM((toks, 2 * HD), F32)] * 3,
        compiler_params=pltpu.CompilerParams(vmem_limit_bytes=VMEM_LIMIT),
        cost_estimate=cost(8 * 4 * toks * toks * 2 * HD, toks * toks * 2),
        name="attn_shared_bwd",
    )(x, ga, o, r, e)


def attn_fwd_kernel(nt, *refs):
    ns = refs[:nt]
    wq, wk, wv, bq, bv = refs[nt : nt + 5]
    att_ref, o_ref, r_ref, q_ref, k_ref, v_ref, e_ref = refs[nt + 5 :]
    rows = ns[0].shape[0]
    for c in range(nt):
        at = slice(c * rows, (c + 1) * rows)
        x = ns[c][...]
        k_ref[at, :] = nn(x, wk[...]).astype(BF)
        v_ref[at, :] = (nn(x, wv[...]) + bv[...]).astype(BF)
    q_ref[...] = ((nn(ns[0][...], wq[...]) + bq[...]) * (HD**-0.5)).astype(BF)
    low = low_lanes(rows)
    for pair in range(q_ref.shape[1] // (2 * HD)):
        lanes = slice(pair * 2 * HD, (pair + 1) * 2 * HD)
        q, k, v = q_ref[:, lanes], k_ref[:, lanes], v_ref[:, lanes]
        zero = jnp.zeros_like(q)
        e0, o0, r0 = softmax_block(jnp.where(low, q, zero), k, v)
        e_ref[2 * pair] = e0
        e1, o1, r1 = softmax_block(jnp.where(low, zero, q), k, v)
        e_ref[2 * pair + 1] = e1
        o = jnp.where(low, o0, o1)
        o_ref[:, lanes] = o
        att_ref[:, lanes] = o.astype(BF)
        r_ref[:, lanes] = jnp.where(
            low, jnp.broadcast_to(r0, (rows, 2 * HD)), jnp.broadcast_to(r1, (rows, 2 * HD))
        )


def attn_fwd_call(ns, w, bq, bv):
    nt = len(ns)
    rows, width = ns[0].shape
    toks = nt * rows
    blk = 4 * HD
    steps = width // blk
    wspec = [pl.BlockSpec((width, blk), lambda j, p=p: (0, p * steps + j)) for p in range(3)]
    bspec = pl.BlockSpec((1, blk), lambda j: (0, j))
    row = lambda n: pl.BlockSpec((n, blk), lambda j: (0, j))
    return pl.pallas_call(
        functools.partial(attn_fwd_kernel, nt),
        grid=(steps,),
        in_specs=[full((rows, width))] * nt + wspec + [bspec, bspec],
        out_specs=[row(rows)] * 4
        + [row(toks)] * 2
        + [pl.BlockSpec((4, rows, toks), lambda j: (j, 0, 0))],
        out_shape=(
            jax.ShapeDtypeStruct((rows, width), BF),
            jax.ShapeDtypeStruct((rows, width), F32),
            jax.ShapeDtypeStruct((rows, width), F32),
            jax.ShapeDtypeStruct((rows, width), BF),
            jax.ShapeDtypeStruct((toks, width), BF),
            jax.ShapeDtypeStruct((toks, width), BF),
            jax.ShapeDtypeStruct((width // HD, rows, toks), BF),
        ),
        compiler_params=params(),
        cost_estimate=cost(4 * toks * width * width + 16 * rows * toks * width, 20 << 20),
        name="attn_fwd",
    )(*ns, w, w, w, bq, bv)


def attn_bwd_kernel(nt, *refs):
    ns = refs[:nt]
    wq, wk, wv, ga_ref, q_ref, k_ref, v_ref, o_ref, r_ref, e_ref = refs[nt : nt + 10]
    dw_ref, gbq_ref, gbv_ref = refs[nt + 10 : nt + 13]
    dxs = refs[nt + 13 : nt + 13 + nt]
    gq, gk, gv, dx = refs[nt + 13 + nt :]
    step = pl.program_id(0)
    rows = ns[0].shape[0]
    low = low_lanes(rows)
    for pair in range(q_ref.shape[1] // (2 * HD)):
        lanes = slice(pair * 2 * HD, (pair + 1) * 2 * HD)
        q, k, v = q_ref[:, lanes], k_ref[:, lanes], v_ref[:, lanes]
        g = ga_ref[:, lanes].astype(F32) * r_ref[:, lanes]
        go = g * o_ref[:, lanes]
        g = g.astype(BF)
        zero = jnp.zeros_like(q)
        halves = []
        for side in range(2):
            mine = low if side == 0 else jnp.logical_not(low)
            qh = jnp.where(mine, q, zero)
            gh = jnp.where(mine, g, zero)
            inner = jnp.sum(jnp.where(mine, go, 0.0), axis=-1, keepdims=True)
            e = e_ref[2 * pair + side]
            dp = nt_dot(gh, v)
            ds = (e.astype(F32) * (dp - inner)).astype(BF)
            halves.append((nn(ds, k), tn_dot(ds, qh), tn_dot(e, gh)))
        gq[:, lanes] = (jnp.where(low, halves[0][0], halves[1][0]) * (HD**-0.5)).astype(BF)
        gk[:, lanes] = (halves[0][1] + halves[1][1]).astype(BF)
        gv[:, lanes] = (halves[0][2] + halves[1][2]).astype(BF)

    @pl.when(step == 0)
    def _():
        dx[...] = jnp.zeros_like(dx)

    gbq_ref[...] = colsum(gq[...].astype(F32))
    gbv_ref[...] = colsum(gv[...].astype(F32))
    dw_ref[0] = tn_dot(ns[0][...], gq[...]).astype(BF)
    dx[0:rows, :] += nt_dot(gq[...], wq[...])
    dwk = jnp.zeros(dw_ref.shape[1:], F32)
    dwv = jnp.zeros(dw_ref.shape[1:], F32)
    for c in range(nt):
        at = slice(c * rows, (c + 1) * rows)
        dx[at, :] += nt_dot(gk[at, :], wk[...]) + nt_dot(gv[at, :], wv[...])
        dwk += tn_dot(ns[c][...], gk[at, :])
        dwv += tn_dot(ns[c][...], gv[at, :])
    dw_ref[1] = dwk.astype(BF)
    dw_ref[2] = dwv.astype(BF)

    @pl.when(step == pl.num_programs(0) - 1)
    def _():
        for c in range(nt):
            dxs[c][...] = dx[c * rows : (c + 1) * rows, :].astype(dxs[c].dtype)


def attn_bwd_call(ns, w, ga, q, k, v, o, r, e):
    nt = len(ns)
    rows, width = ns[0].shape
    toks = nt * rows
    blk = 4 * HD
    steps = width // blk
    wspec = [pl.BlockSpec((width, blk), lambda j, p=p: (0, p * steps + j)) for p in range(3)]
    row = lambda n: pl.BlockSpec((n, blk), lambda j: (0, j))
    return pl.pallas_call(
        functools.partial(attn_bwd_kernel, nt),
        grid=(steps,),
        in_specs=[full((rows, width))] * nt
        + wspec
        + [row(rows), row(rows), row(toks), row(toks), row(rows), row(rows)]
        + [pl.BlockSpec((4, rows, toks), lambda j: (j, 0, 0))],
        out_specs=[pl.BlockSpec((3, width, blk), lambda j: (0, 0, j)), row(1), row(1)]
        + [full((rows, width))] * nt,
        out_shape=[
            jax.ShapeDtypeStruct((3, width, width), BF),
            jax.ShapeDtypeStruct((1, width), F32),
            jax.ShapeDtypeStruct((1, width), F32),
            jax.ShapeDtypeStruct((rows, width), F32),
        ]
        + [jax.ShapeDtypeStruct((rows, width), BF)] * (nt - 1),
        scratch_shapes=[
            pltpu.VMEM((rows, blk), BF),
            pltpu.VMEM((toks, blk), BF),
            pltpu.VMEM((toks, blk), BF),
            pltpu.VMEM((toks, width), F32),
        ],
        compiler_params=params(),
        cost_estimate=cost(8 * toks * width * width + 32 * rows * toks * width, 24 << 20),
        name="attn_bwd",
    )(*ns, w, w, w, ga, q, k, v, o, r, e)


def mid_kernel(nf, nt, *refs):
    (
        att_ref,
        att5_ref,
        xm_ref,
        x5_ref,
        cm_ref,
        c5_ref,
        wo_ref,
        bo_ref,
        g2_ref,
        s2_ref,
        bd_ref,
        wu_ref,
        bu_ref,
        wd_ref,
        out_ref,
        out5_ref,
        gm_ref,
        ga_ref,
        ga5_ref,
        dwo_ref,
        dwu_ref,
        dwd_ref,
        vec_ref,
        gbu_ref,
        att,
        cot,
        mid,
        hat,
        rst,
        two,
        acc,
        gn2,
    ) = refs
    step = pl.program_id(0)
    rm = xm_ref.shape[0]
    r5, width = x5_ref.shape
    half = r5 // 2
    low = low_lanes(half)
    pairs = width // (2 * HD)

    @pl.when(step == 0)
    def _():
        att[0:rm, :] = att_ref[...]
        for pair in range(pairs):
            lanes = slice(pair * 2 * HD, (pair + 1) * 2 * HD)
            even = att5_ref[slot_of(2 * pair, nf, nt)].astype(F32)
            odd = att5_ref[slot_of(2 * pair + 1, nf, nt)].astype(F32)
            top = jnp.where(low, even, swap_halves(odd))
            bot = jnp.where(low, swap_halves(even), odd)
            att[rm : rm + r5, lanes] = jnp.concatenate([top, bot], axis=0).astype(BF)
        cot[0:rm, :] = cm_ref[...]
        cot[rm : rm + r5, :] = c5_ref[...]
        mid[...] = nn(att[...], wo_ref[...]) + bo_ref[...]
        mid[0:rm, :] += xm_ref[...].astype(F32)
        mid[rm : rm + r5, :] += x5_ref[...].astype(F32)
        n, rstd = normalize(mid[...])
        hat[...] = n
        rst[...] = rstd
        two[...] = (n * g2_ref[...] + s2_ref[...]).astype(BF)
        acc[...] = mid[...] + bd_ref[...]
        gn2[...] = jnp.zeros_like(gn2)

    pre = nn(two[...], wu_ref[...]) + bu_ref[...]
    cdf = 0.5 * (1.0 + lax.erf(pre * (0.5**0.5)))
    slope = cdf + pre * (jnp.exp(-0.5 * pre * pre) * 0.3989422804014327)
    act = (pre * cdf).astype(BF)
    acc[...] += nn(act, wd_ref[...])
    dwd_ref[...] = tn_dot(act, cot[...]).astype(BF)
    gpre = (nt_dot(cot[...], wd_ref[...]) * slope).astype(BF)
    gbu_ref[...] = colsum(gpre.astype(F32))
    dwu_ref[...] = tn_dot(two[...], gpre).astype(BF)
    gn2[...] += nt_dot(gpre, wu_ref[...])

    @pl.when(step == pl.num_programs(0) - 1)
    def _():
        out_ref[...] = acc[0:rm, :].astype(BF)
        out5_ref[...] = acc[rm : rm + r5, :]
        e = gn2[...]
        n = hat[...]
        c = cot[...].astype(F32)
        gmid = c + norm_back(e, n, rst[...], g2_ref[...])
        gm_ref[...] = gmid
        branch = gmid.astype(BF)
        vec_ref[0:1, :] = colsum(branch.astype(F32))
        vec_ref[1:2, :] = colsum(e * n)
        vec_ref[2:3, :] = colsum(e)
        vec_ref[3:4, :] = colsum(c)
        dwo_ref[...] = tn_dot(att[...], branch).astype(BF)
        gatt = nt_dot(branch, wo_ref[...])
        ga_ref[...] = gatt[0:rm].astype(BF)
        ga5_ref[...] = jnp.zeros_like(ga5_ref)
        for pair in range(pairs):
            lanes = slice(pair * 2 * HD, (pair + 1) * 2 * HD)
            top, bot = gatt[rm : rm + half, lanes], gatt[rm + half : rm + r5, lanes]
            even = jnp.where(low, top, swap_halves(bot))
            odd = jnp.where(low, swap_halves(top), bot)
            ga5_ref[slot_of(2 * pair, nf, nt)] = even.astype(BF)
            ga5_ref[slot_of(2 * pair + 1, nf, nt)] = odd.astype(BF)


def mid_call(nf, nt, att, att5, xm, x5, cm, c5, wo, bo, g2, s2, bd, wu, bu, wd):
    rm, width = xm.shape
    r5 = x5.shape[0]
    rows = rm + r5
    ff = wu.shape[1]
    blk = 768
    vec = full((1, width))
    return pl.pallas_call(
        functools.partial(mid_kernel, nf, nt),
        grid=(ff // blk,),
        in_specs=[
            full(att.shape),
            full(att5.shape),
            full(xm.shape),
            full(x5.shape),
            full(cm.shape),
            full(c5.shape),
            full(wo.shape),
            vec,
            vec,
            vec,
            vec,
            pl.BlockSpec((width, blk), lambda j: (0, j)),
            pl.BlockSpec((1, blk), lambda j: (0, j)),
            pl.BlockSpec((blk, width), lambda j: (j, 0)),
        ],
        out_specs=[
            full((rm, width)),
            full((r5, width)),
            full((rows, width)),
            full((rm, width)),
            full(att5.shape),
            full((width, width)),
            pl.BlockSpec((width, blk), lambda j: (0, j)),
            pl.BlockSpec((blk, width), lambda j: (j, 0)),
            full((4, width)),
            pl.BlockSpec((1, blk), lambda j: (0, j)),
        ],
        out_shape=[
            jax.ShapeDtypeStruct((rm, width), BF),
            jax.ShapeDtypeStruct((r5, width), F32),
            jax.ShapeDtypeStruct((rows, width), F32),
            jax.ShapeDtypeStruct((rm, width), BF),
            jax.ShapeDtypeStruct(att5.shape, BF),
            jax.ShapeDtypeStruct((width, width), BF),
            jax.ShapeDtypeStruct((width, ff), BF),
            jax.ShapeDtypeStruct((ff, width), BF),
            jax.ShapeDtypeStruct((4, width), F32),
            jax.ShapeDtypeStruct((1, ff), F32),
        ],
        scratch_shapes=[
            pltpu.VMEM((rows, width), BF),
            pltpu.VMEM((rows, width), BF),
            pltpu.VMEM((rows, width), F32),
            pltpu.VMEM((rows, width), F32),
            pltpu.VMEM((rows, 1), F32),
            pltpu.VMEM((rows, width), BF),
            pltpu.VMEM((rows, width), F32),
            pltpu.VMEM((rows, width), F32),
        ],
        compiler_params=params(),
        cost_estimate=cost(12 * rows * width * ff + 6 * rows * width * width, 24 << 20),
        name="mid",
    )(att, att5, xm, x5, cm, c5, wo, bo, g2, s2, bd, wu, bu, wd)


def tail5_kernel(nf, nt, *refs):
    (g_ref, n5_ref, x5_ref, gm_ref, w_ref, dw_ref, g1_ref, dwo_ref, gb_ref, gin_ref, vec_ref, g5, dx) = refs
    step = pl.program_id(0)
    r5, width = x5_ref.shape
    half = r5 // 2
    low = low_lanes(half)
    for pair in range(width // (2 * HD)):
        lanes = slice(pair * 2 * HD, (pair + 1) * 2 * HD)
        even = g_ref[slot_of(2 * pair, nf, nt)].astype(F32)
        odd = g_ref[slot_of(2 * pair + 1, nf, nt)].astype(F32)
        top = jnp.where(low, even, swap_halves(odd))
        bot = jnp.where(low, swap_halves(even), odd)
        g5[:, lanes] = jnp.concatenate([top, bot], axis=0).astype(BF)
    g = g5[...]
    gb_ref[0] = colsum(g.astype(F32))
    dwo_ref[...] = (dw_ref[0].astype(F32) + tn_dot(n5_ref[...], g)).astype(BF)

    @pl.when(step == 0)
    def _():
        dx[...] = jnp.zeros_like(dx)

    dx[...] += nt_dot(g, w_ref[...])

    @pl.when(step == pl.num_programs(0) - 1)
    def _():
        n, rstd = normalize(x5_ref[...].astype(F32))
        e = dx[...]
        gin_ref[...] = gm_ref[...] + norm_back(e, n, rstd, g1_ref[...])
        vec_ref[0:1, :] = colsum(e * n)
        vec_ref[1:2, :] = colsum(e)


def tail5_call(nf, nt, g, n5, x5, gm, w, dw, g1):
    r5, width = x5.shape
    at = gm.shape[0] // r5 - 1
    return pl.pallas_call(
        functools.partial(tail5_kernel, nf, nt),
        grid=(3,),
        in_specs=[
            pl.BlockSpec((g.shape[0], r5 // 2, 2 * HD), lambda j: (0, 0, j)),
            full(n5.shape),
            full(x5.shape),
            pl.BlockSpec((r5, width), lambda j: (at, 0)),
            pl.BlockSpec((width, width), lambda j: (0, j)),
            pl.BlockSpec((1, width, width), lambda j: (j, 0, 0)),
            full((1, width)),
        ],
        out_specs=[
            pl.BlockSpec((width, width), lambda j: (0, j)),
            pl.BlockSpec((1, 1, width), lambda j: (j, 0, 0)),
            full((r5, width)),
            full((2, width)),
        ],
        out_shape=[
            jax.ShapeDtypeStruct((width, 3 * width), BF),
            jax.ShapeDtypeStruct((3, 1, width), F32),
            jax.ShapeDtypeStruct((r5, width), F32),
            jax.ShapeDtypeStruct((2, width), F32),
        ],
        scratch_shapes=[pltpu.VMEM((r5, width), BF), pltpu.VMEM((r5, width), F32)],
        compiler_params=params(),
        cost_estimate=cost(4 * r5 * width * width * 3, 12 << 20),
        name="tail_shared",
    )(g, n5, x5, gm, w, dw, g1)


def tail_kernel(nt, *refs):
    dxs = refs[:nt]
    x_ref, gm_ref, g1_ref, gin_ref, vec_ref = refs[nt:]
    e = dxs[0][...]
    for c in range(1, nt):
        e = e + dxs[c][...].astype(F32)
    n, rstd = normalize(x_ref[...].astype(F32))
    gin_ref[...] = (gm_ref[...] + norm_back(e, n, rstd, g1_ref[...])).astype(BF)
    vec_ref[0:1, :] = colsum(e * n)
    vec_ref[1:2, :] = colsum(e)


def tail_call(dxs, x, gm, g1):
    rows, width = x.shape
    nt = len(dxs)
    return pl.pallas_call(
        functools.partial(tail_kernel, nt),
        grid=(1,),
        in_specs=[full((rows, width))] * (nt + 2) + [full((1, width))],
        out_specs=[full((rows, width)), full((2, width))],
        out_shape=[
            jax.ShapeDtypeStruct((rows, width), BF),
            jax.ShapeDtypeStruct((2, width), F32),
        ],
        compiler_params=params(),
        cost_estimate=cost(30 * rows * width, 6 << 20),
        name="tail",
    )(*dxs, x, gm, g1)


def over(axes, x):
    return lax.all_to_all(x, axes, 0, 0)


def partners(nt, k):
    if nt & (nt - 1):
        return [(i, (i + k) % nt) for i in range(nt)], [(i, (i - k) % nt) for i in range(nt)]
    pairs = [(i, i ^ k) for i in range(nt)]
    return pairs, pairs


def local(
    nf,
    nt,
    ng,
    inputs,
    gain_one,
    shift_one,
    w_qkv,
    bias_query,
    bias_value,
    w_out,
    bias_out,
    gain_two,
    shift_two,
    w_up,
    bias_up,
    w_down,
    bias_down,
    cotangent,
):
    clips, r, width = inputs.shape
    ff = w_up.shape[1]
    g1, s1 = gain_one[None], shift_one[None]
    bq, bv = bias_query[None], bias_value[None]
    rm = nf * r
    x5, c5 = inputs[nf], cotangent[nf]
    xm = over("freq", inputs[:nf]).reshape(rm, width)
    n5, pack5 = q5_call(nf, nt, x5, g1, s1, w_qkv, bq, bv)
    got5 = over(("freq", "tm"), pack5).reshape(-1, 6 * HD)
    nm = ln_call(xm, g1, s1)
    ns = [nm] + [lax.ppermute(nm, "tm", partners(nt, k)[0]) for k in range(1, nt)]
    cm = over("freq", cotangent[:nf]).reshape(rm, width)
    o5, r5, ob5, e5 = attn5_fwd_call(got5)
    att5 = over(("freq", "tm"), ob5.reshape(nf * nt, r // 2, 2 * HD))
    att, o, rr, q, k, v, e = attn_fwd_call(ns, w_qkv, bq, bv)
    out_m, out5, gm, ga, ga5, dwo, dwu, dwd, vec, gbu = mid_call(
        nf,
        nt,
        att,
        att5,
        xm,
        x5,
        cm,
        c5,
        w_out,
        bias_out[None],
        gain_two[None],
        shift_two[None],
        bias_down[None],
        w_up,
        bias_up[None],
        w_down,
    )
    got_ga5 = over(("freq", "tm"), ga5).reshape(-1, 2 * HD)
    g5 = over(
        ("freq", "tm"),
        attn5_bwd_call(got5, got_ga5, o5, r5, e5).reshape(nf * nt, r // 2, 6 * HD),
    )
    dw_main, gbq, gbv, *dxs = attn_bwd_call(ns, w_qkv, ga, q, k, v, o, rr, e)
    dxs = [dxs[0]] + [lax.ppermute(dxs[k], "tm", partners(nt, k)[1]) for k in range(1, nt)]
    gin_m, vec_m = tail_call(dxs, xm, gm, g1)
    dwqkv, gb5, gin5, vec5 = tail5_call(nf, nt, g5, n5, x5, gm, w_qkv, dw_main, g1)

    block_out = over("freq", out_m.reshape(nf, r, width)).astype(F32)
    block_out = jnp.concatenate([block_out, out5[None]], axis=0)
    grad_in = over("freq", gin_m.reshape(nf, r, width)).astype(F32)
    grad_in = jnp.concatenate([grad_in, gin5[None]], axis=0)

    def scatter(x):
        return lax.psum_scatter(x, ALL, scatter_dimension=0, tiled=True).astype(F32)

    dev = nf * nt * ng
    vec1 = vec_m + vec5
    small = jnp.concatenate([vec1, vec, gbq + gb5[0], gbv + gb5[2]], axis=0)
    small = small.reshape(8, dev, width // dev).transpose(1, 0, 2).reshape(dev, -1)
    small = jnp.concatenate([small, gbu.reshape(dev, ff // dev)], axis=1)
    small = jnp.sum(over(ALL, small), axis=0)
    per = width // dev
    piece = lambda i: small[i * per : (i + 1) * per]
    return (
        block_out,
        grad_in,
        piece(0),
        piece(1),
        scatter(dwqkv),
        piece(6),
        piece(7),
        scatter(dwo),
        piece(2),
        piece(3),
        piece(4),
        scatter(dwu),
        small[8 * per :],
        scatter(dwd),
        piece(5),
    )


def solution(mesh):
    tokens = P("grp", ("freq", "tm"), None)
    vec = P(ALL)
    mat = P(ALL, None)
    return jax.shard_map(
        functools.partial(local, mesh.shape["freq"], mesh.shape["tm"], mesh.shape["grp"]),
        mesh=mesh,
        in_specs=(tokens,) + (P(),) * 13 + (tokens,),
        out_specs=(
            tokens,
            tokens,
            vec,
            vec,
            mat,
            vec,
            vec,
            mat,
            vec,
            vec,
            vec,
            mat,
            vec,
            mat,
            vec,
        ),
        check_vma=False,
    )
```

time: 1370 us -> 576 us (0.42)
  waiting for transfers between devices: 932 us -> 382 us
  local copies, waits for them, and re-layouts: 230 us -> 15.3 us
  Pallas kernels: 0 us -> 102 us
  matrix products: 99.4 us -> 0 us
  starting transfers between devices: 0.68 us -> 51.5 us
  blocking collectives: 41.3 us -> 0 us
  other arithmetic: 40.1 us -> 9.54 us
    unnamed x10 -> x4, waiting for transfers between devices: 287 us -> 1.65 us
    all_gather x2 -> x0, waiting for transfers between devices: 225 us -> none  [the longest x1 121 us: local(): lax.all_gather(key_own, ('freq', 'tm'), axis=1, tiled=True)]
    pallas_call x0 -> x9, Pallas kernels: none -> 102 us  [the longest x1 28.7 us: attn_bwd_call(): pl.pallas_call(functools.partial(attn_bwd_kernel, nt), grid=(steps,), in_...]
    dot_general x54 -> x0, matrix products: 99.4 us -> none  [the longest x42 34.4 us: mixed_product(): return jnp.einsum(spec, left, right, preferred_element_type=jnp.float32)]
    reduce_scatter x4, waiting for transfers between devices: 420 us -> 323 us  [scatter(): return lax.psum_scatter(x, ALL, scatter_dimension=0, tiled=True).astype(F32)]
    unnamed x85 -> x64, local copies, waits for them, and re-layouts: 91.7 us -> 3 us
    dynamic_slice x36 -> x0, local copies, waits for them, and re-layouts: 48.1 us -> none  [local(): lax.map(attend_pair, (query_pairs, key_pairs, value_pairs))]
    all_to_all x0 -> x9, starting transfers between devices: none -> 44.2 us  [over(): return lax.all_to_all(x, axes, 0, 0)]
  transfers between devices with their start and end apart: 8 -> 19, of which waited for: 8 -> 13; matrix products, arithmetic and copies ran while one was open for 11% -> 3% of each run, Pallas kernels for 0% -> 14%
where the time goes in v1:
time: 576 us; the launch traced here: 575 us
  waiting for transfers between devices  382 us (66%)
  Pallas kernels  102 us (18%)
  starting transfers between devices  51.5 us (9%)
  local copies, waits for them, and re-layouts  15.3 us (3%)
  between operations  14.2 us (2%)
  other arithmetic  9.54 us (2%)
    reduce_scatter x4, waiting for transfers between devices, scatter(): return lax.psum_scatter(x, ALL, scatter_dimension=0, tiled=True).astype(F32)  323 us
    all_to_all x9, starting transfers between devices, over(): return lax.all_to_all(x, axes, 0, 0)  44.2 us
    all_to_all x9, waiting for transfers between devices, over(): return lax.all_to_all(x, axes, 0, 0)  38.2 us
    pallas_call x1, Pallas kernels, attn_bwd_call(): pl.pallas_call(functools.partial(attn_bwd_kernel, nt), grid=(steps,), in_...  28.7 us
    pallas_call x1, Pallas kernels, mid_call(): pl.pallas_call(functools.partial(mid_kernel, nf, nt), grid=(ff // blk,),...  22.9 us
    pallas_call x1, Pallas kernels, attn_fwd_call(): pl.pallas_call(functools.partial(attn_fwd_kernel, nt), grid=(steps,), in_...  16 us
    ppermute x3, waiting for transfers between devices, local(): lax.ppermute(dxs[k], 'tm', partners(nt, k)[1])  13.7 us
  transfers between devices with their start and end apart: 19, of which 13 were waited for; matrix products, arithmetic and copies ran while one was open for 3% of the time, Pallas kernels for 14%

profile of v1, /device:TPU:0, one launch (start us, length us, event | category | flops | bytes accessed | tf_op | source)
XLA Modules:
  0.0 575.0 jit_solution(12430211753065739466)
XLA Ops:
  7.2 1.9 slice.45
  9.1 6.3 %all-to-all-start = ((bf16[4,80,768]{2,1,0:T(8,128)(2,1)}), bf16[4,80,768]{2,1,0:T(8,128)(2,1)S(1)}, u32[]{:S(2)}, u32[]{:S(2)}) async-start(bf16[4,80,768]{2,1,0:T(8,128)(2,1)} %slice.45), calls=%async_computation | async-start | bytes 983040 | tf_op jit(solution)/shard_map/all_to_all | solution.py:650
  19.3 3.9 q_shared.1
  23.2 6.0 %all-to-all-done = bf16[4,80,768]{2,1,0:T(8,128)(2,1)S(1)} async-done(((bf16[4,80,768]{2,1,0:T(8,128)(2,1)}), bf16[4,80,768]{2,1,0:T(8,128)(2,1)S(1)}, u32[]{:S(2)}, u32[]{:S(2)}) %all-to-all-start) | async-done | bytes 491552 | tf_op jit(solution)/shard_map/all_to_all | solution.py:650
  29.2 4.7 all-to-all-start.1
  34.7 12.3 %all-to-all-done.1 = bf16[16,40,384]{2,1,0:T(8,128)(2,1)S(1)} async-done(((bf16[16,40,384]{2,1,0:T(8,128)(2,1)}), bf16[16,40,384]{2,1,0:T(8,128)(2,1)S(1)}, u32[]{:S(2)}, u32[]{:S(2)}) %all-to-all-start.1) | async-done | bytes 491552 | tf_op jit(solution)/shard_map/all_to_all | solution.py:650
  47.1 3.5 all-to-all-start.3
  53.0 2.2 ln_one.1.refs_0_
  56.6 2.0 collective-permute-start.2
  59.3 7.8 %attn_shared_fwd.1 = (f32[640,128]{1,0:T(8,128)}, f32[640,128]{1,0:T(8,128)}, bf16[640,128]{1,0:T(8,128)(2,1)}, bf16[1280,1280]{1,0:T(8,128)(2,1)}) custom-call(bf16[640,384]{1,0:T(8,128)(2,1)} %bitcast.26), custom_call_target="tpu_custom_call" | custom-call | flops 3355443200 | bytes 3276800 | tf_op jit(solution)/shard_map/attn_shared_fwd/pallas_call | solution.py:176
  67.1 5.5 all-to-all-start.2
  72.6 4.6 collective-permute-done.1.refs_2_
  78.6 16.0 %attn_fwd.1 = (bf16[320,768]{1,0:T(8,128)(2,1)}, f32[320,768]{1,0:T(8,128)}, f32[320,768]{1,0:T(8,128)}, bf16[320,768]{1,0:T(8,128)(2,1)}, bf16[1280,768]{1,0:T(...) custom-call(bf16[320,768]{1,0:T(8,128)(2,1)} %ln_one.1.refs_0_, bf16[320,768]{1,0:T(8,128)(2,1)} %copy-done.27, ...), custom_call_target="tpu_custom_call" | custom-call | flops 8053063680 | bytes 20971520 | tf_op jit(solution)/shard_map/attn_fwd/pallas_call | solution.py:273
  95.3 22.9 %mid.1 = (bf16[320,768]{1,0:T(8,128)(2,1)}, f32[80,768]{1,0:T(8,128)}, f32[400,768]{1,0:T(8,128)}, bf16[320,768]{1,0:T(8,128)(2,1)}, bf16[16,40,128]{2,1,0:T(8,1...) custom-call(bf16[320,768]{1,0:T(8,128)(2,1)} %get-tuple-element.51.r, ...), custom_call_target="tpu_custom_call" | custom-call | flops 12740198400 | bytes 25165824 | tf_op jit(solution)/shard_map/mid/pallas_call | solution.py:494
  118.2 7.1 %all-to-all-start.6 = ((bf16[16,40,128]{2,1,0:T(8,128)(2,1)}), bf16[16,40,128]{2,1,0:T(8,128)(2,1)S(1)}, u32[]{:S(2)}, u32[]{:S(2)}) async-start(bf16[16,40,128]{2,1,0:T(8,128)(2,1)} %get-tuple-element.69), calls=%async_computation.6 | async-start | bytes 327680 | tf_op jit(solution)/shard_map/all_to_all | solution.py:650
  126.1 7.2 %all-to-all-done.6 = bf16[16,40,128]{2,1,0:T(8,128)(2,1)S(1)} async-done(((bf16[16,40,128]{2,1,0:T(8,128)(2,1)}), bf16[16,40,128]{2,1,0:T(8,128)(2,1)S(1)}, u32[]{:S(2)}, u32[]{:S(2)}) %all-to-all-start.6) | async-done | bytes 163872 | tf_op jit(solution)/shard_map/all_to_all | solution.py:650
  134.0 8.5 %attn_shared_bwd.1 = bf16[640,384]{1,0:T(8,128)(2,1)} custom-call(bf16[640,384]{1,0:T(8,128)(2,1)} %bitcast.27, bf16[640,128]{1,0:T(8,128)(2,1)} %bitcast.34, f32[640,128]{1,0:T(8,128)} %get-tuple-element.70.o_ref, f32[640,128]{1,0:T(8,128)} %get-tuple-element.71.r_ref, bf16[1280,1280]{1,0:T(8,128)(2,1)} %get-tuple-element.72.e_ref), custom_call_target="tpu_custom_call" | custom-call | flops 6710886400 | bytes 3276800 | tf_op jit(solution)/shard_map/attn_shared_bwd/pallas_call | solution.py:224
  142.5 3.6 all-to-all-start.7
  146.1 28.7 %attn_bwd.1 = (bf16[3,768,768]{2,1,0:T(8,128)(2,1)}, f32[1,768]{1,0:T(1,128)}, f32[1,768]{1,0:T(1,128)}, f32[320,768]{1,0:T(8,128)}, bf16[320,768]{1,0:T(8,128)(...) custom-call(bf16[320,768]{1,0:T(8,128)(2,1)} %ln_one.1.refs_0_, bf16[320,768]{1,0:T(8,128)(2,1)} %copy-done.27, ...), custom_call_target="tpu_custom_call" | custom-call | flops 16106127360 | bytes 25165824 | tf_op jit(solution)/shard_map/attn_bwd/pallas_call | solution.py:357
  175.6 8.5 %tail_shared.1 = (bf16[768,2304]{1,0:T(8,128)(2,1)}, f32[3,1,768]{2,1,0:T(1,128)}, f32[80,768]{1,0:T(8,128)}, f32[2,768]{1,0:T(2,128)}) custom-call(bf16[16,40,384]{2,1,0:T(8,128)(2,1)} %copy-done.1, bf16[80,768]{1,0:T(8,128)(2,1)} %get-tuple-element.73.refs_1_, bf16[80,768]{1,0:T(8,128)(2,1)} %slice_bitcast_fusion.1.x_ref.refs_3_.refs_2_, ...), custom_call_target="tpu_custom_call" | custom-call | flops 566231040 | bytes 12582912 | tf_op jit(solution)/shard_map/tail_shared/pallas_call | solution.py:588
  185.4 4.9 all-to-all-start.4
  193.9 6.9 %collective-permute-done.3.refs_1_ = bf16[320,768]{1,0:T(8,128)(2,1)S(1)} collective-permute-done((bf16[320,768]{1,0:T(8,128)(2,1)S(1)}, bf16[320,768]{1,0:T(8,128)(2,1)S(1)}, u32[]{:S(2)}, u32[]{:S(2)}) %collective-permute-start.3) | collective-permute-done | bytes 491552 | tf_op jit(solution)/shard_map/ppermute | solution.py:719
  200.8 6.5 %collective-permute-done.4.refs_2_ = bf16[320,768]{1,0:T(8,128)(2,1)S(1)} collective-permute-done((bf16[320,768]{1,0:T(8,128)(2,1)S(1)}, bf16[320,768]{1,0:T(8,128)(2,1)S(1)}, u32[]{:S(2)}, u32[]{:S(2)}) %collective-permute-start.4) | collective-permute-done | bytes 491552 | tf_op jit(solution)/shard_map/ppermute | solution.py:719
  208.4 3.8 tail.1
  212.2 5.0 all-to-all-start.5
  220.8 6.5 %all-to-all-done.5 = bf16[4,80,768]{2,1,0:T(8,128)(2,1)S(1)} async-done(((bf16[4,80,768]{2,1,0:T(8,128)(2,1)}), bf16[4,80,768]{2,1,0:T(8,128)(2,1)S(1)}, u32[]{:S(2)}, u32[]{:S(2)}) %all-to-all-start.5) | async-done | bytes 491552 | tf_op jit(solution)/shard_map/all_to_all | solution.py:650
  227.3 3.6 all-to-all-start.8
  232.1 6.1 %all-to-all-done.8 = f32[32,1,288]{2,1,0:T(1,128)S(1)} async-done(((f32[32,1,288]{2,1,0:T(1,128)}), f32[32,1,288]{2,1,0:T(1,128)S(1)}, u32[]{:S(2)}, u32[]{:S(2)}) %all-to-all-start.8) | async-done | bytes 36896 | tf_op jit(solution)/shard_map/all_to_all | solution.py:650
  240.9 102.2 %reduce-scatter.5.cloned.1.call-done = bf16[24,2304]{1,0:T(8,128)(2,1)} async-done(((bf16[768,2304]{1,0:T(8,128)(2,1)}), bf16[24,2304]{1,0:T(8,128)(2,1)}) %reduce-scatter.5.cloned.1.call-update) | async-done | bytes 110608 | tf_op jit(solution)/shard_map/reduce_scatter | solution.py:729
  344.7 109.8 %reduce-scatter.9.cloned.1.call-done = bf16[24,3072]{1,0:T(8,128)(2,1)} async-done(((bf16[768,3072]{1,0:T(8,128)(2,1)}), bf16[24,3072]{1,0:T(8,128)(2,1)}) %reduce-scatter.9.cloned.1.call-update) | async-done | bytes 147472 | tf_op jit(solution)/shard_map/reduce_scatter | solution.py:729
  456.1 110.7 %reduce-scatter.11.cloned.1.call-done = bf16[96,768]{1,0:T(8,128)(2,1)} async-done(((bf16[3072,768]{1,0:T(8,128)(2,1)}), bf16[96,768]{1,0:T(8,128)(2,1)}) %reduce-scatter.11.cloned.1.call-update) | async-done | bytes 147472 | tf_op jit(solution)/shard_map/reduce_scatter | solution.py:729
  566.8 1.6 convert_element_type.23
  (117 shorter events, 30.1 us)
Async XLA Ops:
  7.2 8.8 %copy-start.17 = (f32[768]{0:T(1024)S(1)}, f32[768]{0:T(1024)}, u32[]{:S(2)}) copy-start(f32[768]{0:T(1024)} %param.17) | copy-start | bytes 9220
  7.2 9.4 %copy-start.18 = (f32[768]{0:T(1024)S(1)}, f32[768]{0:T(1024)}, u32[]{:S(2)}) copy-start(f32[768]{0:T(1024)} %param.19) | copy-start | bytes 9220
  7.2 10.0 %copy-start.19 = (f32[768]{0:T(1024)S(1)}, f32[768]{0:T(1024)}, u32[]{:S(2)}) copy-start(f32[768]{0:T(1024)} %param.20) | copy-start | bytes 9220
  9.1 20.1 %all-to-all-start = ((bf16[4,80,768]{2,1,0:T(8,128)(2,1)}), bf16[4,80,768]{2,1,0:T(8,128)(2,1)S(1)}, u32[]{:S(2)}, u32[]{:S(2)}) async-start(bf16[4,80,768]{2,1,0:T(8,128)(2,1)} %slice.45), calls=%async_computation | async-start | bytes 983040 | tf_op jit(solution)/shard_map/all_to_all | solution.py:650
  19.3 14.6 %copy-start.2 = (bf16[5,80,768]{2,1,0:T(8,128)(2,1)S(1)}, bf16[5,80,768]{2,1,0:T(8,128)(2,1)}, u32[]{:S(2)}) copy-start(bf16[5,80,768]{2,1,0:T(8,128)(2,1)} %param.29) | copy-start | bytes 1843204
  23.2 27.4 %copy-start.20 = (f32[768]{0:T(1024)S(1)}, f32[768]{0:T(1024)}, u32[]{:S(2)}) copy-start(f32[768]{0:T(1024)} %param.22) | copy-start | bytes 9220
  23.2 28.0 %copy-start.21 = (f32[768]{0:T(1024)S(1)}, f32[768]{0:T(1024)}, u32[]{:S(2)}) copy-start(f32[768]{0:T(1024)} %param.23) | copy-start | bytes 9220
  23.2 28.6 %copy-start.22 = (f32[768]{0:T(1024)S(1)}, f32[768]{0:T(1024)}, u32[]{:S(2)}) copy-start(f32[768]{0:T(1024)} %param.24) | copy-start | bytes 9220
  23.2 29.2 %copy-start.23 = (f32[768]{0:T(1024)S(1)}, f32[768]{0:T(1024)}, u32[]{:S(2)}) copy-start(f32[768]{0:T(1024)} %param.28) | copy-start | bytes 9220
  29.2 23.8 %copy-start = (bf16[4,80,768]{2,1,0:T(8,128)(2,1)}, bf16[4,80,768]{2,1,0:T(8,128)(2,1)S(1)}, u32[]{:S(2)}) copy-start(bf16[4,80,768]{2,1,0:T(8,128)(2,1)S(1)} %all-to-all-done) | copy-start | bytes 1474564
  29.2 17.9 %all-to-all-start.1 = ((bf16[16,40,384]{2,1,0:T(8,128)(2,1)}), bf16[16,40,384]{2,1,0:T(8,128)(2,1)S(1)}, u32[]{:S(2)}, u32[]{:S(2)}) async-start(bf16[16,40,384]{2,1,0:T(8,128)(2,1)} %get-tuple-element.52), calls=%async_computation.1 | async-start | bytes 983040 | tf_op jit(solution)/shard_map/all_to_all | solution.py:650
  47.1 12.2 %copy-start.3 = (bf16[16,40,384]{2,1,0:T(8,128)(2,1)}, bf16[16,40,384]{2,1,0:T(8,128)(2,1)S(1)}, u32[]{:S(2)}) copy-start(bf16[16,40,384]{2,1,0:T(8,128)(2,1)S(1)} %all-to-all-done.1) | copy-start | bytes 1474564
  47.1 20.0 %all-to-all-start.3 = ((bf16[4,80,768]{2,1,0:T(8,128)(2,1)}), bf16[4,80,768]{2,1,0:T(8,128)(2,1)S(1)}, u32[]{:S(2)}, u32[]{:S(2)}) async-start(bf16[4,80,768]{2,1,0:T(8,128)(2,1)} %slice.47), calls=%async_computation.3 | async-start | bytes 983040 | tf_op jit(solution)/shard_map/all_to_all | solution.py:650
  55.1 17.5 %collective-permute-start = (bf16[320,768]{1,0:T(8,128)(2,1)}, bf16[320,768]{1,0:T(8,128)(2,1)S(1)}, u32[]{:S(2)}, u32[]{:S(2)}) collective-permute-start(bf16[320,768]{1,0:T(8,128)(2,1)} %ln_one.1.refs_0_), channel_id=1, source_target_pairs={{0,2},{2,0},{4,6},{6,4},{1,3},{3,1},{5,7},{7,5},{8,10},{10,8},{12,... | collective-permute-start | bytes 1474568 | tf_op jit(solution)/shard_map/ppermute | solution.py:690
  55.7 21.5 %collective-permute-start.1 = (bf16[320,768]{1,0:T(8,128)(2,1)}, bf16[320,768]{1,0:T(8,128)(2,1)S(1)}, u32[]{:S(2)}, u32[]{:S(2)}) collective-permute-start(bf16[320,768]{1,0:T(8,128)(2,1)} %ln_one.1.refs_0_), channel_id=1, source_target_pairs={{0,4},{2,6},{4,0},{6,2},{1,5},{3,7},{5,1},{7,3},{8,12},{10,14},{12... | collective-permute-start | bytes 1474568 | tf_op jit(solution)/shard_map/ppermute | solution.py:690
  56.6 22.0 %collective-permute-start.2 = (bf16[320,768]{1,0:T(8,128)(2,1)}, bf16[320,768]{1,0:T(8,128)(2,1)}, u32[]{:S(2)}, u32[]{:S(2)}) collective-permute-start(bf16[320,768]{1,0:T(8,128)(2,1)} %ln_one.1.refs_0_), channel_id=1, source_target_pairs={{0,6},{2,4},{4,2},{6,0},{1,7},{3,5},{5,3},{7,1},{8,14},{10,12},{12... | collective-permute-start | bytes 1474568 | tf_op jit(solution)/shard_map/ppermute | solution.py:690
  67.1 27.5 %copy-start.4 = (bf16[4,80,768]{2,1,0:T(8,128)(2,1)}, bf16[4,80,768]{2,1,0:T(8,128)(2,1)S(1)}, u32[]{:S(2)}) copy-start(bf16[4,80,768]{2,1,0:T(8,128)(2,1)S(1)} %all-to-all-done.3) | copy-start | bytes 1474564
  67.1 27.5 %all-to-all-start.2 = ((bf16[16,40,128]{2,1,0:T(8,128)(2,1)}), bf16[16,40,128]{2,1,0:T(8,128)(2,1)S(1)}, u32[]{:S(2)}, u32[]{:S(2)}) async-start(bf16[16,40,128]{2,1,0:T(8,128)(2,1)} %bitcast.33), calls=%async_computation.2 | async-start | bytes 327680 | tf_op jit(solution)/shard_map/all_to_all | solution.py:650
  118.2 15.1 %all-to-all-start.6 = ((bf16[16,40,128]{2,1,0:T(8,128)(2,1)}), bf16[16,40,128]{2,1,0:T(8,128)(2,1)S(1)}, u32[]{:S(2)}, u32[]{:S(2)}) async-start(bf16[16,40,128]{2,1,0:T(8,128)(2,1)} %get-tuple-element.69), calls=%async_computation.6 | async-start | bytes 327680 | tf_op jit(solution)/shard_map/all_to_all | solution.py:650
  125.4 114.1 %reduce-scatter.7.cloned.1.call-start = ((), (), s32[]{:S(2)}) async-start(), calls=%async_computation.14 | async-start | bytes 1216512 | tf_op jit(solution)/shard_map/reduce_scatter | solution.py:729
  142.5 32.3 %all-to-all-start.7 = ((bf16[16,40,384]{2,1,0:T(8,128)(2,1)}), bf16[16,40,384]{2,1,0:T(8,128)(2,1)S(1)}, u32[]{:S(2)}, u32[]{:S(2)}) async-start(bf16[16,40,384]{2,1,0:T(8,128)(2,1)} %bitcast.30), calls=%async_computation.7 | async-start | bytes 983040 | tf_op jit(solution)/shard_map/all_to_all | solution.py:650
  146.1 197.0 %reduce-scatter.5.cloned.1.call-start = ((), (), s32[]{:S(2)}) async-start(), calls=%async_computation.13 | async-start | bytes 3649536 | tf_op jit(solution)/shard_map/reduce_scatter | solution.py:729
  184.1 270.3 %reduce-scatter.9.cloned.1.call-start = ((), (), s32[]{:S(2)}) async-start(), calls=%async_computation.15 | async-start | bytes 4866048 | tf_op jit(solution)/shard_map/reduce_scatter | solution.py:729
  184.9 381.9 %reduce-scatter.11.cloned.1.call-start = ((), (), s32[]{:S(2)}) async-start(), calls=%async_computation.16 | async-start | bytes 4866048 | tf_op jit(solution)/shard_map/reduce_scatter | solution.py:729
  185.4 26.7 %all-to-all-start.4 = ((bf16[4,80,768]{2,1,0:T(8,128)(2,1)}), bf16[4,80,768]{2,1,0:T(8,128)(2,1)S(1)}, u32[]{:S(2)}, u32[]{:S(2)}) async-start(bf16[4,80,768]{2,1,0:T(8,128)(2,1)} %bitcast.7), calls=%async_computation.4 | async-start | bytes 983040 | tf_op jit(solution)/shard_map/all_to_all | solution.py:650
  190.4 10.4 %collective-permute-start.3 = (bf16[320,768]{1,0:T(8,128)(2,1)S(1)}, bf16[320,768]{1,0:T(8,128)(2,1)S(1)}, u32[]{:S(2)}, u32[]{:S(2)}) collective-permute-start(bf16[320,768]{1,0:T(8,128)(2,1)S(1)} %copy-done.31), channel_id=1, source_target_pairs={{0,2},{2,0},{4,6},{6,4},{1,3},{3,1},{5,7},{7,5},{8,10},{10,8},{12,... | collective-permute-start | bytes 1474568 | tf_op jit(solution)/shard_map/ppermute | solution.py:719
  191.9 15.4 %collective-permute-start.4 = (bf16[320,768]{1,0:T(8,128)(2,1)S(1)}, bf16[320,768]{1,0:T(8,128)(2,1)S(1)}, u32[]{:S(2)}, u32[]{:S(2)}) collective-permute-start(bf16[320,768]{1,0:T(8,128)(2,1)S(1)} %copy-done.30), channel_id=1, source_target_pairs={{0,4},{2,6},{4,0},{6,2},{1,5},{3,7},{5,1},{7,3},{8,12},{10,14},{12... | collective-permute-start | bytes 1474568 | tf_op jit(solution)/shard_map/ppermute | solution.py:719
  193.3 14.3 %collective-permute-start.5 = (bf16[320,768]{1,0:T(8,128)(2,1)S(1)}, bf16[320,768]{1,0:T(8,128)(2,1)S(1)}, u32[]{:S(2)}, u32[]{:S(2)}) collective-permute-start(bf16[320,768]{1,0:T(8,128)(2,1)S(1)} %copy-done.29), channel_id=1, source_target_pairs={{0,6},{2,4},{4,2},{6,0},{1,7},{3,5},{5,3},{7,1},{8,14},{10,12},{12... | collective-permute-start | bytes 1474568 | tf_op jit(solution)/shard_map/ppermute | solution.py:719
  208.4 9.3 %copy-start.12 = (f32[1,3072]{1,0:T(1,128)S(1)}, f32[1,3072]{1,0:T(1,128)}, u32[]{:S(2)}) copy-start(f32[1,3072]{1,0:T(1,128)} %get-tuple-element.82) | copy-start | bytes 36868
  212.2 15.2 %all-to-all-start.5 = ((bf16[4,80,768]{2,1,0:T(8,128)(2,1)}), bf16[4,80,768]{2,1,0:T(8,128)(2,1)S(1)}, u32[]{:S(2)}, u32[]{:S(2)}) async-start(bf16[4,80,768]{2,1,0:T(8,128)(2,1)} %bitcast.29), calls=%async_computation.5 | async-start | bytes 983040 | tf_op jit(solution)/shard_map/all_to_all | solution.py:650
  218.5 12.5 %copy-start.9 = (f32[80,768]{1,0:T(8,128)S(1)}, f32[80,768]{1,0:T(8,128)}, u32[]{:S(2)}) copy-start(f32[80,768]{1,0:T(8,128)} %get-tuple-element.75) | copy-start | bytes 737284
  227.3 10.9 %all-to-all-start.8 = ((f32[32,1,288]{2,1,0:T(1,128)}), f32[32,1,288]{2,1,0:T(1,128)S(1)}, u32[]{:S(2)}, u32[]{:S(2)}) async-start(f32[32,1,288]{2,1,0:T(1,128)} %copy.32), calls=%async_computation.8 | async-start | bytes 98304 | tf_op jit(solution)/shard_map/all_to_all | solution.py:650
  (19 other events, 61.1 us)
Sparse Core Ops, SparseCore 0:
  131.3 105.0 reduce-scatter.6
  241.8 101.1 reduce-scatter.4
  348.5 105.8 reduce-scatter.8
  460.7 106.0 reduce-scatter.10

commit v2 on v1

v2 whole, which is shorter than its diff:
```python
import functools

import jax
import jax.numpy as jnp
from jax import lax
from jax.experimental import pallas as pl
from jax.experimental.pallas import tpu as pltpu
from jax.sharding import PartitionSpec as P

HD = 64
NORM_EPS = 1e-06
BF = jnp.bfloat16
F32 = jnp.float32
ALL = ("freq", "tm", "grp")
VMEM_LIMIT = 60 * 1024 * 1024


def nn(a, b):
    return lax.dot_general(a, b, (((1,), (0,)), ((), ())), preferred_element_type=F32)


def nt_dot(a, b):
    return lax.dot_general(a, b, (((1,), (1,)), ((), ())), preferred_element_type=F32)


def tn_dot(a, b):
    return lax.dot_general(a, b, (((0,), (0,)), ((), ())), preferred_element_type=F32)


def normalize(x):
    mean = jnp.mean(x, axis=-1, keepdims=True)
    centered = x - mean
    var = jnp.mean(centered * centered, axis=-1, keepdims=True)
    rstd = lax.rsqrt(var + NORM_EPS)
    return centered * rstd, rstd


def norm_back(e, n, rstd, gain):
    eg = e * gain
    return rstd * (
        eg - jnp.mean(eg, axis=-1, keepdims=True) - n * jnp.mean(eg * n, axis=-1, keepdims=True)
    )


def colsum(x):
    return jnp.sum(x, axis=0, keepdims=True)


def low_lanes(rows):
    return lax.broadcasted_iota(jnp.int32, (rows, 2 * HD), 1) < HD


def swap_halves(x):
    return pltpu.roll(x, HD, 1)


def slot_of(head, nf, nt):
    per = -(-(12) // nf)
    return (head // per) * nt + head % per


def params(count=1):
    return pltpu.CompilerParams(
        dimension_semantics=("arbitrary",) * count, vmem_limit_bytes=VMEM_LIMIT
    )


def full(shape):
    return pl.BlockSpec(shape, lambda *_: (0,) * len(shape))


def cost(flops, nbytes):
    return pl.CostEstimate(flops=int(flops), bytes_accessed=int(nbytes), transcendentals=0)


def pick_kernel(nf, me_ref, x_ref, c_ref, *outs):
    for k in range(nf):
        outs[k][...] = x_ref[me_ref[0] ^ k]
        outs[nf + k][...] = c_ref[me_ref[0] ^ k]


def pick_call(nf, me, x, c):
    _, rows, width = x.shape
    return pl.pallas_call(
        functools.partial(pick_kernel, nf),
        grid_spec=pltpu.PrefetchScalarGridSpec(
            num_scalar_prefetch=1,
            grid=(1,),
            in_specs=[full(x.shape)] * 2,
            out_specs=[full((rows, width))] * (2 * nf),
        ),
        out_shape=[jax.ShapeDtypeStruct((rows, width), BF)] * (2 * nf),
        compiler_params=params(),
        cost_estimate=cost(0, 4 * x.size),
        name="pick",
    )(me, x, c)


def ln_kernel(nf, *refs):
    g_ref, s_ref, n_ref = refs[nf:]
    for k in range(nf):
        rows = refs[k].shape[0]
        n, _ = normalize(refs[k][...].astype(F32))
        n_ref[k * rows : (k + 1) * rows, :] = (n * g_ref[...] + s_ref[...]).astype(BF)


def ln_call(xs, gain, shift):
    rows, width = xs[0].shape
    return pl.pallas_call(
        functools.partial(ln_kernel, len(xs)),
        out_shape=jax.ShapeDtypeStruct((len(xs) * rows, width), BF),
        compiler_params=pltpu.CompilerParams(vmem_limit_bytes=VMEM_LIMIT),
        cost_estimate=cost(len(xs) * rows * width * 10, len(xs) * rows * width * 4),
        name="ln_one",
    )(*xs, gain, shift)


def q5_kernel(nf, nt, x_ref, g_ref, s_ref, w_ref, bq_ref, bv_ref, n_ref, pack_ref):
    rows, width = x_ref.shape
    half = rows // 2
    hat, _ = normalize(x_ref[...].astype(F32))
    n = (hat * g_ref[...] + s_ref[...]).astype(BF)
    n_ref[...] = n
    low = low_lanes(half)
    pack_ref[...] = jnp.zeros_like(pack_ref)
    for part in range(3):
        proj = nn(n, w_ref[:, part * width : (part + 1) * width])
        if part == 0:
            proj = (proj + bq_ref[...]) * (HD**-0.5)
        if part == 2:
            proj = proj + bv_ref[...]
        for pair in range(width // (2 * HD)):
            blk = proj[:, pair * 2 * HD : (pair + 1) * 2 * HD]
            top, bot = blk[:half], blk[half:]
            even = jnp.where(low, top, swap_halves(bot))
            odd = jnp.where(low, swap_halves(top), bot)
            lanes = slice(part * 2 * HD, (part + 1) * 2 * HD)
            pack_ref[slot_of(2 * pair, nf, nt), :, lanes] = even.astype(BF)
            pack_ref[slot_of(2 * pair + 1, nf, nt), :, lanes] = odd.astype(BF)


def q5_call(nf, nt, x, gain, shift, w, bq, bv):
    rows, width = x.shape
    return pl.pallas_call(
        functools.partial(q5_kernel, nf, nt),
        out_shape=(
            jax.ShapeDtypeStruct((rows, width), BF),
            jax.ShapeDtypeStruct((nf * nt, rows // 2, 6 * HD), BF),
        ),
        compiler_params=pltpu.CompilerParams(vmem_limit_bytes=VMEM_LIMIT),
        cost_estimate=cost(2 * rows * w.size, w.size * 2),
        name="q_shared",
    )(x, gain, shift, w, bq, bv)


def spread(x):
    rows = x.shape[0]
    low = low_lanes(rows)
    zero = jnp.zeros_like(x)
    return jnp.concatenate([jnp.where(low, x, zero), jnp.where(low, swap_halves(x), zero)], axis=0)


def unspread(x):
    half = x.shape[0] // 2
    return x[:half] + swap_halves(x[half:])


def softmax_block(q, k, v):
    s = nt_dot(q, k)
    m = jnp.max(s, axis=-1, keepdims=True)
    e = jnp.exp(s - m)
    total = jnp.sum(e, axis=-1, keepdims=True)
    e = e.astype(BF)
    rinv = 1.0 / total
    return e, nn(e, v) * rinv, rinv


def attn5_fwd_kernel(steps, x_ref, o_ref, r_ref, ob_ref, e_ref, qf, kf, vf, of, rf):
    for part, dst in enumerate((qf, kf, vf)):
        blk = x_ref[:, part * 2 * HD : (part + 1) * 2 * HD].astype(F32)
        dst[...] = spread(blk).astype(BF)
    rows = qf.shape[0] // steps
    low = low_lanes(rows)

    def body(i, carry):
        at = pl.ds(pl.multiple_of(i * rows, rows), rows)
        e, o, rinv = softmax_block(qf[at, :], kf[...], vf[...])
        e_ref[at, :] = e
        of[at, :] = o
        rf[at, :] = jnp.where(low, jnp.broadcast_to(rinv, (rows, 2 * HD)), 0.0)
        return carry

    lax.fori_loop(0, steps, body, 0)
    packed = unspread(of[...])
    o_ref[...] = packed
    ob_ref[...] = packed.astype(BF)
    r_ref[...] = unspread(rf[...])


def attn5_fwd_call(x):
    rows = x.shape[0]
    toks = 2 * rows
    return pl.pallas_call(
        functools.partial(attn5_fwd_kernel, 4),
        out_shape=(
            jax.ShapeDtypeStruct((rows, 2 * HD), F32),
            jax.ShapeDtypeStruct((rows, 2 * HD), F32),
            jax.ShapeDtypeStruct((rows, 2 * HD), BF),
            jax.ShapeDtypeStruct((toks, toks), BF),
        ),
        scratch_shapes=[pltpu.VMEM((toks, 2 * HD), BF)] * 3 + [pltpu.VMEM((toks, 2 * HD), F32)] * 2,
        compiler_params=pltpu.CompilerParams(vmem_limit_bytes=VMEM_LIMIT),
        cost_estimate=cost(4 * 4 * toks * toks * 2 * HD, toks * toks * 2),
        name="attn_shared_fwd",
    )(x)


def attn5_bwd_kernel(
    steps, x_ref, ga_ref, o_ref, r_ref, e_ref, out_ref, qf, kf, vf, gf, inn, dq, dk, dv
):
    for part, dst in enumerate((qf, kf, vf)):
        blk = x_ref[:, part * 2 * HD : (part + 1) * 2 * HD].astype(F32)
        dst[...] = spread(blk).astype(BF)
    g = ga_ref[...].astype(F32) * r_ref[...]
    gs = spread(g)
    gf[...] = gs.astype(BF)
    inn[...] = jnp.sum(gs * spread(o_ref[...]), axis=-1, keepdims=True)
    rows = qf.shape[0] // steps
    dk[...] = jnp.zeros_like(dk)
    dv[...] = jnp.zeros_like(dv)

    def body(i, carry):
        at = pl.ds(pl.multiple_of(i * rows, rows), rows)
        e = e_ref[at, :]
        gb = gf[at, :]
        dp = nt_dot(gb, vf[...])
        ds = (e.astype(F32) * (dp - inn[at, :])).astype(BF)
        dq[at, :] = nn(ds, kf[...]) * (HD**-0.5)
        dk[...] += tn_dot(ds, qf[at, :])
        dv[...] += tn_dot(e, gb)
        return carry

    lax.fori_loop(0, steps, body, 0)
    for part, src in enumerate((dq, dk, dv)):
        out_ref[:, part * 2 * HD : (part + 1) * 2 * HD] = unspread(src[...]).astype(BF)


def attn5_bwd_call(x, ga, o, r, e):
    rows = x.shape[0]
    toks = 2 * rows
    return pl.pallas_call(
        functools.partial(attn5_bwd_kernel, 4),
        out_shape=jax.ShapeDtypeStruct((rows, 6 * HD), BF),
        scratch_shapes=[pltpu.VMEM((toks, 2 * HD), BF)] * 4
        + [pltpu.VMEM((toks, 1), F32)]
        + [pltpu.VMEM((toks, 2 * HD), F32)] * 3,
        compiler_params=pltpu.CompilerParams(vmem_limit_bytes=VMEM_LIMIT),
        cost_estimate=cost(8 * 4 * toks * toks * 2 * HD, toks * toks * 2),
        name="attn_shared_bwd",
    )(x, ga, o, r, e)


def attn_fwd_kernel(nt, *refs):
    ns = refs[:nt]
    wq, wk, wv, bq, bv = refs[nt : nt + 5]
    att_ref, o_ref, r_ref, q_ref, k_ref, v_ref, e_ref = refs[nt + 5 :]
    rows = ns[0].shape[0]
    for c in range(nt):
        at = slice(c * rows, (c + 1) * rows)
        x = ns[c][...]
        k_ref[at, :] = nn(x, wk[...]).astype(BF)
        v_ref[at, :] = (nn(x, wv[...]) + bv[...]).astype(BF)
    q_ref[...] = ((nn(ns[0][...], wq[...]) + bq[...]) * (HD**-0.5)).astype(BF)
    low = low_lanes(rows)

    def body(pair, carry):
        lanes = pl.ds(pl.multiple_of(pair * 2 * HD, 2 * HD), 2 * HD)
        q, k, v = q_ref[:, lanes], k_ref[:, lanes], v_ref[:, lanes]
        zero = jnp.zeros_like(q)
        e0, o0, r0 = softmax_block(jnp.where(low, q, zero), k, v)
        e_ref[2 * pair] = e0
        e1, o1, r1 = softmax_block(jnp.where(low, zero, q), k, v)
        e_ref[2 * pair + 1] = e1
        o = jnp.where(low, o0, o1)
        o_ref[:, lanes] = o
        att_ref[:, lanes] = o.astype(BF)
        r_ref[:, lanes] = jnp.where(
            low, jnp.broadcast_to(r0, (rows, 2 * HD)), jnp.broadcast_to(r1, (rows, 2 * HD))
        )
        return carry

    lax.fori_loop(0, q_ref.shape[1] // (2 * HD), body, 0)


def attn_fwd_call(ns, w, bq, bv):
    nt = len(ns)
    rows, width = ns[0].shape
    toks = nt * rows
    blk = 4 * HD
    steps = width // blk
    wspec = [pl.BlockSpec((width, blk), lambda j, p=p: (0, p * steps + j)) for p in range(3)]
    bspec = pl.BlockSpec((1, blk), lambda j: (0, j))
    row = lambda n: pl.BlockSpec((n, blk), lambda j: (0, j))
    return pl.pallas_call(
        functools.partial(attn_fwd_kernel, nt),
        grid=(steps,),
        in_specs=[full((rows, width))] * nt + wspec + [bspec, bspec],
        out_specs=[row(rows)] * 4
        + [row(toks)] * 2
        + [pl.BlockSpec((4, rows, toks), lambda j: (j, 0, 0))],
        out_shape=(
            jax.ShapeDtypeStruct((rows, width), BF),
            jax.ShapeDtypeStruct((rows, width), F32),
            jax.ShapeDtypeStruct((rows, width), F32),
            jax.ShapeDtypeStruct((rows, width), BF),
            jax.ShapeDtypeStruct((toks, width), BF),
            jax.ShapeDtypeStruct((toks, width), BF),
            jax.ShapeDtypeStruct((width // HD, rows, toks), BF),
        ),
        compiler_params=params(),
        cost_estimate=cost(4 * toks * width * width + 16 * rows * toks * width, 20 << 20),
        name="attn_fwd",
    )(*ns, w, w, w, bq, bv)


def attn_bwd_kernel(ga_ref, q_ref, k_ref, v_ref, o_ref, r_ref, e_ref, gq_ref, gk_ref, gv_ref):
    rows = q_ref.shape[0]
    low = low_lanes(rows)
    q, k, v = q_ref[...], k_ref[...], v_ref[...]
    g = ga_ref[...].astype(F32) * r_ref[...]
    go = g * o_ref[...]
    g = g.astype(BF)
    zero = jnp.zeros_like(q)
    halves = []
    for side in range(2):
        mine = low if side == 0 else jnp.logical_not(low)
        qh = jnp.where(mine, q, zero)
        gh = jnp.where(mine, g, zero)
        inner = jnp.sum(jnp.where(mine, go, 0.0), axis=-1, keepdims=True)
        e = e_ref[side]
        dp = nt_dot(gh, v)
        ds = (e.astype(F32) * (dp - inner)).astype(BF)
        halves.append((nn(ds, k), tn_dot(ds, qh), tn_dot(e, gh)))
    gq_ref[...] = (jnp.where(low, halves[0][0], halves[1][0]) * (HD**-0.5)).astype(BF)
    gk_ref[...] = (halves[0][1] + halves[1][1]).astype(BF)
    gv_ref[...] = (halves[0][2] + halves[1][2]).astype(BF)


def attn_bwd_call(first, steps, ga, q, k, v, o, r, e):
    rows, width = q.shape
    toks = k.shape[0]
    blk = 2 * HD
    row = lambda n: pl.BlockSpec((n, blk), lambda j: (0, j + first))
    out = lambda n: pl.BlockSpec((n, blk), lambda j: (0, j))
    return pl.pallas_call(
        attn_bwd_kernel,
        grid=(steps,),
        in_specs=[row(rows), row(rows), row(toks), row(toks), row(rows), row(rows)]
        + [pl.BlockSpec((2, rows, toks), lambda j: (j + first, 0, 0))],
        out_specs=[out(rows), out(toks), out(toks)],
        out_shape=[jax.ShapeDtypeStruct((n, steps * blk), BF) for n in (rows, toks, toks)],
        compiler_params=params(),
        cost_estimate=cost(32 * rows * toks * blk * steps, steps * (4 << 20)),
        name="attn_bwd",
    )(ga, q, k, v, o, r, e)


def dx_kernel(count, widths, *refs):
    gqs, gks, gvs = refs[:count], refs[count : 2 * count], refs[2 * count : 3 * count]
    w_ref, own, dx, uy, d2, u1, total = refs[3 * count :]
    rows, width = own.shape
    half = rows // 2
    step = pl.program_id(0)
    col = 0
    for i, blk in enumerate(widths):
        part = nt_dot(gks[i][...], w_ref[:, width + col : width + col + blk])
        part += nt_dot(gvs[i][...], w_ref[:, 2 * width + col : 2 * width + col + blk])
        if i == 0:
            total[...] = part
        else:
            total[...] += part
        col += blk

    @pl.when(step == 0)
    def _():
        col = 0
        for i, blk in enumerate(widths):
            total[...] += nt_dot(gqs[i][...], w_ref[:, col : col + blk])
            col += blk
        own[...] = total[...]

    def put(c, top, bot):
        @pl.when(step == c)
        def _():
            top[0][top[1]] = total[:half].astype(BF)
            bot[0][bot[1]] = total[half:].astype(BF)

    put(1, (dx, 0), (u1, Ellipsis))
    put(2, (d2, Ellipsis), (uy, 0))
    put(3, (dx, 1), (uy, 1))


def dx_call(gqs, gks, gvs, w):
    rows, width = gqs[0].shape[0], w.shape[0]
    widths = [g.shape[1] for g in gqs]
    shape = jax.ShapeDtypeStruct
    chunk = [pl.BlockSpec((rows, b), lambda j: (j, 0)) for b in widths]
    return pl.pallas_call(
        functools.partial(dx_kernel, len(gqs), widths),
        grid=(4,),
        in_specs=[full(x.shape) for x in gqs] + chunk + chunk + [full(w.shape)],
        out_specs=[full((rows, width))]
        + [full((2, rows // 2, width))] * 2
        + [full((rows // 2, width))] * 2,
        out_shape=[shape((rows, width), F32)]
        + [shape((2, rows // 2, width), BF)] * 2
        + [shape((rows // 2, width), BF)] * 2,
        scratch_shapes=[pltpu.VMEM((rows, width), F32)],
        compiler_params=params(),
        cost_estimate=cost(16 * rows * width * width, 12 << 20),
        name="dx",
    )(*gqs, *gks, *gvs, w)


def put_pieces(me_ref, src, keep_ref, send_ref, index):
    nt, nf = keep_ref.shape[0], keep_ref.shape[1]
    for k in range(nt):
        for f in range(nf):
            at = (f * nt + (me_ref[1] ^ k)) * 2
            keep_ref[(k, f) + index] = src[at + me_ref[2]]
            send_ref[(k, f) + index] = src[at + 1 - me_ref[2]]


def mid_kernel(nf, nt, fast, me_ref, *refs):
    refs = list(refs)
    if fast:
        *refs, down, up, side, sems = refs
    xms, cms, refs = refs[:nf], refs[nf : 2 * nf], refs[2 * nf :]
    att_ref, att5_ref, x5_ref, c5_ref, wo_ref, bo_ref, g2_ref, s2_ref, bd_ref = refs[:9]
    wu_ref, bu_ref, wd_ref, outs_ref, out5_ref, gm_ref, ga_ref, ga5_ref = refs[9:17]
    *grads, vec_ref, gbu_ref, att, cot, mid, hat, rst, two, acc, gn2 = refs[17:]
    step = pl.program_id(0)
    r5, width = x5_ref.shape
    rm = nf * r5
    half = r5 // 2
    low = low_lanes(half)
    pairs = width // (2 * HD)

    @pl.when(step == 0)
    def _():
        att[0:rm, :] = att_ref[...]
        for pair in range(pairs):
            lanes = slice(pair * 2 * HD, (pair + 1) * 2 * HD)
            even = att5_ref[slot_of(2 * pair, nf, nt)].astype(F32)
            odd = att5_ref[slot_of(2 * pair + 1, nf, nt)].astype(F32)
            top = jnp.where(low, even, swap_halves(odd))
            bot = jnp.where(low, swap_halves(even), odd)
            att[rm : rm + r5, lanes] = jnp.concatenate([top, bot], axis=0).astype(BF)
        for k in range(nf):
            cot[k * r5 : (k + 1) * r5, :] = cms[k][...]
        cot[rm : rm + r5, :] = c5_ref[...]
        mid[...] = nn(att[...], wo_ref[...]) + bo_ref[...]
        for k in range(nf):
            mid[k * r5 : (k + 1) * r5, :] += xms[k][...].astype(F32)
        mid[rm : rm + r5, :] += x5_ref[...].astype(F32)
        n, rstd = normalize(mid[...])
        hat[...] = n
        rst[...] = rstd
        two[...] = (n * g2_ref[...] + s2_ref[...]).astype(BF)
        acc[...] = mid[...] + bd_ref[...]
        gn2[...] = jnp.zeros_like(gn2)

    pre = nn(two[...], wu_ref[...]) + bu_ref[...]
    cdf = 0.5 * (1.0 + lax.erf(pre * (0.5**0.5)))
    slope = cdf + pre * (jnp.exp(-0.5 * pre * pre) * 0.3989422804014327)
    act = (pre * cdf).astype(BF)
    acc[...] += nn(act, wd_ref[...])
    dwd = tn_dot(act, cot[...]).astype(BF)
    if fast:
        pd, pu = down.shape[2], up.shape[2]
        owners = down.shape[1]

        def copies(j):
            to_down = grads[0].at[pl.ds(j * owners, owners), pl.ds(0, pd), :]
            to_up = grads[0].at[:, pl.ds(pd + j * pu, pu), :]
            return (
                pltpu.make_async_copy(down.at[j], to_down, sems.at[0, j]),
                pltpu.make_async_copy(up.at[j], to_up, sems.at[1, j]),
            )

        down[step] = dwd.reshape(down.shape[1:])
    else:
        grads[0][...] = dwd
    gpre = (nt_dot(cot[...], wd_ref[...]) * slope).astype(BF)
    gbu_ref[...] = colsum(gpre.astype(F32))
    dwu = tn_dot(two[...], gpre)
    if fast:
        up[step] = dwu.reshape(up.shape[1:]).astype(BF)
        for copy in copies(step):
            copy.start()
    else:
        grads[1][...] = dwu.astype(BF)
    gn2[...] += nt_dot(gpre, wu_ref[...])

    @pl.when(step == pl.num_programs(0) - 1)
    def _():
        for k in range(nf):
            outs_ref[me_ref[0] ^ k] = acc[k * r5 : (k + 1) * r5, :].astype(BF)
        out5_ref[...] = acc[rm : rm + r5, :]
        e = gn2[...]
        n = hat[...]
        c = cot[...].astype(F32)
        gmid = c + norm_back(e, n, rst[...], g2_ref[...])
        gm_ref[...] = gmid
        branch = gmid.astype(BF)
        vec_ref[0:1, :] = colsum(branch.astype(F32))
        vec_ref[1:2, :] = colsum(e * n)
        vec_ref[2:3, :] = colsum(e)
        vec_ref[3:4, :] = colsum(c)
        dwo = tn_dot(att[...], branch)
        if fast:
            side[...] = dwo.reshape(side.shape).astype(BF)
            put_pieces(me_ref, side, grads[1], grads[2], ())
        else:
            grads[2][...] = dwo.astype(BF)
        gatt = nt_dot(branch, wo_ref[...])
        ga_ref[...] = gatt[0:rm].astype(BF)
        ga5_ref[...] = jnp.zeros_like(ga5_ref)
        for pair in range(pairs):
            lanes = slice(pair * 2 * HD, (pair + 1) * 2 * HD)
            top, bot = gatt[rm : rm + half, lanes], gatt[rm + half : rm + r5, lanes]
            even = jnp.where(low, top, swap_halves(bot))
            odd = jnp.where(low, swap_halves(top), bot)
            ga5_ref[slot_of(2 * pair, nf, nt)] = even.astype(BF)
            ga5_ref[slot_of(2 * pair + 1, nf, nt)] = odd.astype(BF)
        if fast:
            for j in range(nf):
                for copy in copies(j):
                    copy.wait()


def mid_call(nf, nt, fast, me, xms, cms, att, att5, x5, c5, wo, bo, g2, s2, bd, wu, bu, wd):
    r5, width = x5.shape
    rm = nf * r5
    rows = rm + r5
    ff = wu.shape[1]
    blk = ff // nf
    shape = jax.ShapeDtypeStruct
    if fast:
        dev = nf * nt * 2
        pd, pu = ff // dev, width // dev
        oshape = (nt, nf, pu, width)
        gspecs = [pl.BlockSpec(memory_space=pl.ANY)] + [full(oshape)] * 2
        gshapes = [shape((dev, pd + nf * pu, width), BF)] + [shape(oshape, BF)] * 2
        extra = [
            pltpu.VMEM((nf, nt * 2, pd, width), BF),
            pltpu.VMEM((nf, dev, pu, width), BF),
            pltpu.VMEM((dev, pu, width), BF),
            pltpu.SemaphoreType.DMA((2, nf)),
        ]
    else:
        gspecs = [
            pl.BlockSpec((blk, width), lambda j, *_: (j, 0)),
            pl.BlockSpec((width, blk), lambda j, *_: (0, j)),
            full((width, width)),
        ]
        gshapes = [shape((ff, width), BF), shape((width, ff), BF), shape((width, width), BF)]
        extra = []
    ins = [*xms, *cms, att, att5, x5, c5, wo, bo, g2, s2, bd]
    return pl.pallas_call(
        functools.partial(mid_kernel, nf, nt, fast),
        grid_spec=pltpu.PrefetchScalarGridSpec(
            num_scalar_prefetch=1,
            grid=(nf,),
            in_specs=[full(x.shape) for x in ins]
            + [
                pl.BlockSpec((width, blk), lambda j, *_: (0, j)),
                pl.BlockSpec((1, blk), lambda j, *_: (0, j)),
                pl.BlockSpec((blk, width), lambda j, *_: (j, 0)),
            ],
            out_specs=[
                full((nf, r5, width)),
                full((r5, width)),
                full((rows, width)),
                full((rm, width)),
                full(att5.shape),
            ]
            + gspecs
            + [full((4, width)), pl.BlockSpec((1, blk), lambda j, *_: (0, j))],
            scratch_shapes=[
                pltpu.VMEM((rows, width), BF),
                pltpu.VMEM((rows, width), BF),
                pltpu.VMEM((rows, width), F32),
                pltpu.VMEM((rows, width), F32),
                pltpu.VMEM((rows, 1), F32),
                pltpu.VMEM((rows, width), BF),
                pltpu.VMEM((rows, width), F32),
                pltpu.VMEM((rows, width), F32),
            ]
            + extra,
        ),
        out_shape=[
            shape((nf, r5, width), BF),
            shape((r5, width), F32),
            shape((rows, width), F32),
            shape((rm, width), BF),
            shape(att5.shape, BF),
        ]
        + gshapes
        + [shape((4, width), F32), shape((1, ff), F32)],
        compiler_params=params(),
        cost_estimate=cost(12 * rows * width * ff + 6 * rows * width * width, 24 << 20),
        name="mid",
    )(me, *ins, wu, bu, wd)


def tail5_kernel(nf, nt, fast, widths, *refs):
    if fast:
        me_ref, *refs = refs
        *refs, side = refs
    count = len(widths)
    gqs, gks, gvs = refs[:count], refs[count : 2 * count], refs[2 * count : 3 * count]
    ns, refs = refs[3 * count : 3 * count + nt], refs[3 * count + nt :]
    g_ref, n5_ref, x5_ref, gm_ref, w_ref, g1_ref = refs[:6]
    (*dwo, gb_ref, gin_ref, vec_ref, g5, dx, dw, xt) = refs[6:]
    step = pl.program_id(0)
    r5, width = x5_ref.shape
    half = r5 // 2
    low = low_lanes(half)
    for pair in range(width // (2 * HD)):
        lanes = slice(pair * 2 * HD, (pair + 1) * 2 * HD)
        even = g_ref[slot_of(2 * pair, nf, nt)].astype(F32)
        odd = g_ref[slot_of(2 * pair + 1, nf, nt)].astype(F32)
        top = jnp.where(low, even, swap_halves(odd))
        bot = jnp.where(low, swap_halves(even), odd)
        g5[:, lanes] = jnp.concatenate([top, bot], axis=0).astype(BF)
    g = g5[...]
    gb5 = colsum(g.astype(F32))
    rows = ns[0].shape[0]

    def add(mains, chunks):
        col = 0
        for main, blk in zip(mains, widths):
            lanes = slice(col, col + blk)
            gb_ref[0, :, lanes] = gb5[:, lanes] + colsum(main[...].astype(F32))
            dw[:, lanes] = nn(xt[:, 0 : chunks * rows], main[...]) + tn_dot(n5_ref[...], g[:, lanes])
            col += blk

    @pl.when(step == 0)
    def _():
        dx[...] = jnp.zeros_like(dx)
        for c in range(nt):
            xt[:, c * rows : (c + 1) * rows] = ns[c][...].T
        add(gqs, 1)

    @pl.when(step == 1)
    def _():
        add(gks, nt)

    @pl.when(step == 2)
    def _():
        add(gvs, nt)

    if fast:
        side[...] = dw[...].reshape(side.shape).astype(BF)
        put_pieces(me_ref, side, dwo[0], dwo[1], (0,))
    else:
        dwo[0][...] = dw[...].astype(BF)

    dx[...] += nt_dot(g, w_ref[...])

    @pl.when(step == pl.num_programs(0) - 1)
    def _():
        n, rstd = normalize(x5_ref[...].astype(F32))
        e = dx[...]
        gin_ref[...] = gm_ref[...] + norm_back(e, n, rstd, g1_ref[...])
        vec_ref[0:1, :] = colsum(e * n)
        vec_ref[1:2, :] = colsum(e)


def tail5_call(nf, nt, fast, me, gqs, gks, gvs, ns, g, n5, x5, gm, w, g1):
    r5, width = x5.shape
    at = gm.shape[0] // r5 - 1
    bshape = jax.ShapeDtypeStruct
    if fast:
        pu = width // (nf * nt * 2)
        wspecs = [pl.BlockSpec((nt, nf, 1, pu, width), lambda j, *_: (0, 0, j, 0, 0))] * 2
        wshapes = [bshape((nt, nf, 3, pu, width), BF)] * 2
        extra = [pltpu.VMEM((nf * nt * 2, pu, width), BF)]
    else:
        wspecs = [pl.BlockSpec((width, width), lambda j, *_: (0, j))]
        wshapes = [bshape((width, 3 * width), BF)]
        extra = []
    return pl.pallas_call(
        functools.partial(tail5_kernel, nf, nt, fast, [x.shape[1] for x in gqs]),
        grid_spec=pltpu.PrefetchScalarGridSpec(
            num_scalar_prefetch=int(fast),
            grid=(3,),
            in_specs=[full(x.shape) for x in (*gqs, *gks, *gvs, *ns)]
            + [
                pl.BlockSpec((g.shape[0], r5 // 2, 2 * HD), lambda j, *_: (0, 0, j)),
                full(n5.shape),
                full(x5.shape),
                pl.BlockSpec((r5, width), lambda j, *_: (at, 0)),
                pl.BlockSpec((width, width), lambda j, *_: (0, j)),
                full((1, width)),
            ],
            out_specs=wspecs
            + [
                pl.BlockSpec((1, 1, width), lambda j, *_: (j, 0, 0)),
                full((r5, width)),
                full((2, width)),
            ],
            scratch_shapes=[
                pltpu.VMEM((r5, width), BF),
                pltpu.VMEM((r5, width), F32),
                pltpu.VMEM((width, width), F32),
                pltpu.VMEM((width, nt * ns[0].shape[0]), BF),
            ]
            + extra,
        ),
        out_shape=wshapes
        + [
            bshape((3, 1, width), F32),
            bshape((r5, width), F32),
            bshape((2, width), F32),
        ],
        compiler_params=params(),
        cost_estimate=cost(4 * r5 * width * width * 3 + 4 * width * width * 1280, 16 << 20),
        name="tail_shared",
    )(*([me] if fast else []), *gqs, *gks, *gvs, *ns, g, n5, x5, gm, w, g1)


def tail_kernel(nf, me_ref, own, gx, gy, rd, ru, *refs):
    xs, (gm_ref, g1_ref, gin_ref, vec_ref) = refs[:nf], refs[nf:]
    rows = xs[0].shape[0]
    half = rd.shape[0]
    gain_sum = shift_sum = 0.0
    for k in range(nf):
        at = slice(k * rows, (k + 1) * rows)
        lower = k * rows < half
        one, two = (gx, rd) if lower else (gy, ru)
        part = slice(k * rows, (k + 1) * rows) if lower else slice(k * rows - half, (k + 1) * rows - half)
        e = own[at, :] + one[0, part, :].astype(F32) + two[part, :].astype(F32)
        n, rstd = normalize(xs[k][...].astype(F32))
        gin_ref[me_ref[0] ^ k] = (gm_ref[at, :] + norm_back(e, n, rstd, g1_ref[...])).astype(BF)
        gain_sum += colsum(e * n)
        shift_sum += colsum(e)
    vec_ref[0:1, :] = gain_sum
    vec_ref[1:2, :] = shift_sum


def tail_call(me, own, gx, gy, rd, ru, xs, gm, g1):
    rows, width = xs[0].shape
    nf = len(xs)
    half = nf * rows // 2
    return pl.pallas_call(
        functools.partial(tail_kernel, nf),
        grid_spec=pltpu.PrefetchScalarGridSpec(
            num_scalar_prefetch=1,
            grid=(1,),
            in_specs=[full((nf * rows, width))]
            + [full((1, half, width))] * 2
            + [full((half, width))] * 2
            + [full((rows, width))] * nf
            + [full((nf * rows, width)), full((1, width))],
            out_specs=[full((nf, rows, width)), full((2, width))],
        ),
        out_shape=[
            jax.ShapeDtypeStruct((nf, rows, width), BF),
            jax.ShapeDtypeStruct((2, width), F32),
        ],
        compiler_params=params(),
        cost_estimate=cost(30 * nf * rows * width, 6 << 20),
        name="tail",
    )(me, own, gx, gy, rd, ru, *xs, gm, g1)


def pair_sum_kernel(nd, nu, *refs):
    ins, (dx, d0, d2, uy, u0, u1) = refs[: 2 * (nd + nu)], refs[2 * (nd + nu) :]
    outs = ((d0, (dx, 0), d2, (dx, 1)), (u0, u1, (uy, 0), (uy, 1)))
    for side, pairs in enumerate((ins[: 2 * nd], ins[2 * nd :])):
        at = 0
        for keep, got in zip(pairs[0::2], pairs[1::2]):
            rows = keep.shape[2]
            for k in range(4):
                total = (keep[k, 0].astype(F32) + got[k, 0].astype(F32)).astype(BF)
                out = outs[side][k]
                if isinstance(out, tuple):
                    out[0][out[1], 0, at : at + rows, :] = total
                else:
                    out[0, at : at + rows, :] = total
            at += rows


def pair_sum(ds, us, steps):
    width = ds[0][0].shape[3]
    specs, args = [], []
    for keep, got, first in ds + us:
        spec = pl.BlockSpec((4, 1) + keep.shape[2:], lambda j, f=first: (0, j + f, 0, 0))
        specs += [spec, spec]
        args += [keep, got]
    ospecs, oshapes = [], []
    for side in (ds, us):
        rows = sum(x[0].shape[2] for x in side)
        one = pl.BlockSpec((1, rows, width), lambda j: (j, 0, 0))
        two = pl.BlockSpec((2, 1, rows, width), lambda j: (0, j, 0, 0))
        ospecs += [two, one, one]
        oshapes += [
            jax.ShapeDtypeStruct((2, steps, rows, width), BF),
            jax.ShapeDtypeStruct((steps, rows, width), BF),
            jax.ShapeDtypeStruct((steps, rows, width), BF),
        ]
    return pl.pallas_call(
        functools.partial(pair_sum_kernel, len(ds), len(us)),
        grid=(steps,),
        in_specs=specs,
        out_specs=ospecs,
        out_shape=oshapes,
        compiler_params=params(),
        cost_estimate=cost(1 << 20, 8 << 20),
        name="pair_sum",
    )(*args)


def relay_sum_kernel(d2, gx, u1, gy, sd, su):
    sd[...] = (d2[...].astype(F32) + gx[0].astype(F32)).astype(BF)
    su[...] = (u1[...].astype(F32) + gy[0].astype(F32)).astype(BF)


def relay_sum(d2, gx, u1, gy):
    second = lambda x: pl.BlockSpec((1,) + x.shape[1:], lambda *_: (1,) + (0,) * (x.ndim - 1))
    return pl.pallas_call(
        relay_sum_kernel,
        grid=(1,),
        in_specs=[full(d2.shape), second(gx), full(u1.shape), second(gy)],
        out_specs=[full(d2.shape), full(u1.shape)],
        out_shape=[jax.ShapeDtypeStruct(d2.shape, BF), jax.ShapeDtypeStruct(u1.shape, BF)],
        compiler_params=params(),
        cost_estimate=cost(d2.size, 6 * d2.size),
        name="relay_sum",
    )(d2, gx, u1, gy)


def along(axis, k, x):
    return lax.ppermute(x, axis, [(i, i ^ k) for i in range(4)])


def relay_start(dx, uy):
    return along("tm", 1, dx), along("tm", 2, uy)


def relay_end(gx, gy, d2, u1):
    sd, su = relay_sum(d2, gx, u1, gy)
    return along("tm", 2, sd), along("tm", 1, su)


def tm_sum_kernel(nf, groups, me_ref, *refs):
    count = len(groups)
    outs, total = refs[3 * count : 3 * count + nf], refs[-1]
    for i, (first, blocks, at) in enumerate(groups):
        own, gx, rd = refs[3 * i : 3 * i + 3]
        rows = own.shape[1]
        for f in range(blocks):
            part = own[f].astype(F32) + gx[0, f].astype(F32) + rd[f].astype(F32)
            total[first + f, at : at + rows, :] = part.astype(BF)
    for k in range(nf):
        outs[k][...] = total[me_ref[0] ^ k]


def tm_sum(nf, me, groups):
    specs, args, where, rows = [], [], [], 0
    for own, gx, rd, first, at in groups:
        specs += [full(own.shape), full((1,) + own.shape), full(own.shape)]
        args += [own, gx, rd]
        where.append((first, own.shape[0], at))
        rows = max(rows, at + own.shape[1])
    width = groups[0][0].shape[2]
    return pl.pallas_call(
        functools.partial(tm_sum_kernel, nf, where),
        grid_spec=pltpu.PrefetchScalarGridSpec(
            num_scalar_prefetch=1,
            grid=(1,),
            in_specs=specs,
            out_specs=[full((rows, width))] * nf,
            scratch_shapes=[pltpu.VMEM((nf, rows, width), BF)],
        ),
        out_shape=[jax.ShapeDtypeStruct((rows, width), BF)] * nf,
        compiler_params=params(),
        cost_estimate=cost(1 << 20, 5 << 20),
        name="tm_sum",
    )(me, *args)


def last_sum_kernel(nf, places, *refs):
    parts, outs = refs[:nf], refs[nf:]
    for at, rows, out, col in places:
        lanes = parts[0].shape[1]
        total = parts[0][at : at + rows, :].astype(F32)
        for part in parts[1:]:
            total = total + part[at : at + rows, :].astype(F32)
        outs[out][:, col : col + lanes] = total


def last_sum(parts, places, shapes):
    nf = len(parts)
    return pl.pallas_call(
        functools.partial(last_sum_kernel, nf, places),
        out_shape=[jax.ShapeDtypeStruct(x, F32) for x in shapes],
        compiler_params=pltpu.CompilerParams(vmem_limit_bytes=VMEM_LIMIT),
        cost_estimate=cost(nf * parts[0].size, 2 * nf * parts[0].size),
        name="last_sum",
    )(*parts)


def swap_cores(x):
    return lax.ppermute(x, "grp", [(0, 1), (1, 0)])


def exchange(axis, parts):
    pairs = lambda k: [(i, i ^ k) for i in range(len(parts))]
    return [parts[0]] + [lax.ppermute(parts[k], axis, pairs(k)) for k in range(1, len(parts))]


def tie(x, *deps):
    flat, tree = jax.tree.flatten(x)
    tied = lax.optimization_barrier((flat, deps))[0]
    return jax.tree.unflatten(tree, tied)


def over(axes, x):
    return lax.all_to_all(x, axes, 0, 0)


def local(
    nf,
    nt,
    ng,
    inputs,
    gain_one,
    shift_one,
    w_qkv,
    bias_query,
    bias_value,
    w_out,
    bias_out,
    gain_two,
    shift_two,
    w_up,
    bias_up,
    w_down,
    bias_down,
    cotangent,
):
    _, r, width = inputs.shape
    ff = w_up.shape[1]
    dev = nf * nt * ng
    per = width // dev
    fast = ng == 2 and per % 8 == 0 and ff // nf == width
    me = jnp.stack([lax.axis_index(a) for a in ALL]).astype(jnp.int32)
    g1, s1 = gain_one[None], shift_one[None]
    bq, bv = bias_query[None], bias_value[None]
    both = ("freq", "tm")
    x5, c5 = inputs[nf], cotangent[nf]

    picked = pick_call(nf, me, inputs, cotangent)
    xs = exchange("freq", picked[:nf])
    n5, pack5 = q5_call(nf, nt, x5, g1, s1, w_qkv, bq, bv)
    nm = ln_call(tie(xs, pack5), g1, s1)
    ns = exchange("tm", [nm] * nt)
    got5 = over(both, tie(pack5, nm)).reshape(-1, 6 * HD)
    cs = exchange("freq", tie(picked[nf:], got5))
    o5, r5, ob5, e5 = attn5_fwd_call(got5)
    att5 = over(both, ob5.reshape(nf * nt, r // 2, 2 * HD))
    att, o, rr, q, k, v, e = attn_fwd_call(tie(ns, ob5), w_qkv, bq, bv)
    bout, g2, s2, bdown, bup = (x[None] for x in (bias_out, gain_two, shift_two, bias_down, bias_up))
    outs, out5, gm, ga, ga5, *dws, vec, gbu = mid_call(
        nf, nt, fast, me, xs, cs, att, att5, x5, c5, w_out, bout, g2, s2, bdown, w_up, bup, w_down
    )
    pieces = lambda x: x.reshape(nt, nf, -1, width)
    half, pd = nf // 2, ff // dev
    if fast:
        dff = lax.psum_scatter(dws[0].reshape(-1, width), ALL, scatter_dimension=0, tiled=True)
        keep_o, got_o = pieces(dws[1]), pieces(swap_cores(dws[2]))
    got_ga5 = over(both, ga5).reshape(-1, 2 * HD)
    block0 = attn_bwd_call(0, 3, ga, q, k, v, o, rr, e)
    order = block0[0]
    g5 = attn5_bwd_call(got5, tie(got_ga5, order), o5, r5, e5).reshape(nf * nt, r // 2, 6 * HD)
    order = g5
    g5 = over(both, g5)
    block1 = attn_bwd_call(3, 3, tie(ga, order), q, k, v, o, rr, e)
    gqs, gks, gvs = zip(block0, block1)
    own, dxm, uym, d2m, u1m = dx_call(gqs, gks, gvs, w_qkv)
    gxm, gym = relay_start(dxm, uym)
    order = own
    outs = over("freq", tie(outs, order))
    *dwqkv, gb, gin5, vec5 = tail5_call(
        nf, nt, fast, me, tie(gqs, order), gks, gvs, ns, g5, n5, x5, gm, w_qkv, g1
    )
    order = gb
    if fast:
        keep, got = pieces(dwqkv[0]), pieces(swap_cores(dwqkv[1]))
    sdm, sum_ = relay_sum(*tie((d2m, gxm, u1m, gym), order))
    rdm, rum = along("tm", 2, sdm), along("tm", 1, sum_)
    gin, vec_m = tail_call(me, own, gxm, gym, rdm, rum, xs, gm, g1)
    order = vec_m
    gin = over("freq", gin)
    if fast:
        dxq, d0q, d2q, uyq, u0q, u1q = pair_sum(
            [(keep, tie(got, order), 0), (keep_o, got_o, 0)],
            [(keep, got, half), (keep_o, got_o, half)],
            half,
        )
        gxq, gyq = relay_start(dxq, uyq)
        sdq, suq = relay_sum(d2q, gxq, u1q, gyq)
        rdq, ruq = along("tm", 2, sdq), along("tm", 1, suq)
        sums_q = exchange(
            "freq", tm_sum(nf, me, [(d0q, gxq, rdq, 0, 0), (u0q, gyq, ruq, half, 0)])
        )
        places = [(i * per, per, 0, i * width) for i in range(3)] + [(3 * per, per, 1, 0)]
        dwqkv, dwo = last_sum(sums_q, places, [(per, 3 * width), (per, width)])
        dwd = dff[:pd].astype(F32)
        dwu = dff[pd:].astype(F32).reshape(nf, per, width).transpose(1, 0, 2).reshape(per, ff)
    else:
        dwd, dwu, dwo, dwqkv = (
            lax.psum_scatter(x, ALL, scatter_dimension=0, tiled=True).astype(F32)
            for x in dws + dwqkv
        )
    block_out = jnp.concatenate([outs.astype(F32), out5[None]], axis=0)
    grad_in = jnp.concatenate([gin.astype(F32), gin5[None]], axis=0)
    vec1 = vec_m + vec5
    small = jnp.concatenate([vec1, vec, gb[0], gb[2]], axis=0)
    small = small.reshape(8, dev, width // dev).transpose(1, 0, 2).reshape(dev, -1)
    small = jnp.concatenate([small, gbu.reshape(dev, ff // dev)], axis=1)
    small = jnp.sum(over(ALL, small), axis=0)
    piece = lambda i: small[i * per : (i + 1) * per]
    return (
        block_out,
        grad_in,
        piece(0),
        piece(1),
        dwqkv,
        piece(6),
        piece(7),
        dwo,
        piece(2),
        piece(3),
        piece(4),
        dwu,
        small[8 * per :],
        dwd,
        piece(5),
    )


def solution(mesh):
    tokens = P("grp", ("freq", "tm"), None)
    vec = P(ALL)
    mat = P(ALL, None)
    return jax.shard_map(
        functools.partial(local, mesh.shape["freq"], mesh.shape["tm"], mesh.shape["grp"]),
        mesh=mesh,
        in_specs=(tokens,) + (P(),) * 13 + (tokens,),
        out_specs=(
            tokens,
            tokens,
            vec,
            vec,
            mat,
            vec,
            vec,
            mat,
            vec,
            vec,
            vec,
            mat,
            vec,
            mat,
            vec,
        ),
        check_vma=False,
    )
```

time: 576 us -> 292 us (0.51)
  waiting for transfers between devices: 382 us -> 41.7 us
  Pallas kernels: 102 us -> 129 us
  blocking collectives: 0 us -> 16.4 us
  starting transfers between devices: 51.5 us -> 62.8 us
  local copies, waits for them, and re-layouts: 15.3 us -> 21.1 us
    reduce_scatter x4 -> x1, waiting for transfers between devices: 323 us -> 0.01 us  [local(): lax.psum_scatter(dws[0].reshape(-1, width), ALL, scatter_dimension=0, til...]
    all_to_all x9 -> x6, waiting for transfers between devices: 38.2 us -> 6.51 us  [over(): return lax.all_to_all(x, axes, 0, 0)]
    pallas_call x5 -> x13, Pallas kernels: 66 us -> 88.7 us  [the longest x1 22.9 us: mid_call(): pl.pallas_call(functools.partial(mid_kernel, nf, nt, fast), grid_spec=plt...]
    ppermute x6 -> x22, starting transfers between devices: 6.98 us -> 27.1 us  [the longest x12 17.9 us: exchange(): lax.ppermute(parts[k], axis, pairs(k))]
    all_to_all x0 -> x1, blocking collectives: none -> 16.4 us  [over(): return lax.all_to_all(x, axes, 0, 0)]
    ppermute x6 -> x22, waiting for transfers between devices: 19.7 us -> 35.2 us  [the longest x8 23.7 us: along(): return lax.ppermute(x, axis, [(i, i ^ k) for i in range(4)])]
    all_to_all x9 -> x6, starting transfers between devices: 44.2 us -> 35.5 us  [over(): return lax.all_to_all(x, axes, 0, 0)]
  transfers between devices with their start and end apart: 19 -> 29, of which waited for: 13 -> 11; matrix products, arithmetic and copies ran while one was open for 3% -> 6% of each run, Pallas kernels for 14% -> 35%
where the time goes in v2:
time: 292 us; the launch traced here: 291 us
  Pallas kernels  129 us (44%)
  starting transfers between devices  62.8 us (22%)
  waiting for transfers between devices  41.7 us (14%)
  local copies, waits for them, and re-layouts  21.1 us (7%)
  blocking collectives  16.4 us (6%)
  between operations  14.6 us (5%)
  other arithmetic  5.57 us (2%)
    all_to_all x6, starting transfers between devices, over(): return lax.all_to_all(x, axes, 0, 0)  35.5 us
    ppermute x8, waiting for transfers between devices, along(): return lax.ppermute(x, axis, [(i, i ^ k) for i in range(4)])  23.7 us
    pallas_call x1, Pallas kernels, mid_call(): pl.pallas_call(functools.partial(mid_kernel, nf, nt, fast), grid_spec=plt...  22.9 us
    pallas_call x1, Pallas kernels, attn_fwd_call(): pl.pallas_call(functools.partial(attn_fwd_kernel, nt), grid=(steps,), in_...  19.5 us
    pallas_call x2, Pallas kernels, attn_bwd_call(): pl.pallas_call(attn_bwd_kernel, grid=(steps,), in_specs=[row(rows), row(r...  18.2 us
    ppermute x12, starting transfers between devices, exchange(): lax.ppermute(parts[k], axis, pairs(k))  17.9 us
    all_to_all x1, blocking collectives, over(): return lax.all_to_all(x, axes, 0, 0)  16.4 us
    pallas_call x1, Pallas kernels, tail5_call(): pl.pallas_call(functools.partial(tail5_kernel, nf, nt, fast, [x.shape[1]...  14.9 us
  transfers between devices with their start and end apart: 29, of which 11 were waited for; matrix products, arithmetic and copies ran while one was open for 6% of the time, Pallas kernels for 35%

profile of v2, /device:TPU:0, one launch (start us, length us, event | category | flops | bytes accessed | tf_op | source)
XLA Modules:
  0.0 290.7 jit_solution(13563345117128116223)
XLA Ops:
  7.8 2.9 %pick.1 = (bf16[80,768]{1,0:T(8,128)(2,1)}, bf16[80,768]{1,0:T(8,128)(2,1)}, bf16[80,768]{1,0:T(8,128)(2,1)}, bf16[80,768]{1,0:T(8,128)(2,1)}, bf16[80,768]{1,0:...) custom-call(s32[3]{0:T(128)} %pad_add_fusion.me_ref.refs_0_, ...), custom_call_target="tpu_custom_call" | custom-call | bytes 1228800 | tf_op jit(solution)/shard_map/pick/pallas_call | solution.py:84
  10.7 3.0 %collective-permute-start = (bf16[80,768]{1,0:T(8,128)(2,1)}, bf16[80,768]{1,0:T(8,128)(2,1)S(1)}, u32[]{:S(2)}, u32[]{:S(2)}) collective-permute-start(bf16[80,768]{1,0:T(8,128)(2,1)} %get-tuple-element.104), channel_id=1, source_target_pairs={{0,8},{8,0},{16,24},{24,16},{1,9},{9,1},{17,25},{25,17},{2,10},{10... | collective-permute-start | bytes 368648 | tf_op jit(solution)/shard_map/ppermute | solution.py:922
  13.7 2.6 collective-permute-start.1
  23.0 3.8 %q_shared.1 = (bf16[80,768]{1,0:T(8,128)(2,1)}, bf16[16,40,384]{2,1,0:T(8,128)(2,1)}) custom-call(bf16[80,768]{1,0:T(8,128)(2,1)} %slice_bitcast_fusion.1.x_ref.refs_10_.refs_13_, f32[1,768]{1,0:T(1,128)} %broadcast_in_dim.33.g_ref.refs_4_.refs_16_.refs_5_, f32[1,768]{1,0:T(1,128)} %broadcast_in_dim.34.s_ref.refs_5_, bf16[768,2304]{1,0:T(8,128)(2,1)} %refs_15_.1, ...), custom_call_target="tpu_custom_call" | custom-call | flops 283115520 | bytes 3538944 | tf_op jit(solution)/shard_map/q_shared/pallas_call | solution.py:144
  29.8 7.1 %all-to-all-start = ((bf16[16,40,384]{2,1,0:T(8,128)(2,1)}), bf16[16,40,384]{2,1,0:T(8,128)(2,1)S(1)}, u32[]{:S(2)}, u32[]{:S(2)}) async-start(bf16[16,40,384]{2,1,0:T(8,128)(2,1)} %get-tuple-element.116), calls=%async_computation | async-start | bytes 983040 | tf_op jit(solution)/shard_map/all_to_all | solution.py:932
  39.3 2.8 collective-permute-start.8
  44.4 6.5 %all-to-all-done = bf16[16,40,384]{2,1,0:T(8,128)(2,1)S(1)} async-done(((bf16[16,40,384]{2,1,0:T(8,128)(2,1)}), bf16[16,40,384]{2,1,0:T(8,128)(2,1)S(1)}, u32[]{:S(2)}, u32[]{:S(2)}) %all-to-all-start) | async-done | bytes 491552 | tf_op jit(solution)/shard_map/all_to_all | solution.py:932
  53.1 7.8 %attn_shared_fwd.1 = (f32[640,128]{1,0:T(8,128)}, f32[640,128]{1,0:T(8,128)}, bf16[640,128]{1,0:T(8,128)(2,1)}, bf16[1280,1280]{1,0:T(8,128)(2,1)}) custom-call(bf16[640,384]{1,0:T(8,128)(2,1)} %bitcast.33), custom_call_target="tpu_custom_call" | custom-call | flops 3355443200 | bytes 3276800 | tf_op jit(solution)/shard_map/attn_shared_fwd/pallas_call | solution.py:203
  63.2 2.9 collective-permute-done.7.refs_2_.refs_9_
  66.4 5.4 %all-to-all-start.1 = ((bf16[16,40,128]{2,1,0:T(8,128)(2,1)}), bf16[16,40,128]{2,1,0:T(8,128)(2,1)S(1)}, u32[]{:S(2)}, u32[]{:S(2)}) async-start(bf16[16,40,128]{2,1,0:T(8,128)(2,1)} %bitcast.39), calls=%async_computation.1 | async-start | bytes 327680 | tf_op jit(solution)/shard_map/all_to_all | solution.py:932
  72.1 19.5 %attn_fwd.1 = (bf16[320,768]{1,0:T(8,128)(2,1)}, f32[320,768]{1,0:T(8,128)}, f32[320,768]{1,0:T(8,128)}, bf16[320,768]{1,0:T(8,128)(2,1)}, bf16[1280,768]{1,0:T(...) custom-call(bf16[320,768]{1,0:T(8,128)(2,1)} %ln_one.1.refs_0_.refs_7_, ...), custom_call_target="tpu_custom_call" | custom-call | flops 8053063680 | bytes 20971520 | tf_op jit(solution)/shard_map/attn_fwd/pallas_call | solution.py:304
  92.4 22.9 %mid.1 = (bf16[4,80,768]{2,1,0:T(8,128)(2,1)}, f32[80,768]{1,0:T(8,128)}, f32[400,768]{1,0:T(8,128)}, bf16[320,768]{1,0:T(8,128)(2,1)}, bf16[16,40,128]{2,1,0:T(...) custom-call(s32[3]{0:T(128)} %pad_add_fusion.me_ref.refs_0_, ...), custom_call_target="tpu_custom_call" | custom-call | flops 12740198400 | bytes 25165824 | tf_op jit(solution)/shard_map/mid/pallas_call | solution.py:570
  115.3 6.9 %all-to-all-start.2 = ((bf16[16,40,128]{2,1,0:T(8,128)(2,1)}), bf16[16,40,128]{2,1,0:T(8,128)(2,1)S(1)}, u32[]{:S(2)}, u32[]{:S(2)}) async-start(bf16[16,40,128]{2,1,0:T(8,128)(2,1)} %get-tuple-element.136), calls=%async_computation.2 | async-start | bytes 327680 | tf_op jit(solution)/shard_map/all_to_all | solution.py:932
  122.2 9.1 %attn_bwd.2 = (bf16[320,384]{1,0:T(8,128)(2,1)}, bf16[1280,384]{1,0:T(8,128)(2,1)}, bf16[1280,384]{1,0:T(8,128)(2,1)}) custom-call(bf16[320,768]{1,0:T(8,128)(2,1)} %get-tuple-element.141.ga_ref, bf16[320,768]{1,0:T(8,128)(2,1)} %get-tuple-element.129.q_ref, bf16[1280,768]{1,0:T(8,128)(2,1)} %get-tuple-element.130.k_ref, ...), custom_call_target="tpu_custom_call" | custom-call | flops 5033164800 | bytes 12582912 | tf_op jit(solution)/shard_map/attn_bwd/pallas_call | solution.py:355
  132.0 8.8 %attn_shared_bwd.1 = bf16[640,384]{1,0:T(8,128)(2,1)} custom-call(bf16[640,384]{1,0:T(8,128)(2,1)} %bitcast.34, bf16[640,128]{1,0:T(8,128)(2,1)} %bitcast.40, f32[640,128]{1,0:T(8,128)} %get-tuple-element.138.o_ref, f32[640,128]{1,0:T(8,128)} %get-tuple-element.139.r_ref, bf16[1280,1280]{1,0:T(8,128)(2,1)} %get-tuple-element.140.e_ref), custom_call_target="tpu_custom_call" | custom-call | flops 6710886400 | bytes 3276800 | tf_op jit(solution)/shard_map/attn_shared_bwd/pallas_call | solution.py:251
  140.7 6.9 %all-to-all-start.4 = ((bf16[16,40,384]{2,1,0:T(8,128)(2,1)}), bf16[16,40,384]{2,1,0:T(8,128)(2,1)S(1)}, u32[]{:S(2)}, u32[]{:S(2)}) async-start(bf16[16,40,384]{2,1,0:T(8,128)(2,1)} %bitcast.35), calls=%async_computation.4 | async-start | bytes 983040 | tf_op jit(solution)/shard_map/all_to_all | solution.py:932
  147.7 9.2 %attn_bwd.3 = (bf16[320,384]{1,0:T(8,128)(2,1)}, bf16[1280,384]{1,0:T(8,128)(2,1)}, bf16[1280,384]{1,0:T(8,128)(2,1)}) custom-call(bf16[320,768]{1,0:T(8,128)(2,1)} %get-tuple-element.141.ga_ref, bf16[320,768]{1,0:T(8,128)(2,1)} %get-tuple-element.129.q_ref, bf16[1280,768]{1,0:T(8,128)(2,1)} %get-tuple-element.130.k_ref, ...), custom_call_target="tpu_custom_call" | custom-call | flops 5033164800 | bytes 12582912 | tf_op jit(solution)/shard_map/attn_bwd/pallas_call | solution.py:355
  156.8 10.0 %dx.1 = (f32[320,768]{1,0:T(8,128)}, bf16[2,160,768]{2,1,0:T(8,128)(2,1)}, bf16[2,160,768]{2,1,0:T(8,128)(2,1)}, bf16[160,768]{1,0:T(8,128)(2,1)}, bf16[160,768]{1,0:T(8,128)(2,1)}) custom-call(bf16[320,384]{1,0:T(8,128)(2,1)} %get-tuple-element.154.refs_0_.refs_1_, bf16[320,384]{1,0:T(8,128)(2,1)} %get-tuple-element.155.refs_1_.refs_2_, ...), custom_call_target="tpu_custom_call" | custom-call | flops 3019898880 | bytes 12582912 | tf_op jit(solution)/shard_map/dx/pallas_call | solution.py:408
  167.7 14.9 %tail_shared.1 = (bf16[4,4,3,24,768]{4,3,2,1,0:T(8,128)(2,1)}, bf16[4,4,3,24,768]{4,3,2,1,0:T(8,128)(2,1)}, f32[3,1,768]{2,1,0:T(1,128)}, f32[80,768]{1,0:T(8,128)}, f32[2,768]{1,0:T(2,128)}) custom-call(s32[3]{0:T(128)} %pad_add_fusion.me_ref.refs_0_, bf16[320,384]{1,0:T(8,128)(2,1)} %get-tuple-element.154.refs_0_.refs_1_, ...), custom_call_target="tpu_custom_call" | custom-call | flops 3586129920 | bytes 16777216 | tf_op jit(solution)/shard_map/tail_shared/pallas_call | solution.py:694
  186.1 4.6 %all-to-all-start.3 = ((bf16[4,80,768]{2,1,0:T(8,128)(2,1)}), bf16[4,80,768]{2,1,0:T(8,128)(2,1)S(1)}, u32[]{:S(2)}, u32[]{:S(2)}) async-start(bf16[4,80,768]{2,1,0:T(8,128)(2,1)} %get-tuple-element.148), calls=%async_computation.3 | async-start | bytes 983040 | tf_op jit(solution)/shard_map/all_to_all | solution.py:932
  190.7 10.0 %collective-permute-done.9.gx = bf16[2,160,768]{2,1,0:T(8,128)(2,1)S(1)} collective-permute-done((bf16[2,160,768]{2,1,0:T(8,128)(2,1)}, bf16[2,160,768]{2,1,0:T(8,128)(2,1)S(1)}, u32[]{:S(2)}, u32[]{:S(2)}) %collective-permute-start.9) | collective-permute-done | bytes 491552 | tf_op jit(solution)/shard_map/ppermute | solution.py:846
  200.7 2.8 collective-permute-done.10.gy
  205.6 2.4 collective-permute-start.11
  209.4 3.0 %collective-permute-done.11.rd = bf16[160,768]{1,0:T(8,128)(2,1)S(1)} collective-permute-done((bf16[160,768]{1,0:T(8,128)(2,1)}, bf16[160,768]{1,0:T(8,128)(2,1)S(1)}, u32[]{:S(2)}, u32[]{:S(2)}) %collective-permute-start.11) | collective-permute-done | bytes 245792 | tf_op jit(solution)/shard_map/ppermute | solution.py:846
  215.1 4.3 %tail.1 = (bf16[4,80,768]{2,1,0:T(8,128)(2,1)}, f32[2,768]{1,0:T(2,128)}) custom-call(s32[3]{0:T(128)} %pad_add_fusion.me_ref.refs_0_, f32[320,768]{1,0:T(8,128)} %get-tuple-element.147.own, bf16[2,160,768]{2,1,0:T(8,128)(2,1)} %copy-done.4, bf16[2,160,768]{2,1,0:T(8,128)(2,1)} %collective-permute-done.10.gy, bf16[160,768]{1,0:T(8,128)(2,1)} %copy-done.14, ...), custom_call_target="tpu_custom_call" | custom-call | flops 7372800 | bytes 6291456 | tf_op jit(solution)/shard_map/tail/pallas_call | solution.py:757
  220.9 3.6 %pair_sum.1 = (bf16[2,2,96,768]{3,2,1,0:T(8,128)(2,1)}, bf16[2,96,768]{2,1,0:T(8,128)(2,1)}, bf16[2,96,768]{2,1,0:T(8,128)(2,1)}, bf16[2,2,96,768]{3,2,1,0:T(8,1...) custom-call(bf16[4,4,72,768]{3,2,1,0:T(8,128)(2,1)} %bitcast.28, bf16[4,4,72,768]{3,2,1,0:T(8,128)(2,1)} %bitcast.30, ...), custom_call_target="tpu_custom_call" | custom-call | flops 1048576 | bytes 8388608 | tf_op jit(solution)/shard_map/pair_sum/pallas_call | solution.py:814
  226.4 16.4 %all_to_all.39 = f32[32,1,288]{2,1,0:T(1,128)S(1)} all-to-all(f32[32,1,288]{2,1,0:T(1,128)S(1)} %copy.34), channel_id=1, replica_groups=mesh['freq'=4,'tm'=4,'grp'=2] {'freq','tm','grp'}, dimensions={0} | all-to-all | bytes 73728 | tf_op jit(solution)/shard_map/all_to_all | solution.py:932
  242.8 4.6 %all-to-all-start.5 = ((bf16[4,80,768]{2,1,0:T(8,128)(2,1)}), bf16[4,80,768]{2,1,0:T(8,128)(2,1)S(1)}, u32[]{:S(2)}, u32[]{:S(2)}) async-start(bf16[4,80,768]{2,1,0:T(8,128)(2,1)} %get-tuple-element.165), calls=%async_computation.5 | async-start | bytes 983040 | tf_op jit(solution)/shard_map/all_to_all | solution.py:932
  253.9 5.6 %collective-permute-done.17.refs_2_ = bf16[2,96,768]{2,1,0:T(8,128)(2,1)S(1)} collective-permute-done((bf16[2,96,768]{2,1,0:T(8,128)(2,1)}, bf16[2,96,768]{2,1,0:T(8,128)(2,1)S(1)}, u32[]{:S(2)}, u32[]{:S(2)}) %collective-permute-start.17) | collective-permute-done | bytes 294944 | tf_op jit(solution)/shard_map/ppermute | solution.py:846
  260.4 3.3 %tm_sum.1 = (bf16[96,768]{1,0:T(8,128)(2,1)}, bf16[96,768]{1,0:T(8,128)(2,1)}, bf16[96,768]{1,0:T(8,128)(2,1)}, bf16[96,768]{1,0:T(8,128)(2,1)}) custom-call(s32[3]{0:T(128)} %pad_add_fusion.me_ref.refs_0_, bf16[2,96,768]{2,1,0:T(8,128)(2,1)} %get-tuple-element.176.refs_0_, bf16[2,2,96,768]{3,2,1,0:T(8,128)(2,1)} %copy-done.2, ...), custom_call_target="tpu_custom_call" | custom-call | flops 1048576 | bytes 5242880 | tf_op jit(solution)/shard_map/tm_sum/pallas_call | solution.py:879
  265.5 2.4 collective-permute-start.20
  272.5 6.4 %collective-permute-done.20.refs_2_ = bf16[96,768]{1,0:T(8,128)(2,1)S(1)} collective-permute-done((bf16[96,768]{1,0:T(8,128)(2,1)}, bf16[96,768]{1,0:T(8,128)(2,1)S(1)}, u32[]{:S(2)}, u32[]{:S(2)}) %collective-permute-start.20) | collective-permute-done | bytes 147488 | tf_op jit(solution)/shard_map/ppermute | solution.py:922
  (158 shorter events, 53.9 us)
Async XLA Ops:
  10.7 16.1 %collective-permute-start = (bf16[80,768]{1,0:T(8,128)(2,1)}, bf16[80,768]{1,0:T(8,128)(2,1)S(1)}, u32[]{:S(2)}, u32[]{:S(2)}) collective-permute-start(bf16[80,768]{1,0:T(8,128)(2,1)} %get-tuple-element.104), channel_id=1, source_target_pairs={{0,8},{8,0},{16,24},{24,16},{1,9},{9,1},{17,25},{25,17},{2,10},{10... | collective-permute-start | bytes 368648 | tf_op jit(solution)/shard_map/ppermute | solution.py:922
  13.7 13.1 %collective-permute-start.1 = (bf16[80,768]{1,0:T(8,128)(2,1)}, bf16[80,768]{1,0:T(8,128)(2,1)S(1)}, u32[]{:S(2)}, u32[]{:S(2)}) collective-permute-start(bf16[80,768]{1,0:T(8,128)(2,1)} %get-tuple-element.105), channel_id=1, source_target_pairs={{0,16},{8,24},{16,0},{24,8},{1,17},{9,25},{17,1},{25,9},{2,18},{10... | collective-permute-start | bytes 368648 | tf_op jit(solution)/shard_map/ppermute | solution.py:922
  16.3 10.5 %collective-permute-start.2 = (bf16[80,768]{1,0:T(8,128)(2,1)}, bf16[80,768]{1,0:T(8,128)(2,1)S(1)}, u32[]{:S(2)}, u32[]{:S(2)}) collective-permute-start(bf16[80,768]{1,0:T(8,128)(2,1)} %get-tuple-element.106), channel_id=1, source_target_pairs={{0,24},{8,16},{16,8},{24,0},{1,25},{9,17},{17,9},{25,1},{2,26},{10... | collective-permute-start | bytes 368648 | tf_op jit(solution)/shard_map/ppermute | solution.py:922
  26.8 25.2 %copy-start.34 = (bf16[80,768]{1,0:T(8,128)(2,1)S(1)}, bf16[80,768]{1,0:T(8,128)(2,1)}, u32[]{:S(2)}) copy-start(bf16[80,768]{1,0:T(8,128)(2,1)} %get-tuple-element.119) | copy-start | bytes 368644
  29.8 21.0 %all-to-all-start = ((bf16[16,40,384]{2,1,0:T(8,128)(2,1)}), bf16[16,40,384]{2,1,0:T(8,128)(2,1)S(1)}, u32[]{:S(2)}, u32[]{:S(2)}) async-start(bf16[16,40,384]{2,1,0:T(8,128)(2,1)} %get-tuple-element.116), calls=%async_computation | async-start | bytes 983040 | tf_op jit(solution)/shard_map/all_to_all | solution.py:932
  39.3 21.6 %collective-permute-start.8 = (bf16[320,768]{1,0:T(8,128)(2,1)}, bf16[320,768]{1,0:T(8,128)(2,1)S(1)}, u32[]{:S(2)}, u32[]{:S(2)}) collective-permute-start(bf16[320,768]{1,0:T(8,128)(2,1)} %ln_one.1.refs_0_.refs_7_), channel_id=1, source_target_pairs={{0,6},{2,4},{4,2},{6,0},{1,7},{3,5},{5,3},{7,1},{8,14},{10,12},{12... | collective-permute-start | bytes 1474568 | tf_op jit(solution)/shard_map/ppermute | solution.py:922
  42.1 23.9 %collective-permute-start.7 = (bf16[320,768]{1,0:T(8,128)(2,1)}, bf16[320,768]{1,0:T(8,128)(2,1)S(1)}, u32[]{:S(2)}, u32[]{:S(2)}) collective-permute-start(bf16[320,768]{1,0:T(8,128)(2,1)} %ln_one.1.refs_0_.refs_7_), channel_id=1, source_target_pairs={{0,4},{2,6},{4,0},{6,2},{1,5},{3,7},{5,1},{7,3},{8,12},{10,14},{12... | collective-permute-start | bytes 1474568 | tf_op jit(solution)/shard_map/ppermute | solution.py:922
  42.7 23.7 %collective-permute-start.6 = (bf16[320,768]{1,0:T(8,128)(2,1)}, bf16[320,768]{1,0:T(8,128)(2,1)S(1)}, u32[]{:S(2)}, u32[]{:S(2)}) collective-permute-start(bf16[320,768]{1,0:T(8,128)(2,1)} %ln_one.1.refs_0_.refs_7_), channel_id=1, source_target_pairs={{0,2},{2,0},{4,6},{6,4},{1,3},{3,1},{5,7},{7,5},{8,10},{10,8},{12,... | collective-permute-start | bytes 1474568 | tf_op jit(solution)/shard_map/ppermute | solution.py:922
  50.9 40.7 %collective-permute-start.3 = (bf16[80,768]{1,0:T(8,128)(2,1)S(1)}, bf16[80,768]{1,0:T(8,128)(2,1)S(1)}, u32[]{:S(2)}, u32[]{:S(2)}) collective-permute-start(bf16[80,768]{1,0:T(8,128)(2,1)S(1)} %copy-done.35), channel_id=1, source_target_pairs={{0,8},{8,0},{16,24},{24,16},{1,9},{9,1},{17,25},{25,17},{2,10},{10... | collective-permute-start | bytes 368648 | tf_op jit(solution)/shard_map/ppermute | solution.py:922
  52.0 39.6 %collective-permute-start.4 = (bf16[80,768]{1,0:T(8,128)(2,1)S(1)}, bf16[80,768]{1,0:T(8,128)(2,1)S(1)}, u32[]{:S(2)}, u32[]{:S(2)}) collective-permute-start(bf16[80,768]{1,0:T(8,128)(2,1)S(1)} %copy-done.34), channel_id=1, source_target_pairs={{0,16},{8,24},{16,0},{24,8},{1,17},{9,25},{17,1},{25,9},{2,18},{10... | collective-permute-start | bytes 368648 | tf_op jit(solution)/shard_map/ppermute | solution.py:922
  61.0 30.6 %collective-permute-start.5 = (bf16[80,768]{1,0:T(8,128)(2,1)S(1)}, bf16[80,768]{1,0:T(8,128)(2,1)S(1)}, u32[]{:S(2)}, u32[]{:S(2)}) collective-permute-start(bf16[80,768]{1,0:T(8,128)(2,1)S(1)} %copy-done.33), channel_id=1, source_target_pairs={{0,24},{8,16},{16,8},{24,0},{1,25},{9,17},{17,9},{25,1},{2,26},{10... | collective-permute-start | bytes 368648 | tf_op jit(solution)/shard_map/ppermute | solution.py:922
  66.4 25.2 %all-to-all-start.1 = ((bf16[16,40,128]{2,1,0:T(8,128)(2,1)}), bf16[16,40,128]{2,1,0:T(8,128)(2,1)S(1)}, u32[]{:S(2)}, u32[]{:S(2)}) async-start(bf16[16,40,128]{2,1,0:T(8,128)(2,1)} %bitcast.39), calls=%async_computation.1 | async-start | bytes 327680 | tf_op jit(solution)/shard_map/all_to_all | solution.py:932
  71.8 209.6 %reduce-scatter.2.cloned.1.call-start = ((), (), s32[]{:S(2)}) async-start(), calls=%async_computation.8 | async-start | bytes 9732096 | tf_op jit(solution)/shard_map/reduce_scatter | solution.py:983
  115.3 16.0 %all-to-all-start.2 = ((bf16[16,40,128]{2,1,0:T(8,128)(2,1)}), bf16[16,40,128]{2,1,0:T(8,128)(2,1)S(1)}, u32[]{:S(2)}, u32[]{:S(2)}) async-start(bf16[16,40,128]{2,1,0:T(8,128)(2,1)} %get-tuple-element.136), calls=%async_computation.2 | async-start | bytes 327680 | tf_op jit(solution)/shard_map/all_to_all | solution.py:932
  140.7 26.1 %all-to-all-start.4 = ((bf16[16,40,384]{2,1,0:T(8,128)(2,1)}), bf16[16,40,384]{2,1,0:T(8,128)(2,1)S(1)}, u32[]{:S(2)}, u32[]{:S(2)}) async-start(bf16[16,40,384]{2,1,0:T(8,128)(2,1)} %bitcast.35), calls=%async_computation.4 | async-start | bytes 983040 | tf_op jit(solution)/shard_map/all_to_all | solution.py:932
  182.6 25.9 %copy-start.22 = (f32[1,3072]{1,0:T(1,128)S(1)}, f32[1,3072]{1,0:T(1,128)}, u32[]{:S(2)}) copy-start(f32[1,3072]{1,0:T(1,128)} %get-tuple-element.170) | copy-start | bytes 36868
  182.6 26.7 %copy-start.21 = (f32[4,768]{1,0:T(4,128)S(1)}, f32[4,768]{1,0:T(4,128)}, u32[]{:S(2)}) copy-start(f32[4,768]{1,0:T(4,128)} %get-tuple-element.169) | copy-start | bytes 36868
  182.6 36.8 %collective-permute-start.13 = (bf16[4,4,3,24,768]{4,3,2,1,0:T(8,128)(2,1)}, bf16[4,4,3,24,768]{4,3,2,1,0:T(8,128)(2,1)S(1)}, u32[]{:S(2)}, u32[]{:S(2)}) collective-permute-start(bf16[4,4,3,24,768]{4,3,2,1,0:T(8,128)(2,1)} %get-tuple-element.172), channel_id=1, source_target_pairs={{0,1},{1,0},{2,3},{3,2},{4,5},{5,4},{6,7},{7,6},{8,9},{9,8},{10,11... | collective-permute-start | bytes 5308424 | tf_op jit(solution)/shard_map/ppermute | solution.py:917
  182.7 18.0 %collective-permute-start.9 = (bf16[2,160,768]{2,1,0:T(8,128)(2,1)}, bf16[2,160,768]{2,1,0:T(8,128)(2,1)S(1)}, u32[]{:S(2)}, u32[]{:S(2)}) collective-permute-start(bf16[2,160,768]{2,1,0:T(8,128)(2,1)} %get-tuple-element.150), channel_id=1, source_target_pairs={{0,2},{2,0},{4,6},{6,4},{1,3},{3,1},{5,7},{7,5},{8,10},{10,8},{12,... | collective-permute-start | bytes 1474568 | tf_op jit(solution)/shard_map/ppermute | solution.py:846
  184.6 18.9 %collective-permute-start.10 = (bf16[2,160,768]{2,1,0:T(8,128)(2,1)}, bf16[2,160,768]{2,1,0:T(8,128)(2,1)}, u32[]{:S(2)}, u32[]{:S(2)}) collective-permute-start(bf16[2,160,768]{2,1,0:T(8,128)(2,1)} %get-tuple-element.151), channel_id=1, source_target_pairs={{0,4},{2,6},{4,0},{6,2},{1,5},{3,7},{5,1},{7,3},{8,12},{10,14},{12... | collective-permute-start | bytes 1474568 | tf_op jit(solution)/shard_map/ppermute | solution.py:846
  186.1 33.4 %collective-permute-start.14 = (bf16[4,4,24,768]{3,2,1,0:T(8,128)(2,1)}, bf16[4,4,24,768]{3,2,1,0:T(8,128)(2,1)S(1)}, u32[]{:S(2)}, u32[]{:S(2)}) collective-permute-start(bf16[4,4,24,768]{3,2,1,0:T(8,128)(2,1)} %get-tuple-element.175), channel_id=1, source_target_pairs={{0,1},{1,0},{2,3},{3,2},{4,5},{5,4},{6,7},{7,6},{8,9},{9,8},{10,11... | collective-permute-start | bytes 1769480 | tf_op jit(solution)/shard_map/ppermute | solution.py:917
  186.1 40.3 %all-to-all-start.3 = ((bf16[4,80,768]{2,1,0:T(8,128)(2,1)}), bf16[4,80,768]{2,1,0:T(8,128)(2,1)S(1)}, u32[]{:S(2)}, u32[]{:S(2)}) async-start(bf16[4,80,768]{2,1,0:T(8,128)(2,1)} %get-tuple-element.148), calls=%async_computation.3 | async-start | bytes 983040 | tf_op jit(solution)/shard_map/all_to_all | solution.py:932
  205.6 6.8 %collective-permute-start.11 = (bf16[160,768]{1,0:T(8,128)(2,1)}, bf16[160,768]{1,0:T(8,128)(2,1)S(1)}, u32[]{:S(2)}, u32[]{:S(2)}) collective-permute-start(bf16[160,768]{1,0:T(8,128)(2,1)} %get-tuple-element.163), channel_id=1, source_target_pairs={{0,4},{2,6},{4,0},{6,2},{1,5},{3,7},{5,1},{7,3},{8,12},{10,14},{12... | collective-permute-start | bytes 737288 | tf_op jit(solution)/shard_map/ppermute | solution.py:846
  208.0 6.4 %collective-permute-start.12 = (bf16[160,768]{1,0:T(8,128)(2,1)}, bf16[160,768]{1,0:T(8,128)(2,1)S(1)}, u32[]{:S(2)}, u32[]{:S(2)}) collective-permute-start(bf16[160,768]{1,0:T(8,128)(2,1)} %get-tuple-element.164), channel_id=1, source_target_pairs={{0,2},{2,0},{4,6},{6,4},{1,3},{3,1},{5,7},{7,5},{8,10},{10,8},{12,... | collective-permute-start | bytes 737288 | tf_op jit(solution)/shard_map/ppermute | solution.py:846
  224.5 22.9 %collective-permute-start.15 = (bf16[2,2,96,768]{3,2,1,0:T(8,128)(2,1)}, bf16[2,2,96,768]{3,2,1,0:T(8,128)(2,1)S(1)}, u32[]{:S(2)}, u32[]{:S(2)}) collective-permute-start(bf16[2,2,96,768]{3,2,1,0:T(8,128)(2,1)} %get-tuple-element.177), channel_id=1, source_target_pairs={{0,2},{2,0},{4,6},{6,4},{1,3},{3,1},{5,7},{7,5},{8,10},{10,8},{12,... | collective-permute-start | bytes 1769480 | tf_op jit(solution)/shard_map/ppermute | solution.py:846
  224.6 22.7 %collective-permute-start.16 = (bf16[2,2,96,768]{3,2,1,0:T(8,128)(2,1)}, bf16[2,2,96,768]{3,2,1,0:T(8,128)(2,1)S(1)}, u32[]{:S(2)}, u32[]{:S(2)}) collective-permute-start(bf16[2,2,96,768]{3,2,1,0:T(8,128)(2,1)} %get-tuple-element.180), channel_id=1, source_target_pairs={{0,4},{2,6},{4,0},{6,2},{1,5},{3,7},{5,1},{7,3},{8,12},{10,14},{12... | collective-permute-start | bytes 1769480 | tf_op jit(solution)/shard_map/ppermute | solution.py:846
  242.8 26.6 %all-to-all-start.5 = ((bf16[4,80,768]{2,1,0:T(8,128)(2,1)}), bf16[4,80,768]{2,1,0:T(8,128)(2,1)S(1)}, u32[]{:S(2)}, u32[]{:S(2)}) async-start(bf16[4,80,768]{2,1,0:T(8,128)(2,1)} %get-tuple-element.165), calls=%async_computation.5 | async-start | bytes 983040 | tf_op jit(solution)/shard_map/all_to_all | solution.py:932
  250.5 9.0 %collective-permute-start.17 = (bf16[2,96,768]{2,1,0:T(8,128)(2,1)}, bf16[2,96,768]{2,1,0:T(8,128)(2,1)S(1)}, u32[]{:S(2)}, u32[]{:S(2)}) collective-permute-start(bf16[2,96,768]{2,1,0:T(8,128)(2,1)} %get-tuple-element.181), channel_id=1, source_target_pairs={{0,4},{2,6},{4,0},{6,2},{1,5},{3,7},{5,1},{7,3},{8,12},{10,14},{12... | collective-permute-start | bytes 884744 | tf_op jit(solution)/shard_map/ppermute | solution.py:846
  251.1 8.6 %collective-permute-start.18 = (bf16[2,96,768]{2,1,0:T(8,128)(2,1)}, bf16[2,96,768]{2,1,0:T(8,128)(2,1)S(1)}, u32[]{:S(2)}, u32[]{:S(2)}) collective-permute-start(bf16[2,96,768]{2,1,0:T(8,128)(2,1)} %get-tuple-element.183), channel_id=1, source_target_pairs={{0,2},{2,0},{4,6},{6,4},{1,3},{3,1},{5,7},{7,5},{8,10},{10,8},{12,... | collective-permute-start | bytes 884744 | tf_op jit(solution)/shard_map/ppermute | solution.py:846
  263.8 8.7 %collective-permute-start.19 = (bf16[96,768]{1,0:T(8,128)(2,1)}, bf16[96,768]{1,0:T(8,128)(2,1)S(1)}, u32[]{:S(2)}, u32[]{:S(2)}) collective-permute-start(bf16[96,768]{1,0:T(8,128)(2,1)} %get-tuple-element.185), channel_id=1, source_target_pairs={{0,8},{8,0},{16,24},{24,16},{1,9},{9,1},{17,25},{25,17},{2,10},{10... | collective-permute-start | bytes 442376 | tf_op jit(solution)/shard_map/ppermute | solution.py:922
  265.5 13.3 %collective-permute-start.20 = (bf16[96,768]{1,0:T(8,128)(2,1)}, bf16[96,768]{1,0:T(8,128)(2,1)S(1)}, u32[]{:S(2)}, u32[]{:S(2)}) collective-permute-start(bf16[96,768]{1,0:T(8,128)(2,1)} %get-tuple-element.186), channel_id=1, source_target_pairs={{0,16},{8,24},{16,0},{24,8},{1,17},{9,25},{17,1},{25,9},{2,18},{10... | collective-permute-start | bytes 442376 | tf_op jit(solution)/shard_map/ppermute | solution.py:922
  267.9 10.9 %collective-permute-start.21 = (bf16[96,768]{1,0:T(8,128)(2,1)}, bf16[96,768]{1,0:T(8,128)(2,1)S(1)}, u32[]{:S(2)}, u32[]{:S(2)}) collective-permute-start(bf16[96,768]{1,0:T(8,128)(2,1)} %get-tuple-element.187), channel_id=1, source_target_pairs={{0,24},{8,16},{16,8},{24,0},{1,25},{9,17},{17,9},{25,1},{2,26},{10... | collective-permute-start | bytes 442376 | tf_op jit(solution)/shard_map/ppermute | solution.py:922
  (36 other events, 158.1 us)
Sparse Core Ops, SparseCore 0:
  115.4 152.1 reduce-scatter.1

commit v3 on v2

v3 whole, which is shorter than its diff:
```python
import functools

import jax
import jax.numpy as jnp
from jax import lax
from jax.experimental import pallas as pl
from jax.experimental.pallas import tpu as pltpu
from jax.sharding import PartitionSpec as P

HD = 64
NORM_EPS = 1e-06
BF = jnp.bfloat16
F32 = jnp.float32
ALL = ("freq", "tm", "grp")
VMEM_LIMIT = 60 * 1024 * 1024
GAIN1, SHIFT1, BIAS_Q, BIAS_V, BIAS_OUT, GAIN2, SHIFT2, BIAS_DOWN, BIAS_UP = range(9)


def row_of(ref, i):
    return ref[i : i + 1, :]


def nn(a, b):
    return lax.dot_general(a, b, (((1,), (0,)), ((), ())), preferred_element_type=F32)


def nt_dot(a, b):
    return lax.dot_general(a, b, (((1,), (1,)), ((), ())), preferred_element_type=F32)


def tn_dot(a, b):
    return lax.dot_general(a, b, (((0,), (0,)), ((), ())), preferred_element_type=F32)


def normalize(x):
    mean = jnp.mean(x, axis=-1, keepdims=True)
    centered = x - mean
    var = jnp.mean(centered * centered, axis=-1, keepdims=True)
    rstd = lax.rsqrt(var + NORM_EPS)
    return centered * rstd, rstd


def norm_back(e, n, rstd, gain):
    eg = e * gain
    return rstd * (
        eg - jnp.mean(eg, axis=-1, keepdims=True) - n * jnp.mean(eg * n, axis=-1, keepdims=True)
    )


def colsum(x):
    return jnp.sum(x, axis=0, keepdims=True)


def low_lanes(rows):
    return lax.broadcasted_iota(jnp.int32, (rows, 2 * HD), 1) < HD


def swap_halves(x):
    return pltpu.roll(x, HD, 1)


def slot_of(head, nf, nt):
    per = -(-(12) // nf)
    return (head // per) * nt + head % per


def params(count=1):
    return pltpu.CompilerParams(
        dimension_semantics=("arbitrary",) * count, vmem_limit_bytes=VMEM_LIMIT
    )


def full(shape):
    return pl.BlockSpec(shape, lambda *_: (0,) * len(shape))


def clip_at(x, i):
    return pl.BlockSpec((None,) + x.shape[1:], lambda *_: (i, 0, 0))


def cost(flops, nbytes, weight=1):
    return pl.CostEstimate(
        flops=int(weight * flops), bytes_accessed=int(weight * nbytes), transcendentals=0
    )


def pick_kernel(nf, count, me_ref, x_ref, *refs):
    vecs, outs = refs[:count], refs[count:]
    for k in range(nf):
        outs[k][...] = x_ref[me_ref[0] ^ k]
    if count:
        width = x_ref.shape[2]
        for i in range(count - 1):
            outs[nf][i : i + 1, :] = vecs[i][...].reshape(1, width)
        last = vecs[count - 1]
        for i in range(last.shape[0] // width):
            at = count - 1 + i
            outs[nf][at : at + 1, :] = last[i * width : (i + 1) * width].reshape(1, width)


def pick_call(nf, me, x, vecs=()):
    _, rows, width = x.shape
    count = 8 + -(-sum(v.shape[0] for v in vecs) // width) // 8 * 8
    more = [(count, width)] if vecs else []
    return pl.pallas_call(
        functools.partial(pick_kernel, nf, len(vecs)),
        grid_spec=pltpu.PrefetchScalarGridSpec(
            num_scalar_prefetch=1,
            grid=(1,),
            in_specs=[full(x.shape)] + [full(v.shape) for v in vecs],
            out_specs=[full((rows, width))] * nf + [full(y) for y in more],
        ),
        out_shape=[jax.ShapeDtypeStruct((rows, width), BF)] * nf
        + [jax.ShapeDtypeStruct(y, F32) for y in more],
        compiler_params=params(),
        cost_estimate=cost(0, 4 * x.size),
        name="pick",
    )(me, x, *vecs)


def assemble_kernel(nf, me_ref, *refs):
    for k in range(nf):
        refs[-1][me_ref[0] ^ k] = refs[k][...].astype(F32)
    refs[-1][nf] = refs[nf][...]


def assemble_call(nf, me, parts, five):
    rows, width = five.shape
    return pl.pallas_call(
        functools.partial(assemble_kernel, nf),
        grid_spec=pltpu.PrefetchScalarGridSpec(
            num_scalar_prefetch=1,
            grid=(1,),
            in_specs=[full((rows, width))] * (nf + 1),
            out_specs=full((nf + 1, rows, width)),
        ),
        out_shape=jax.ShapeDtypeStruct((nf + 1, rows, width), F32),
        compiler_params=params(),
        cost_estimate=cost(0, 8 * (nf + 1) * five.size),
        name="assemble",
    )(me, *parts, five)


def ln_kernel(nf, *refs):
    vec_ref, n_ref = refs[nf:]
    for k in range(nf):
        rows = refs[k].shape[0]
        n, _ = normalize(refs[k][...].astype(F32))
        n = n * row_of(vec_ref, GAIN1) + row_of(vec_ref, SHIFT1)
        n_ref[k * rows : (k + 1) * rows, :] = n.astype(BF)


def ln_call(xs, vecs):
    rows, width = xs[0].shape
    return pl.pallas_call(
        functools.partial(ln_kernel, len(xs)),
        grid=(1,),
        in_specs=[full((rows, width))] * len(xs) + [full(vecs.shape)],
        out_specs=full((len(xs) * rows, width)),
        out_shape=jax.ShapeDtypeStruct((len(xs) * rows, width), BF),
        compiler_params=pltpu.CompilerParams(vmem_limit_bytes=VMEM_LIMIT),
        cost_estimate=cost(len(xs) * rows * width * 10, len(xs) * rows * width * 4, 100),
        name="ln_one",
    )(*xs, vecs)


def q5_kernel(nf, nt, x_ref, vec_ref, w_ref, n_ref, pack_ref):
    rows, width = x_ref.shape
    half = rows // 2
    hat, _ = normalize(x_ref[...].astype(F32))
    n = (hat * row_of(vec_ref, GAIN1) + row_of(vec_ref, SHIFT1)).astype(BF)
    n_ref[...] = n
    low = low_lanes(half)
    pack_ref[...] = jnp.zeros_like(pack_ref)
    for part in range(3):
        proj = nn(n, w_ref[:, part * width : (part + 1) * width])
        if part == 0:
            proj = (proj + row_of(vec_ref, BIAS_Q)) * (HD**-0.5)
        if part == 2:
            proj = proj + row_of(vec_ref, BIAS_V)
        for pair in range(width // (2 * HD)):
            blk = proj[:, pair * 2 * HD : (pair + 1) * 2 * HD]
            top, bot = blk[:half], blk[half:]
            even = jnp.where(low, top, swap_halves(bot))
            odd = jnp.where(low, swap_halves(top), bot)
            lanes = slice(part * 2 * HD, (part + 1) * 2 * HD)
            pack_ref[slot_of(2 * pair, nf, nt), :, lanes] = even.astype(BF)
            pack_ref[slot_of(2 * pair + 1, nf, nt), :, lanes] = odd.astype(BF)


def q5_call(nf, nt, x, vecs, w):
    _, rows, width = x.shape
    return pl.pallas_call(
        functools.partial(q5_kernel, nf, nt),
        grid=(1,),
        in_specs=[clip_at(x, nf), full(vecs.shape), full(w.shape)],
        out_specs=[full((rows, width)), full((nf * nt, rows // 2, 6 * HD))],
        out_shape=(
            jax.ShapeDtypeStruct((rows, width), BF),
            jax.ShapeDtypeStruct((nf * nt, rows // 2, 6 * HD), BF),
        ),
        compiler_params=pltpu.CompilerParams(vmem_limit_bytes=VMEM_LIMIT),
        cost_estimate=cost(2 * rows * w.size, w.size * 2),
        name="q_shared",
    )(x, vecs, w)


def spread(x):
    rows = x.shape[0]
    low = low_lanes(rows)
    zero = jnp.zeros_like(x)
    return jnp.concatenate([jnp.where(low, x, zero), jnp.where(low, swap_halves(x), zero)], axis=0)


def unspread(x):
    half = x.shape[0] // 2
    return x[:half] + swap_halves(x[half:])


def stack_heads(x):
    low = low_lanes(x.shape[0])
    zero = jnp.zeros_like(x)
    return jnp.concatenate([jnp.where(low, x, zero), jnp.where(low, zero, x)], axis=0)


def softmax_block(q, k, v):
    s = nt_dot(q, k)
    m = jnp.max(s, axis=-1, keepdims=True)
    e = jnp.exp(s - m)
    total = jnp.sum(e, axis=-1, keepdims=True)
    e = e.astype(BF)
    rinv = 1.0 / total
    return e, nn(e, v) * rinv, rinv


def attn5_fwd_kernel(x_ref, o_ref, r_ref, ob_ref, e_ref, qf, kf, vf, of, rf):
    step = pl.program_id(0)

    @pl.when(step == 0)
    def _():
        for part, dst in enumerate((qf, kf, vf)):
            blk = x_ref[:, part * 2 * HD : (part + 1) * 2 * HD].astype(F32)
            dst[...] = spread(blk).astype(BF)

    rows = e_ref.shape[0]
    at = pl.ds(pl.multiple_of(step * rows, rows), rows)
    e, o, rinv = softmax_block(qf[at, :], kf[...], vf[...])
    e_ref[...] = e
    of[at, :] = o
    rf[at, :] = jnp.where(low_lanes(rows), jnp.broadcast_to(rinv, (rows, 2 * HD)), 0.0)

    @pl.when(step == pl.num_programs(0) - 1)
    def _():
        packed = unspread(of[...])
        o_ref[...] = packed
        ob_ref[...] = packed.astype(BF)
        r_ref[...] = unspread(rf[...])


def attn5_fwd_call(x):
    rows = x.shape[0]
    toks = 2 * rows
    shape = jax.ShapeDtypeStruct
    return pl.pallas_call(
        attn5_fwd_kernel,
        grid=(4,),
        in_specs=[full(x.shape)],
        out_specs=[full((rows, 2 * HD))] * 3 + [pl.BlockSpec((toks // 4, toks), lambda j: (j, 0))],
        out_shape=(
            shape((rows, 2 * HD), F32),
            shape((rows, 2 * HD), F32),
            shape((rows, 2 * HD), BF),
            shape((toks, toks), BF),
        ),
        scratch_shapes=[pltpu.VMEM((toks, 2 * HD), BF)] * 3 + [pltpu.VMEM((toks, 2 * HD), F32)] * 2,
        compiler_params=params(),
        cost_estimate=cost(4 * 4 * toks * toks * 2 * HD, toks * toks * 2),
        name="attn_shared_fwd",
    )(x)


def attn5_bwd_kernel(x_ref, ga_ref, o_ref, r_ref, e_ref, out_ref, qf, kf, vf, gf, inn, dq, dk, dv):
    step = pl.program_id(0)

    @pl.when(step == 0)
    def _():
        for part, dst in enumerate((qf, kf, vf)):
            blk = x_ref[:, part * 2 * HD : (part + 1) * 2 * HD].astype(F32)
            dst[...] = spread(blk).astype(BF)
        g = ga_ref[...].astype(F32) * r_ref[...]
        gs = spread(g)
        gf[...] = gs.astype(BF)
        inn[...] = jnp.sum(gs * spread(o_ref[...]), axis=-1, keepdims=True)
        dk[...] = jnp.zeros_like(dk)
        dv[...] = jnp.zeros_like(dv)

    rows = e_ref.shape[0]
    at = pl.ds(pl.multiple_of(step * rows, rows), rows)
    e = e_ref[...]
    gb = gf[at, :]
    dp = nt_dot(gb, vf[...])
    ds = (e.astype(F32) * (dp - inn[at, :])).astype(BF)
    dq[at, :] = nn(ds, kf[...]) * (HD**-0.5)
    dk[...] += tn_dot(ds, qf[at, :])
    dv[...] += tn_dot(e, gb)

    @pl.when(step == pl.num_programs(0) - 1)
    def _():
        for part, src in enumerate((dq, dk, dv)):
            out_ref[:, part * 2 * HD : (part + 1) * 2 * HD] = unspread(src[...]).astype(BF)


def attn5_bwd_call(x, ga, o, r, e):
    rows = x.shape[0]
    toks = 2 * rows
    return pl.pallas_call(
        attn5_bwd_kernel,
        grid=(4,),
        in_specs=[full(y.shape) for y in (x, ga, o, r)]
        + [pl.BlockSpec((toks // 4, toks), lambda j: (j, 0))],
        out_specs=full((rows, 6 * HD)),
        out_shape=jax.ShapeDtypeStruct((rows, 6 * HD), BF),
        scratch_shapes=[pltpu.VMEM((toks, 2 * HD), BF)] * 4
        + [pltpu.VMEM((toks, 1), F32)]
        + [pltpu.VMEM((toks, 2 * HD), F32)] * 3,
        compiler_params=params(),
        cost_estimate=cost(8 * 4 * toks * toks * 2 * HD, toks * toks * 2),
        name="attn_shared_bwd",
    )(x, ga, o, r, e)


def kv_kernel(count, first_v, *refs):
    xs, (w_ref, vec_ref, kv_ref) = refs[:count], refs[count:]
    rows = xs[0].shape[0]
    shift = jnp.where(pl.program_id(0) >= first_v, row_of(vec_ref, BIAS_V), 0.0)
    for c in range(count):
        part = nn(xs[c][...], w_ref[...]) + shift
        kv_ref[c * rows : (c + 1) * rows, :] = part.astype(BF)


def kv_call(xs, w, vecs, weight):
    rows, width = xs[0].shape
    blk = width // 2
    steps = width // blk
    return pl.pallas_call(
        functools.partial(kv_kernel, len(xs), steps),
        grid=(2 * steps,),
        in_specs=[full((rows, width))] * len(xs)
        + [
            pl.BlockSpec((width, blk), lambda j: (0, steps + j)),
            pl.BlockSpec((8, blk), lambda j: (0, j % steps)),
        ],
        out_specs=pl.BlockSpec((len(xs) * rows, blk), lambda j: (0, j)),
        out_shape=jax.ShapeDtypeStruct((len(xs) * rows, 2 * width), BF),
        compiler_params=params(),
        cost_estimate=cost(4 * len(xs) * rows * width * width, 6 << 20, weight),
        name="kv",
    )(*xs, w, vecs)


def attn_fwd_kernel(x_ref, wq_ref, vec_ref, k0, k1, v0, v1, att_ref, o_ref, r_ref, q_ref, e_ref, kc, vc):
    rows = x_ref.shape[0]
    kc[0:rows, :] = k0[...]
    kc[rows:, :] = k1[...]
    vc[0:rows, :] = v0[...]
    vc[rows:, :] = v1[...]
    q = ((nn(x_ref[...], wq_ref[...]) + row_of(vec_ref, BIAS_Q)) * (HD**-0.5)).astype(BF)
    q_ref[...] = q
    low = low_lanes(rows)
    zero = jnp.zeros_like(q)
    k, v = kc[...], vc[...]
    e0, o0, r0 = softmax_block(jnp.where(low, q, zero), k, v)
    e_ref[0] = e0
    e1, o1, r1 = softmax_block(jnp.where(low, zero, q), k, v)
    e_ref[1] = e1
    o = jnp.where(low, o0, o1)
    o_ref[...] = o
    att_ref[...] = o.astype(BF)
    r_ref[...] = jnp.where(
        low, jnp.broadcast_to(r0, (rows, 2 * HD)), jnp.broadcast_to(r1, (rows, 2 * HD))
    )


def kv_specs(kv0, kv1, pairs):
    one = lambda x, at: pl.BlockSpec((x.shape[0], 2 * HD), lambda j, at=at: (0, j + at))
    return [one(kv0, 0), one(kv1, 0), one(kv0, pairs), one(kv1, pairs)]


def attn_fwd_call(x, w, vecs, kv0, kv1):
    rows, width = x.shape
    toks = rows + kv1.shape[0]
    blk = 2 * HD
    pairs = width // blk
    row = pl.BlockSpec((rows, blk), lambda j: (0, j))
    shape = jax.ShapeDtypeStruct
    return pl.pallas_call(
        attn_fwd_kernel,
        grid=(pairs,),
        in_specs=[full(x.shape), pl.BlockSpec((width, blk), lambda j: (0, j))]
        + [pl.BlockSpec((8, blk), lambda j: (0, j))]
        + kv_specs(kv0, kv1, pairs),
        out_specs=[row] * 4 + [pl.BlockSpec((2, rows, toks), lambda j: (j, 0, 0))],
        out_shape=(
            shape((rows, width), BF),
            shape((rows, width), F32),
            shape((rows, width), F32),
            shape((rows, width), BF),
            shape((width // HD, rows, toks), BF),
        ),
        scratch_shapes=[pltpu.VMEM((toks, blk), BF)] * 2,
        compiler_params=params(),
        cost_estimate=cost(16 * rows * toks * width, 20 << 20, 0.01),
        name="attn_fwd",
    )(x, w, vecs, kv0, kv1, kv0, kv1)


def attn_bwd_kernel(ga_ref, q_ref, k0, k1, v0, v1, o_ref, r_ref, e_ref, gq_ref, gkv_ref, kc, vc):
    rows = q_ref.shape[0]
    kc[0:rows, :] = k0[...]
    kc[rows:, :] = k1[...]
    vc[0:rows, :] = v0[...]
    vc[rows:, :] = v1[...]
    low = low_lanes(rows)
    stack = stack_heads
    g = ga_ref[...].astype(F32) * r_ref[...]
    inner = jnp.sum(stack(g * o_ref[...]), axis=-1, keepdims=True)
    gs, qs = stack(g.astype(BF)), stack(q_ref[...])
    e = e_ref[...].reshape(2 * rows, e_ref.shape[2])
    dp = nt_dot(gs, vc[...])
    ds = (e.astype(F32) * (dp - inner)).astype(BF)
    dq = nn(ds, kc[...])
    gq_ref[...] = (jnp.where(low, dq[:rows], dq[rows:]) * (HD**-0.5)).astype(BF)
    gkv_ref[0] = tn_dot(ds, qs).astype(BF)
    gkv_ref[1] = tn_dot(e, gs).astype(BF)


def attn_bwd_call(ga, q, kv0, kv1, o, r, e):
    rows, width = q.shape
    toks = e.shape[2]
    blk = 2 * HD
    steps = width // blk
    row = pl.BlockSpec((rows, blk), lambda j: (0, j))
    return pl.pallas_call(
        attn_bwd_kernel,
        grid=(steps,),
        in_specs=[row, row]
        + kv_specs(kv0, kv1, steps)
        + [row, row, pl.BlockSpec((2, rows, toks), lambda j: (j, 0, 0))],
        out_specs=[row, pl.BlockSpec((2, toks, blk), lambda j: (0, 0, j))],
        out_shape=[
            jax.ShapeDtypeStruct((rows, steps * blk), BF),
            jax.ShapeDtypeStruct((2, toks, steps * blk), BF),
        ],
        scratch_shapes=[pltpu.VMEM((toks, blk), BF)] * 2,
        compiler_params=params(),
        cost_estimate=cost(32 * rows * toks * blk * steps, steps * (4 << 20)),
        name="attn_bwd",
    )(ga, q, kv0, kv1, kv0, kv1, o, r, e)


def put_pieces(me_ref, src, keep_ref, send_ref, index):
    nt, nf = keep_ref.shape[0], keep_ref.shape[1]
    for k in range(nt):
        for f in range(nf):
            at = (f * nt + (me_ref[1] ^ k)) * 2
            keep_ref[(k, f) + index] = src[at + me_ref[2]]
            send_ref[(k, f) + index] = src[at + 1 - me_ref[2]]


def spread_over(n, vec, lanes):
    size = vec.shape[1]
    scale = -(-(1 << 21) // n)
    assert all((i * scale) >> 21 == i // n for i in range(size))
    dev = size // n
    col = lax.broadcasted_iota(jnp.int32, (dev, size), 1)
    mine = ((col * scale) >> 21) == lax.broadcasted_iota(jnp.int32, (dev, size), 0)
    left = jnp.where(mine, jnp.broadcast_to(vec, (dev, size)), 0.0).astype(BF)
    row = lax.broadcasted_iota(jnp.int32, (size, lanes), 0)
    place = row - ((row * scale) >> 21) * n
    hit = place == lax.broadcasted_iota(jnp.int32, (size, lanes), 1)
    return nn(left, jnp.where(hit, 1.0, 0.0).astype(BF))


def dx_kernel(gq_ref, gkv_ref, n0, n1, n2, n3, w_ref, own, *refs):
    *others, vec_ref, total, n_all = refs
    width = w_ref.shape[0]
    step = pl.program_id(0)
    e = nt_dot(gkv_ref[0], w_ref[:, width : 2 * width])
    total[...] = e + nt_dot(gkv_ref[1], w_ref[:, 2 * width :])

    @pl.when(step == 0)
    def _():
        total[...] += nt_dot(gq_ref[...], w_ref[:, 0:width])
        own[...] = total[...]
        vec_ref[...] = jnp.zeros_like(vec_ref)

    for c, n in enumerate((n0, n1, n2, n3)):

        @pl.when(step == c)
        def _():
            n_all[...] = n[...]

    vec_ref[0:1, :] += colsum(total[...] * n_all[...].astype(F32))
    vec_ref[1:2, :] += colsum(total[...])
    for c, out in enumerate(others):

        @pl.when(step == c + 1)
        def _():
            out[...] = total[...].astype(BF)


def dx_call(gq, gkv, ns, w):
    rows, width = gq.shape
    shape = jax.ShapeDtypeStruct
    return pl.pallas_call(
        dx_kernel,
        grid=(4,),
        in_specs=[full(gq.shape), pl.BlockSpec((2, rows, width), lambda j: (0, j, 0))]
        + [full((rows, width))] * 4
        + [full(w.shape)],
        out_specs=[full((rows, width))] * 4 + [full((2, width))],
        out_shape=[shape((rows, width), F32)]
        + [shape((rows, width), BF)] * 3
        + [shape((2, width), F32)],
        scratch_shapes=[pltpu.VMEM((rows, width), F32), pltpu.VMEM((rows, width), BF)],
        compiler_params=params(),
        cost_estimate=cost(16 * rows * width * width, 12 << 20),
        name="dx",
    )(gq, gkv, *ns, w)


def mid_kernel(nf, nt, fast, me_ref, *refs):
    refs = list(refs)
    if fast:
        *refs, down, up, side, sems = refs
    xms, cms, refs = refs[:nf], refs[nf : 2 * nf], refs[2 * nf :]
    att_ref, att5_ref, x5_ref, c5_ref, wo_ref, vec_in = refs[:6]
    wu_ref, wd_ref, outs_ref, out5_ref, gm_ref, ga_ref, ga5_ref = refs[6:13]
    *grads, vec_ref, gbu_ref, att, cot, mid, hat, rst, two, acc, gn2 = refs[13:]
    step = pl.program_id(0)
    r5, width = x5_ref.shape
    rm = nf * r5
    half = r5 // 2
    low = low_lanes(half)
    pairs = width // (2 * HD)

    @pl.when(step == 0)
    def _():
        att[0:rm, :] = att_ref[...]
        for pair in range(pairs):
            lanes = slice(pair * 2 * HD, (pair + 1) * 2 * HD)
            even = att5_ref[slot_of(2 * pair, nf, nt)].astype(F32)
            odd = att5_ref[slot_of(2 * pair + 1, nf, nt)].astype(F32)
            top = jnp.where(low, even, swap_halves(odd))
            bot = jnp.where(low, swap_halves(even), odd)
            att[rm : rm + r5, lanes] = jnp.concatenate([top, bot], axis=0).astype(BF)
        for k in range(nf):
            cot[k * r5 : (k + 1) * r5, :] = cms[k][...]
        cot[rm : rm + r5, :] = c5_ref[...]
        mid[...] = nn(att[...], wo_ref[...]) + row_of(vec_in, BIAS_OUT)
        for k in range(nf):
            mid[k * r5 : (k + 1) * r5, :] += xms[k][...].astype(F32)
        mid[rm : rm + r5, :] += x5_ref[...].astype(F32)
        n, rstd = normalize(mid[...])
        hat[...] = n
        rst[...] = rstd
        two[...] = (n * row_of(vec_in, GAIN2) + row_of(vec_in, SHIFT2)).astype(BF)
        acc[...] = mid[...] + row_of(vec_in, BIAS_DOWN)
        gn2[...] = jnp.zeros_like(gn2)

    pre = nn(two[...], wu_ref[...]) + vec_in[pl.ds(BIAS_UP + step, 1), :]
    cdf = 0.5 * (1.0 + lax.erf(pre * (0.5**0.5)))
    slope = cdf + pre * (jnp.exp(-0.5 * pre * pre) * 0.3989422804014327)
    act = (pre * cdf).astype(BF)
    acc[...] += nn(act, wd_ref[...])
    dwd = tn_dot(act, cot[...]).astype(BF)
    if fast:
        pd, pu = down.shape[2], up.shape[2]
        owners = down.shape[1]

        def copies(j):
            to_down = grads[0].at[:, j, pl.ds(0, pd), :]
            return [pltpu.make_async_copy(down.at[j], to_down, sems.at[0, j])] + [
                pltpu.make_async_copy(
                    up.at[j, pl.ds(f * owners, owners)],
                    grads[0].at[:, f, pl.ds(pd + j * pu, pu), :],
                    sems.at[1 + f, j],
                )
                for f in range(nf)
            ]

        down[step] = dwd.reshape(down.shape[1:])
    else:
        grads[0][...] = dwd
    gpre = (nt_dot(cot[...], wd_ref[...]) * slope).astype(BF)
    gbu_ref[...] = colsum(gpre.astype(F32))
    dwu = tn_dot(two[...], gpre)
    if fast:
        up[step] = dwu.reshape(up.shape[1:]).astype(BF)
        for copy in copies(step):
            copy.start()
    else:
        grads[1][...] = dwu.astype(BF)
    gn2[...] += nt_dot(gpre, wu_ref[...])

    @pl.when(step == pl.num_programs(0) - 1)
    def _():
        for k in range(nf):
            outs_ref[me_ref[0] ^ k] = acc[k * r5 : (k + 1) * r5, :].astype(BF)
        out5_ref[...] = acc[rm : rm + r5, :]
        e = gn2[...]
        n = hat[...]
        c = cot[...].astype(F32)
        gmid = c + norm_back(e, n, rst[...], row_of(vec_in, GAIN2))
        gm_ref[...] = gmid
        branch = gmid.astype(BF)
        vec_ref[0:1, :] = colsum(branch.astype(F32))
        vec_ref[1:2, :] = colsum(e * n)
        vec_ref[2:3, :] = colsum(e)
        vec_ref[3:4, :] = colsum(c)
        dwo = tn_dot(att[...], branch)
        if fast:
            side[...] = dwo.reshape(side.shape).astype(BF)
            put_pieces(me_ref, side, grads[1], grads[2], ())
        else:
            grads[2][...] = dwo.astype(BF)
        gatt = nt_dot(branch, wo_ref[...])
        ga_ref[...] = gatt[0:rm].astype(BF)
        ga5_ref[...] = jnp.zeros_like(ga5_ref)
        for pair in range(pairs):
            lanes = slice(pair * 2 * HD, (pair + 1) * 2 * HD)
            top, bot = gatt[rm : rm + half, lanes], gatt[rm + half : rm + r5, lanes]
            even = jnp.where(low, top, swap_halves(bot))
            odd = jnp.where(low, swap_halves(top), bot)
            ga5_ref[slot_of(2 * pair, nf, nt)] = even.astype(BF)
            ga5_ref[slot_of(2 * pair + 1, nf, nt)] = odd.astype(BF)
        if fast:
            for j in range(nf):
                for copy in copies(j):
                    copy.wait()


def mid_call(nf, nt, fast, me, xms, cms, att, att5, x5, c5, wo, vecs, wu, wd):
    _, r5, width = x5.shape
    rm = nf * r5
    rows = rm + r5
    ff = wu.shape[1]
    blk = ff // nf
    shape = jax.ShapeDtypeStruct
    if fast:
        dev = nf * nt * 2
        pd, pu = ff // dev, width // dev
        oshape = (nt, nf, pu, width)
        gspecs = [pl.BlockSpec(memory_space=pl.ANY)] + [full(oshape)] * 2
        gshapes = [shape((nt * 2, nf, pd + nf * pu, width), BF)] + [shape(oshape, BF)] * 2
        extra = [
            pltpu.VMEM((nf, nt * 2, pd, width), BF),
            pltpu.VMEM((nf, dev, pu, width), BF),
            pltpu.VMEM((dev, pu, width), BF),
            pltpu.SemaphoreType.DMA((1 + nf, nf)),
        ]
    else:
        gspecs = [
            pl.BlockSpec((blk, width), lambda j, *_: (j, 0)),
            pl.BlockSpec((width, blk), lambda j, *_: (0, j)),
            full((width, width)),
        ]
        gshapes = [shape((ff, width), BF), shape((width, ff), BF), shape((width, width), BF)]
        extra = []
    ins = [*xms, *cms, att, att5, x5, c5, wo, vecs]
    return pl.pallas_call(
        functools.partial(mid_kernel, nf, nt, fast),
        grid_spec=pltpu.PrefetchScalarGridSpec(
            num_scalar_prefetch=1,
            grid=(nf,),
            in_specs=[clip_at(x, nf) if x.ndim == 3 and x.shape[0] == nf + 1 else full(x.shape) for x in ins]
            + [
                pl.BlockSpec((width, blk), lambda j, *_: (0, j)),
                pl.BlockSpec((blk, width), lambda j, *_: (j, 0)),
            ],
            out_specs=[
                full((nf, r5, width)),
                full((r5, width)),
                full((rows, width)),
                full((rm, width)),
                full(att5.shape),
            ]
            + gspecs
            + [full((4, width)), pl.BlockSpec((1, blk), lambda j, *_: (0, j))],
            scratch_shapes=[
                pltpu.VMEM((rows, width), BF),
                pltpu.VMEM((rows, width), BF),
                pltpu.VMEM((rows, width), F32),
                pltpu.VMEM((rows, width), F32),
                pltpu.VMEM((rows, 1), F32),
                pltpu.VMEM((rows, width), BF),
                pltpu.VMEM((rows, width), F32),
                pltpu.VMEM((rows, width), F32),
            ]
            + extra,
        ),
        out_shape=[
            shape((nf, r5, width), BF),
            shape((r5, width), F32),
            shape((rows, width), F32),
            shape((rm, width), BF),
            shape(att5.shape, BF),
        ]
        + gshapes
        + [shape((4, width), F32), shape((1, ff), F32)],
        compiler_params=params(),
        cost_estimate=cost(12 * rows * width * ff + 6 * rows * width * width, 24 << 20),
        name="mid",
    )(me, *ins, wu, wd)


def tail5_kernel(nf, nt, fast, *refs):
    refs = list(refs)
    if fast:
        me_ref = refs.pop(0)
        *refs, side, small = refs
    (gq_ref, gkv_ref), ns, refs = refs[:2], refs[2 : 2 + nt], refs[2 + nt :]
    g_ref, n5_ref, x5_ref, gm_ref, w_ref, in_ref, vm_ref, v2_ref, gbu_ref = refs[:9]
    (*dwo, gin_ref, vec_ref, dx, x_all, g_all, sums) = refs[9:]
    step = pl.program_id(0)
    r5, width = x5_ref.shape
    half = r5 // 2
    low = low_lanes(half)
    rows = ns[0].shape[0]

    @pl.when(step == 0)
    def _():
        x_all[0:r5, :] = n5_ref[...]
        for c in range(nt):
            x_all[r5 + c * rows : r5 + (c + 1) * rows, :] = ns[c][...]
        dx[...] = jnp.zeros_like(dx)

    for pair in range(width // (2 * HD)):
        lanes = slice(pair * 2 * HD, (pair + 1) * 2 * HD)
        even = g_ref[slot_of(2 * pair, nf, nt)].astype(F32)
        odd = g_ref[slot_of(2 * pair + 1, nf, nt)].astype(F32)
        top = jnp.where(low, even, swap_halves(odd))
        bot = jnp.where(low, swap_halves(even), odd)
        g_all[0:r5, lanes] = jnp.concatenate([top, bot], axis=0).astype(BF)
    dx[...] += nt_dot(g_all[0:r5, :], w_ref[...])

    def finish(end):
        g = g_all[0:end, :]
        sums[pl.ds(step, 1), :] = colsum(g.astype(F32))
        dw = tn_dot(x_all[0:end, :], g)
        if fast:
            side[...] = dw.reshape(side.shape).astype(BF)
        else:
            dwo[0][...] = dw.astype(BF)

    @pl.when(step < 2)
    def _():
        g_all[r5:, :] = gkv_ref[0]
        finish(r5 + nt * rows)

    @pl.when(step == 2)
    def _():
        g_all[r5 : r5 + rows, :] = gq_ref[...]
        finish(r5 + rows)
        n, rstd = normalize(x5_ref[...].astype(F32))
        e = dx[...]
        gin_ref[...] = gm_ref[...] + norm_back(e, n, rstd, row_of(in_ref, GAIN1))
        main = vm_ref[0:1, :] - row_of(in_ref, SHIFT1) * vm_ref[1:2, :]
        vec_ref[0:1, :] = main / row_of(in_ref, GAIN1) + colsum(e * n)
        vec_ref[1:2, :] = vm_ref[1:2, :] + colsum(e)
        vec_ref[2:6, :] = v2_ref[...]
        vec_ref[6:7, :] = sums[2:3, :]
        vec_ref[7:8, :] = sums[1:2, :]
        if fast:
            per = width // small.shape[0]
            lanes = width // 4
            total = 0.0
            for i in range(8):
                part = spread_over(per, vec_ref[i : i + 1, :], 2 * HD)
                part = jnp.concatenate([part, jnp.zeros((part.shape[0], lanes - 2 * HD), F32)], 1)
                total += pltpu.roll(part, i * per, 1) if i else part
            wide = spread_over(gbu_ref.shape[1] // small.shape[0], gbu_ref[...], 2 * HD)
            rest = width - lanes - 2 * HD
            line = jnp.concatenate([total, wide, jnp.zeros((wide.shape[0], rest), F32)], 1)
            small[...] = jnp.broadcast_to(line[:, None, :], small.shape).astype(BF)
            keep, send = (x.at[:, :, side.shape[1] :, :] for x in dwo[0:2])
            put_pieces(me_ref, small, keep, send, ())

    if fast:
        for i in range(3):

            @pl.when(step == (i + 2) % 3)
            def _():
                keep, send = (x.at[:, :, 0 : side.shape[1], :] for x in dwo[2 * i : 2 * i + 2])
                put_pieces(me_ref, side, keep, send, ())


def tail5_call(nf, nt, fast, me, gq, gkv, ns, g, n5, x5, gm, w, vecs, vm, v2, gbu):
    _, r5, width = x5.shape
    at = gm.shape[0] // r5 - 1
    toks = gkv.shape[1]
    part = lambda j: (j + 1) % 3
    bshape = jax.ShapeDtypeStruct
    if fast:
        pu = width // (nf * nt * 2)
        heights = (pu + 8,) * 2 + (pu,) * 4
        wspecs = [full((nt, nf, n, width)) for n in heights]
        wshapes = [bshape((nt, nf, n, width), BF) for n in heights]
        extra = [pltpu.VMEM((nf * nt * 2, n, width), BF) for n in (pu, 8)]
    else:
        wspecs = [pl.BlockSpec((width, width), lambda j, *_: (0, part(j)))]
        wshapes = [bshape((width, 3 * width), BF)]
        extra = []
    return pl.pallas_call(
        functools.partial(tail5_kernel, nf, nt, fast),
        grid_spec=pltpu.PrefetchScalarGridSpec(
            num_scalar_prefetch=int(fast),
            grid=(3,),
            in_specs=[full(gq.shape)]
            + [pl.BlockSpec((1, toks, width), lambda j, *_: (jnp.minimum(j, 1), 0, 0))]
            + [full(x.shape) for x in ns]
            + [
                pl.BlockSpec((g.shape[0], r5 // 2, 2 * HD), lambda j, *_: (0, 0, part(j))),
                full(n5.shape),
                clip_at(x5, nf),
                pl.BlockSpec((r5, width), lambda j, *_: (at, 0)),
                pl.BlockSpec((width, width), lambda j, *_: (0, part(j))),
            ]
            + [full(x.shape) for x in (vecs, vm, v2, gbu)],
            out_specs=wspecs + [full((r5, width)), full((8, width))],
            scratch_shapes=[
                pltpu.VMEM((r5, width), F32),
                pltpu.VMEM((r5 + toks, width), BF),
                pltpu.VMEM((r5 + toks, width), BF),
                pltpu.VMEM((8, width), F32),
            ]
            + extra,
        ),
        out_shape=wshapes + [bshape((r5, width), F32), bshape((8, width), F32)],
        compiler_params=params(),
        cost_estimate=cost(4 * r5 * width * width * 3 + 4 * width * width * toks, 16 << 20),
        name="tail_shared",
    )(*([me] if fast else []), gq, gkv, *ns, g, n5, x5, gm, w, vecs, vm, v2, gbu)


def tail_kernel(nf, nt, *refs):
    dxs, xs, refs = refs[:nt], refs[nt : nt + nf], refs[nt + nf :]
    gm_ref, vec_ref, *gins = refs
    rows = xs[0].shape[0]
    for k in range(nf):
        at = slice(k * rows, (k + 1) * rows)
        e = dxs[0][at, :]
        for c in range(1, nt):
            e = e + dxs[c][at, :].astype(F32)
        n, rstd = normalize(xs[k][...].astype(F32))
        gins[k][...] = (gm_ref[at, :] + norm_back(e, n, rstd, row_of(vec_ref, GAIN1))).astype(BF)


def tail_call(dxs, xs, gm, vecs):
    rows, width = xs[0].shape
    nf, nt = len(xs), len(dxs)
    return pl.pallas_call(
        functools.partial(tail_kernel, nf, nt),
        grid=(1,),
        in_specs=[full((nf * rows, width))] * nt
        + [full((rows, width))] * nf
        + [full((nf * rows, width)), full(vecs.shape)],
        out_specs=[full((rows, width))] * nf,
        out_shape=[jax.ShapeDtypeStruct((rows, width), BF)] * nf,
        compiler_params=params(),
        cost_estimate=cost(30 * nf * rows * width, 6 << 20, 1000),
        name="tail",
    )(*dxs, *xs, gm, vecs)


def pair_sum_kernel(count, *refs):
    ins, (dx, d0, d2, uy, u0, u1) = refs[: 4 * count], refs[4 * count :]
    outs = ((d0, dx.at[0], d2, dx.at[1]), (u0, u1, uy.at[0], uy.at[1]))
    for side in range(2):
        pairs = ins[2 * count * side : 2 * count * (side + 1)]
        at = 0
        for keep, got in zip(pairs[0::2], pairs[1::2]):
            rows = keep.shape[2]
            for k in range(4):
                total = (keep[k, 0].astype(F32) + got[k, 0].astype(F32)).astype(BF)
                outs[side][k][0, at : at + rows, :] = total
            at += rows


def pair_sum(trios):
    _, blocks, _, width = trios[0][0].shape
    steps = blocks // 2
    rows = sum(x[0].shape[2] for x in trios)
    specs, args = [], []
    for first in (0, steps):
        for keep, got in trios:
            spec = pl.BlockSpec((4, 1) + keep.shape[2:], lambda j, f=first: (0, j + f, 0, 0))
            specs += [spec, spec]
            args += [keep, got]
    two = pl.BlockSpec((2, 1, rows, width), lambda j: (0, j, 0, 0))
    one = pl.BlockSpec((1, rows, width), lambda j: (j, 0, 0))
    shape = jax.ShapeDtypeStruct
    return pl.pallas_call(
        functools.partial(pair_sum_kernel, len(trios)),
        grid=(steps,),
        in_specs=specs,
        out_specs=[two, one, one] * 2,
        out_shape=[
            shape((2, steps, rows, width), BF),
            shape((steps, rows, width), BF),
            shape((steps, rows, width), BF),
        ]
        * 2,
        compiler_params=params(),
        cost_estimate=cost(1 << 20, 8 << 20),
        name="pair_sum",
    )(*args)


def relay_sum_kernel(d2, gx, u1, gy, sd, su):
    sd[...] = (d2[...].astype(F32) + gx[0].astype(F32)).astype(BF)
    su[...] = (u1[...].astype(F32) + gy[0].astype(F32)).astype(BF)


def relay_sum(d2, gx, u1, gy):
    second = lambda x: pl.BlockSpec((1,) + x.shape[1:], lambda *_: (1,) + (0,) * (x.ndim - 1))
    return pl.pallas_call(
        relay_sum_kernel,
        grid=(1,),
        in_specs=[full(d2.shape), second(gx), full(u1.shape), second(gy)],
        out_specs=[full(d2.shape), full(u1.shape)],
        out_shape=[jax.ShapeDtypeStruct(d2.shape, BF), jax.ShapeDtypeStruct(u1.shape, BF)],
        compiler_params=params(),
        cost_estimate=cost(d2.size, 6 * d2.size, 1),
        name="relay_sum",
    )(d2, gx, u1, gy)


def along(axis, k, x):
    return lax.ppermute(x, axis, [(i, i ^ k) for i in range(4)])


def relay_start(dx, uy):
    return along("tm", 1, dx), along("tm", 2, uy)


def relay_end(gx, gy, d2, u1):
    sd, su = relay_sum(d2, gx, u1, gy)
    return along("tm", 2, sd), along("tm", 1, su)


def tm_sum_kernel(nf, lead, me_ref, *refs):
    d0, gx, rd, u0, gy, ru = refs[:6]
    outs, total = refs[6 : 6 + nf], refs[-1]
    half = d0.shape[0]
    for first, own, one, two in ((0, d0, gx, rd), (half, u0, gy, ru)):
        for f in range(half):
            part = own[f].astype(F32) + one[0, f, lead:, :].astype(F32) + two[f, lead:, :].astype(F32)
            total[first + f] = part.astype(BF)
    for k in range(nf):
        outs[k][...] = total[me_ref[0] ^ k]


def tm_sum(nf, me, d0, gx, rd, u0, gy, ru):
    _, rows, width = d0.shape
    first = full((1,) + gx.shape[1:])
    return pl.pallas_call(
        functools.partial(tm_sum_kernel, nf, gx.shape[2] - rows),
        grid_spec=pltpu.PrefetchScalarGridSpec(
            num_scalar_prefetch=1,
            grid=(1,),
            in_specs=[full(d0.shape), first, full(rd.shape)] * 2,
            out_specs=[full((rows, width))] * nf,
            scratch_shapes=[pltpu.VMEM((nf, rows, width), BF)],
        ),
        out_shape=[jax.ShapeDtypeStruct((rows, width), BF)] * nf,
        compiler_params=params(),
        cost_estimate=cost(1 << 20, 5 << 20),
        name="tm_sum",
    )(me, d0, gx, rd, u0, gy, ru)


def last_sum_kernel(nf, places, first_vec, per, *refs):
    parts, outs = refs[:nf], refs[nf:]
    if len(parts[0].shape) == 3:
        parts = [parts[0].at[i] for i in range(parts[0].shape[0])]
    for at, rows, out, col in places:
        lanes = parts[0].shape[1]
        total = parts[0][at : at + rows, :].astype(F32)
        for part in parts[1:]:
            total = total + part[at : at + rows, :].astype(F32)
        if out is None:
            for i in range(8):
                outs[first_vec + i][...] = (pltpu.roll(total, lanes - i * per, 1) if i else total)[0, 0:per]
            outs[first_vec + 8][...] = total[0, lanes // 4 : lanes // 4 + outs[first_vec + 8].shape[0]]
        else:
            outs[out][:, col : col + lanes] = total


def last_sum(parts, places, shapes, first_vec=None, per=None):
    nf = len(parts)
    return pl.pallas_call(
        functools.partial(last_sum_kernel, nf, places, first_vec, per),
        out_shape=[jax.ShapeDtypeStruct(x, F32) for x in shapes],
        compiler_params=pltpu.CompilerParams(vmem_limit_bytes=VMEM_LIMIT),
        cost_estimate=cost(nf * parts[0].size, 2 * nf * parts[0].size, 1),
        name="last_sum",
    )(*parts)


def swap_cores(x):
    return lax.ppermute(x, "grp", [(0, 1), (1, 0)])


def exchange(axis, parts):
    pairs = lambda k: [(i, i ^ k) for i in range(len(parts))]
    return [parts[0]] + [lax.ppermute(parts[k], axis, pairs(k)) for k in range(1, len(parts))]


def tie(x, *deps):
    flat, tree = jax.tree.flatten(x)
    tied = lax.optimization_barrier((flat, deps))[0]
    return jax.tree.unflatten(tree, tied)


def over(axes, x):
    return lax.all_to_all(x, axes, 0, 0)


def local(
    nf,
    nt,
    ng,
    inputs,
    gain_one,
    shift_one,
    w_qkv,
    bias_query,
    bias_value,
    w_out,
    bias_out,
    gain_two,
    shift_two,
    w_up,
    bias_up,
    w_down,
    bias_down,
    cotangent,
):
    _, r, width = inputs.shape
    ff = w_up.shape[1]
    dev = nf * nt * ng
    per = width // dev
    fast = ng == 2 and per % 8 == 0 and ff // nf == width
    me = jnp.stack([lax.axis_index(a) for a in ALL]).astype(jnp.int32)
    both = ("freq", "tm")
    *picked, vecs = pick_call(
        nf,
        me,
        inputs,
        (gain_one, shift_one, bias_query, bias_value, bias_out, gain_two, shift_two, bias_down, bias_up),
    )
    xs = exchange("freq", picked)
    n5, pack5 = q5_call(nf, nt, tie(inputs, picked[0]), vecs, w_qkv)
    got5 = over(both, pack5).reshape(-1, 6 * HD)
    nm = ln_call(tie(xs, pack5), vecs)
    ns = exchange("tm", [nm] * nt)
    kv0 = kv_call([nm], w_qkv, vecs, 100)
    o5, r5, ob5, e5 = attn5_fwd_call(tie(got5, kv0))
    att5 = over(both, ob5.reshape(nf * nt, r // 2, 2 * HD))
    cs = exchange("freq", tie(pick_call(nf, me, tie(cotangent, pack5)), nm))
    kv1 = kv_call(tie(ns[1:], ob5), w_qkv, vecs, 0.01)
    att, o, rr, q, e = attn_fwd_call(nm, w_qkv, vecs, kv0, kv1)
    outs, out5, gm, ga, ga5, *dws, vec, gbu = mid_call(
        nf,
        nt,
        fast,
        me,
        xs,
        cs,
        att,
        att5,
        inputs,
        cotangent,
        w_out,
        vecs,
        w_up,
        w_down,
    )
    pieces = lambda x: x.reshape(nt, nf, -1, width)
    pd = ff // dev
    if fast:
        dff = lax.psum_scatter(
            dws[0].reshape(nt * ng, nf * (pd + nf * per), width),
            ("tm", "grp"),
            scatter_dimension=0,
            tiled=True,
        )
        keep_o, got_o = pieces(dws[1]), pieces(swap_cores(dws[2]))
    got_ga5 = over(both, ga5).reshape(-1, 2 * HD)
    gq, gkv = attn_bwd_call(ga, q, kv0, kv1, o, rr, e)
    g5 = attn5_bwd_call(got5, tie(got_ga5, gq, *([got_o] if fast else [])), o5, r5, e5).reshape(nf * nt, r // 2, 6 * HD)
    *dxs, vec_m = dx_call(tie(gq, g5), gkv, ns, w_qkv)
    dxs = exchange("tm", dxs)
    g5 = over(both, g5)
    *dwqkv, gin5, vec8 = tail5_call(
        nf, nt, fast, me, tie(gq, vec_m), gkv, ns, g5, n5, inputs, gm, w_qkv, vecs, vec_m, vec, gbu
    )
    outs = over("freq", tie(outs, g5))
    gin = tail_call(tie(dxs, vec8), xs, gm, vecs)
    order = gin[0]
    gin = exchange("freq", gin)
    if fast:
        trios = [(dwqkv[i], swap_cores(dwqkv[i + 1])) for i in (0, 2, 4)]
        trios += [(keep_o, got_o)]
        trios[0] = (trios[0][0], tie(trios[0][1], order))
        dxq, d0q, d2q, uyq, u0q, u1q = pair_sum(trios)
        gxq, gyq = relay_start(dxq, uyq)
        sdq, suq = relay_sum(d2q, gxq, u1q, gyq)
        rdq, ruq = along("tm", 2, sdq), along("tm", 1, suq)
        dff = over("freq", tie(dff, dxq).reshape(nf, -1, width))
        sums_q = exchange("freq", tm_sum(nf, me, d0q, gxq, rdq, u0q, gyq, ruq))
        places = [(0, pd, 0, 0)] + [(pd + i * per, per, 1, i * width) for i in range(nf)]
        dwd, dwu = last_sum([dff], places, [(pd, width), (per, ff)])
        places = [(0, per, 0, 0), (per, 8, None, 0), (per + 8, per, 0, width)]
        places += [(2 * per + 8, per, 0, 2 * width), (3 * per + 8, per, 1, 0)]
        shapes = [(per, 3 * width), (per, width)] + [(per,)] * 8 + [(pd,)]
        dwqkv, dwo, *small, gbu = last_sum(sums_q, places, shapes, 2, per)
        piece = lambda i: small[i]
    else:
        dwd, dwu, dwo, dwqkv = (
            lax.psum_scatter(x, ALL, scatter_dimension=0, tiled=True).astype(F32)
            for x in dws + dwqkv
        )
        small = vec8.reshape(8, dev, per).transpose(1, 0, 2).reshape(dev, -1)
        small = jnp.concatenate([small, gbu.reshape(dev, pd)], axis=1)
        small = jnp.sum(over(ALL, small), axis=0)
        piece = lambda i: small[i * per : (i + 1) * per]
        gbu = small[8 * per :]
    block_out = jnp.concatenate([outs.astype(F32), out5[None]], axis=0)
    grad_in = assemble_call(nf, me, gin, gin5)
    return (
        block_out,
        grad_in,
        piece(0),
        piece(1),
        dwqkv,
        piece(6),
        piece(7),
        dwo,
        piece(2),
        piece(3),
        piece(4),
        dwu,
        gbu,
        dwd,
        piece(5),
    )


def solution(mesh):
    tokens = P("grp", ("freq", "tm"), None)
    vec = P(ALL)
    mat = P(ALL, None)
    return jax.shard_map(
        functools.partial(local, mesh.shape["freq"], mesh.shape["tm"], mesh.shape["grp"]),
        mesh=mesh,
        in_specs=(tokens,) + (P(),) * 13 + (tokens,),
        out_specs=(
            tokens,
            tokens,
            vec,
            vec,
            mat,
            vec,
            vec,
            mat,
            vec,
            vec,
            vec,
            mat,
            vec,
            mat,
            vec,
        ),
        check_vma=False,
    )
```

time: 292 us -> 275 us (0.942)
  blocking collectives: 16.4 us -> 0 us
  local copies, waits for them, and re-layouts: 21.1 us -> 12.8 us
  Pallas kernels: 129 us -> 136 us
  other arithmetic: 5.57 us -> 1.79 us
    all_to_all x1 -> x0, blocking collectives: 16.4 us -> none  [over(): return lax.all_to_all(x, axes, 0, 0)]
    ppermute x12 -> x18, waiting for transfers between devices: 11.5 us -> 22.1 us  [exchange(): lax.ppermute(parts[k], axis, pairs(k))]
    pallas_call x14 -> x18, Pallas kernels: 101 us -> 111 us  [the longest x1 16.2 us: attn_bwd_call(): pl.pallas_call(attn_bwd_kernel, grid=(steps,), in_specs=[row, row] + kv_s...]
    ppermute x12 -> x18, starting transfers between devices: 17.9 us -> 25.8 us  [exchange(): lax.ppermute(parts[k], axis, pairs(k))]
    broadcast_in_dim x8 -> x0, local copies, waits for them, and re-layouts: 7.47 us -> none  [the longest x2 2.55 us: local(): bq, bv = (bias_query[None], bias_value[None])]
    ppermute x8 -> x4, starting transfers between devices: 9.11 us -> 3.23 us  [along(): return lax.ppermute(x, axis, [(i, i ^ k) for i in range(4)])]
    unnamed x78 -> x72, local copies, waits for them, and re-layouts: 7.46 us -> 12.8 us
    ppermute x8 -> x4, waiting for transfers between devices: 23.7 us -> 18.3 us  [along(): return lax.ppermute(x, axis, [(i, i ^ k) for i in range(4)])]
  transfers between devices with their start and end apart: 29 -> 33, of which waited for: 11 -> 9; matrix products, arithmetic and copies ran while one was open for 6% -> 0% of each run, Pallas kernels for 35% -> 40%
where the time goes in v3:
time: 275 us; the launch traced here: 273 us
  Pallas kernels  136 us (49%)
  starting transfers between devices  64.5 us (23%)
  waiting for transfers between devices  43.5 us (16%)
  between operations  14.4 us (5%)
  local copies, waits for them, and re-layouts  12.8 us (5%)
    all_to_all x6, starting transfers between devices, over(): return lax.all_to_all(x, axes, 0, 0)  34.7 us
    ppermute x18, starting transfers between devices, exchange(): lax.ppermute(parts[k], axis, pairs(k))  25.8 us
    pallas_call x1, Pallas kernels, mid_call(): pl.pallas_call(functools.partial(mid_kernel, nf, nt, fast), grid_spec=plt...  22.9 us
    ppermute x18, waiting for transfers between devices, exchange(): lax.ppermute(parts[k], axis, pairs(k))  22.1 us
    ppermute x4, waiting for transfers between devices, along(): return lax.ppermute(x, axis, [(i, i ^ k) for i in range(4)])  18.3 us
    pallas_call x1, Pallas kernels, attn_bwd_call(): pl.pallas_call(attn_bwd_kernel, grid=(steps,), in_specs=[row, row] + kv_s...  16.2 us
    pallas_call x1, Pallas kernels, attn_fwd_call(): pl.pallas_call(attn_fwd_kernel, grid=(pairs,), in_specs=[full(x.shape), p...  14.6 us
    pallas_call x1, Pallas kernels, tail5_call(): pl.pallas_call(functools.partial(tail5_kernel, nf, nt, fast), grid_spec=p...  13.5 us
  transfers between devices with their start and end apart: 33, of which 9 were waited for; matrix products, arithmetic and copies ran while one was open for 0% of the time, Pallas kernels for 40%

profile of v3, /device:TPU:0, one launch (start us, length us, event | category | flops | bytes accessed | tf_op | source)
XLA Modules:
  0.0 273.1 jit_solution(2189733802557673709)
XLA Ops:
  7.8 2.6 pick.2
  10.4 3.0 %collective-permute-start = (bf16[80,768]{1,0:T(8,128)(2,1)}, bf16[80,768]{1,0:T(8,128)(2,1)S(1)}, u32[]{:S(2)}, u32[]{:S(2)}) collective-permute-start(bf16[80,768]{1,0:T(8,128)(2,1)} %get-tuple-element.113), channel_id=1, source_target_pairs={{0,8},{8,0},{16,24},{24,16},{1,9},{9,1},{17,25},{25,17},{2,10},{10... | collective-permute-start | bytes 368648 | tf_op jit(solution)/shard_map/ppermute | solution.py:1017
  13.4 2.6 collective-permute-start.1
  16.0 3.9 %q_shared.1 = (bf16[80,768]{1,0:T(8,128)(2,1)}, bf16[16,40,384]{2,1,0:T(8,128)(2,1)}) custom-call(bf16[5,80,768]{2,1,0:T(8,128)(2,1)} %refs_9_.1, f32[16,768]{1,0:T(8,128)} %get-tuple-element.117.vec_ref.refs_4_.refs_2_.refs_13_.refs_9_.refs_12_, bf16[768,2304]{1,0:T(8,128)(2,1)} %refs_11_.3), custom_call_target="tpu_custom_call" | custom-call | flops 283115520 | bytes 3538944 | tf_op jit(solution)/shard_map/q_shared/pallas_call | solution.py:193
  19.9 7.1 %all-to-all-start = ((bf16[16,40,384]{2,1,0:T(8,128)(2,1)}), bf16[16,40,384]{2,1,0:T(8,128)(2,1)S(1)}, u32[]{:S(2)}, u32[]{:S(2)}) async-start(bf16[16,40,384]{2,1,0:T(8,128)(2,1)} %get-tuple-element.118), calls=%async_computation | async-start | bytes 983040 | tf_op jit(solution)/shard_map/all_to_all | solution.py:1027
  30.6 2.8 %collective-permute-start.8 = (bf16[320,768]{1,0:T(8,128)(2,1)}, bf16[320,768]{1,0:T(8,128)(2,1)S(1)}, u32[]{:S(2)}, u32[]{:S(2)}) collective-permute-start(bf16[320,768]{1,0:T(8,128)(2,1)} %ln_one.1.refs_0_.x_ref.n0.refs_3_), channel_id=1, source_target_pairs={{0,6},{2,4},{4,2},{6,0},{1,7},{3,5},{5,3},{7,1},{8,14},{10,12},{12... | collective-permute-start | bytes 1474568 | tf_op jit(solution)/shard_map/ppermute | solution.py:1017
  34.1 4.6 %kv.2.k0.v0 = bf16[320,1536]{1,0:T(8,128)(2,1)} custom-call(bf16[320,768]{1,0:T(8,128)(2,1)} %ln_one.1.refs_0_.x_ref.n0.refs_3_, bf16[768,2304]{1,0:T(8,128)(2,1)} %refs_11_.3, f32[16,768]{1,0:T(8,128)} %get-tuple-element.117.vec_ref.refs_4_.refs_2_.refs_13_.refs_9_.refs_12_), custom_call_target="tpu_custom_call" | custom-call | flops 75497472000 | bytes 629145600 | tf_op jit(solution)/shard_map/kv/pallas_call | solution.py:345
  41.7 7.8 %attn_shared_fwd.1 = (f32[640,128]{1,0:T(8,128)}, f32[640,128]{1,0:T(8,128)}, bf16[640,128]{1,0:T(8,128)(2,1)}, bf16[1280,1280]{1,0:T(8,128)(2,1)}) custom-call(bf16[640,384]{1,0:T(8,128)(2,1)} %bitcast.12), custom_call_target="tpu_custom_call" | custom-call | flops 3355443200 | bytes 3276800 | tf_op jit(solution)/shard_map/attn_shared_fwd/pallas_call | solution.py:264
  49.5 4.6 %all-to-all-start.1 = ((bf16[16,40,128]{2,1,0:T(8,128)(2,1)}), bf16[16,40,128]{2,1,0:T(8,128)(2,1)S(1)}, u32[]{:S(2)}, u32[]{:S(2)}) async-start(bf16[16,40,128]{2,1,0:T(8,128)(2,1)} %bitcast.16), calls=%async_computation.1 | async-start | bytes 327680 | tf_op jit(solution)/shard_map/all_to_all | solution.py:1027
  54.4 2.5 pick.3
  58.9 2.3 collective-permute-start.4
  63.0 6.7 %kv.3.k1.v1 = bf16[960,1536]{1,0:T(8,128)(2,1)} custom-call(bf16[320,768]{1,0:T(8,128)(2,1)} %copy-done.11, bf16[320,768]{1,0:T(8,128)(2,1)} %copy-done.10, bf16[320,768]{1,0:T(8,128)(2,1)} %copy-done.9, bf16[768,2304]{1,0:T(8,128)(2,1)} %refs_11_.3, f32[16,768]{1,0:T(8,128)} %get-tuple-element.117.vec_ref.refs_4_.refs_2_.refs_13_.refs_9_.refs_12_), custom_call_target="tpu_custom_call" | custom-call | flops 22649240 | bytes 62914 | tf_op jit(solution)/shard_map/kv/pallas_call | solution.py:345
  69.6 14.6 %attn_fwd.1 = (bf16[320,768]{1,0:T(8,128)(2,1)}, f32[320,768]{1,0:T(8,128)}, f32[320,768]{1,0:T(8,128)}, bf16[320,768]{1,0:T(8,128)(2,1)}, bf16[12,320,1280]{2,1,0:T(8,128)(2,1)}) custom-call(bf16[320,768]{1,0:T(8,128)(2,1)} %ln_one.1.refs_0_.x_ref.n0.refs_3_, bf16[768,2304]{1,0:T(8,128)(2,1)} %refs_11_.3, ...), custom_call_target="tpu_custom_call" | custom-call | flops 50331648 | bytes 209715 | tf_op jit(solution)/shard_map/attn_fwd/pallas_call | solution.py:396
  85.0 22.9 %mid.1 = (bf16[4,80,768]{2,1,0:T(8,128)(2,1)}, f32[80,768]{1,0:T(8,128)}, f32[400,768]{1,0:T(8,128)}, bf16[320,768]{1,0:T(8,128)(2,1)}, bf16[16,40,128]{2,1,0:T(...) custom-call(s32[3]{0:T(128)} %pad_add_fusion.me_ref.refs_0_, ...), custom_call_target="tpu_custom_call" | custom-call | flops 12740198400 | bytes 25165824 | tf_op jit(solution)/shard_map/mid/pallas_call | solution.py:671
  108.0 7.0 %all-to-all-start.2 = ((bf16[16,40,128]{2,1,0:T(8,128)(2,1)}), bf16[16,40,128]{2,1,0:T(8,128)(2,1)S(1)}, u32[]{:S(2)}, u32[]{:S(2)}) async-start(bf16[16,40,128]{2,1,0:T(8,128)(2,1)} %get-tuple-element.139), calls=%async_computation.2 | async-start | bytes 327680 | tf_op jit(solution)/shard_map/all_to_all | solution.py:1027
  115.1 16.2 %attn_bwd.1 = (bf16[320,768]{1,0:T(8,128)(2,1)}, bf16[2,1280,768]{2,1,0:T(8,128)(2,1)}) custom-call(bf16[320,768]{1,0:T(8,128)(2,1)} %get-tuple-element.140.ga_ref, bf16[320,768]{1,0:T(8,128)(2,1)} %get-tuple-element.141.q_ref, bf16[320,1536]{1,0:T(8,128)(2,1)} %kv.2.k0.v0, bf16[960,1536]{1,0:T(8,128)(2,1)} %kv.3.k1.v1, bf16[320,1536]{1,0:T(8,128)(2,1)} %kv.2.k0.v0, ...), custom_call_target="tpu_custom_call" | custom-call | flops 10066329600 | bytes 25165824 | tf_op jit(solution)/shard_map/attn_bwd/pallas_call | solution.py:443
  131.9 7.9 %attn_shared_bwd.1 = bf16[640,384]{1,0:T(8,128)(2,1)} custom-call(bf16[640,384]{1,0:T(8,128)(2,1)} %bitcast.13, bf16[640,128]{1,0:T(8,128)(2,1)} %bitcast.17, f32[640,128]{1,0:T(8,128)} %get-tuple-element.148.o_ref, f32[640,128]{1,0:T(8,128)} %get-tuple-element.149.r_ref, bf16[1280,1280]{1,0:T(8,128)(2,1)} %get-tuple-element.150.e_ref), custom_call_target="tpu_custom_call" | custom-call | flops 6710886400 | bytes 3276800 | tf_op jit(solution)/shard_map/attn_shared_bwd/pallas_call | solution.py:316
  139.8 6.9 %all-to-all-start.3 = ((bf16[16,40,384]{2,1,0:T(8,128)(2,1)}), bf16[16,40,384]{2,1,0:T(8,128)(2,1)S(1)}, u32[]{:S(2)}, u32[]{:S(2)}) async-start(bf16[16,40,384]{2,1,0:T(8,128)(2,1)} %bitcast.14), calls=%async_computation.3 | async-start | bytes 983040 | tf_op jit(solution)/shard_map/all_to_all | solution.py:1027
  146.7 10.7 %dx.1 = (f32[320,768]{1,0:T(8,128)}, bf16[320,768]{1,0:T(8,128)(2,1)}, bf16[320,768]{1,0:T(8,128)(2,1)}, bf16[320,768]{1,0:T(8,128)(2,1)}, f32[2,768]{1,0:T(2,128)}) custom-call(bf16[320,768]{1,0:T(8,128)(2,1)} %get-tuple-element.169.gq_ref.refs_1_, bf16[2,1280,768]{2,1,0:T(8,128)(2,1)} %get-tuple-element.154.gkv_ref.refs_2_, ...), custom_call_target="tpu_custom_call" | custom-call | flops 3019898880 | bytes 12582912 | tf_op jit(solution)/shard_map/dx/pallas_call | solution.py:515
  162.4 13.5 %tail_shared.1 = (bf16[4,4,32,768]{3,2,1,0:T(8,128)(2,1)}, bf16[4,4,32,768]{3,2,1,0:T(8,128)(2,1)}, bf16[4,4,24,768]{3,2,1,0:T(8,128)(2,1)}, bf16[4,4,24,768]{3,...) custom-call(s32[3]{0:T(128)} %pad_add_fusion.me_ref.refs_0_, ...), custom_call_target="tpu_custom_call" | custom-call | flops 3586129920 | bytes 16777216 | tf_op jit(solution)/shard_map/tail_shared/pallas_call | solution.py:814
  175.9 4.3 %all-to-all-start.4 = ((bf16[4,80,768]{2,1,0:T(8,128)(2,1)}), bf16[4,80,768]{2,1,0:T(8,128)(2,1)S(1)}, u32[]{:S(2)}, u32[]{:S(2)}) async-start(bf16[4,80,768]{2,1,0:T(8,128)(2,1)} %get-tuple-element.151), calls=%async_computation.4 | async-start | bytes 983040 | tf_op jit(solution)/shard_map/all_to_all | solution.py:1027
  180.2 14.6 %collective-permute-done.12.refs_3_ = bf16[320,768]{1,0:T(8,128)(2,1)S(1)} collective-permute-done((bf16[320,768]{1,0:T(8,128)(2,1)}, bf16[320,768]{1,0:T(8,128)(2,1)S(1)}, u32[]{:S(2)}, u32[]{:S(2)}) %collective-permute-start.12) | collective-permute-done | bytes 491552 | tf_op jit(solution)/shard_map/ppermute | solution.py:1017
  196.1 3.7 %tail.1 = (bf16[80,768]{1,0:T(8,128)(2,1)}, bf16[80,768]{1,0:T(8,128)(2,1)}, bf16[80,768]{1,0:T(8,128)(2,1)}, bf16[80,768]{1,0:T(8,128)(2,1)}) custom-call(f32[320,768]{1,0:T(8,128)} %get-tuple-element.159.refs_0_, bf16[320,768]{1,0:T(8,128)(2,1)} %copy-done.27, bf16[320,768]{1,0:T(8,128)(2,1)} %copy-done.28, bf16[320,768]{1,0:T(8,128)(2,1)} %copy-done.29, ...), custom_call_target="tpu_custom_call" | custom-call | flops 7372800000 | bytes 6291456000 | tf_op jit(solution)/shard_map/tail/pallas_call | solution.py:862
  201.1 3.9 %pair_sum.1 = (bf16[2,2,104,768]{3,2,1,0:T(8,128)(2,1)}, bf16[2,104,768]{2,1,0:T(8,128)(2,1)}, bf16[2,104,768]{2,1,0:T(8,128)(2,1)}, bf16[2,2,104,768]{3,2,1,0:T...) custom-call(bf16[4,4,32,768]{3,2,1,0:T(8,128)(2,1)} %get-tuple-element.174.refs_0_.refs_8_, ...), custom_call_target="tpu_custom_call" | custom-call | flops 1048576 | bytes 8388608 | tf_op jit(solution)/shard_map/pair_sum/pallas_call | solution.py:903
  205.1 4.8 %all-to-all-start.5 = ((bf16[4,192,768]{2,1,0:T(8,128)(2,1)}), bf16[4,192,768]{2,1,0:T(8,128)(2,1)S(1)}, u32[]{:S(2)}, u32[]{:S(2)}) async-start(bf16[4,192,768]{2,1,0:T(8,128)(2,1)} %bitcast.11), calls=%async_computation.6 | async-start | bytes 2359296 | tf_op jit(solution)/shard_map/all_to_all | solution.py:1027
  211.0 15.1 %collective-permute-done.20.gy.refs_4_ = bf16[2,2,104,768]{3,2,1,0:T(8,128)(2,1)S(1)} collective-permute-done((bf16[2,2,104,768]{3,2,1,0:T(8,128)(2,1)}, bf16[2,2,104,768]{3,2,1,0:T(8,128)(2,1)S(1)}, u32[]{:S(2)}, u32[]{:S(2)}) %collective-permute-start.20) | collective-permute-done | bytes 639008 | tf_op jit(solution)/shard_map/ppermute | solution.py:940
  233.1 2.4 collective-permute-start.14
  239.5 3.3 %tm_sum.1 = (bf16[104,768]{1,0:T(8,128)(2,1)}, bf16[104,768]{1,0:T(8,128)(2,1)}, bf16[104,768]{1,0:T(8,128)(2,1)}, bf16[104,768]{1,0:T(8,128)(2,1)}) custom-call(s32[3]{0:T(128)} %pad_add_fusion.me_ref.refs_0_, bf16[2,104,768]{2,1,0:T(8,128)(2,1)} %get-tuple-element.182.refs_0_, bf16[2,2,104,768]{3,2,1,0:T(8,128)(2,1)} %copy-done.3, ...), custom_call_target="tpu_custom_call" | custom-call | flops 1048576 | bytes 5242880 | tf_op jit(solution)/shard_map/tm_sum/pallas_call | solution.py:967
  244.2 2.4 collective-permute-start.24
  247.2 3.8 %collective-permute-done.14.refs_2_ = bf16[80,768]{1,0:T(8,128)(2,1)S(1)} collective-permute-done((bf16[80,768]{1,0:T(8,128)(2,1)S(1)}, bf16[80,768]{1,0:T(8,128)(2,1)S(1)}, u32[]{:S(2)}, u32[]{:S(2)}) %collective-permute-start.14) | collective-permute-done | bytes 122912 | tf_op jit(solution)/shard_map/ppermute | solution.py:1017
  251.6 3.0 %assemble.1 = f32[5,80,768]{2,1,0:T(8,128)} custom-call(s32[3]{0:T(128)} %pad_add_fusion.me_ref.refs_0_, bf16[80,768]{1,0:T(8,128)(2,1)} %get-tuple-element.164.refs_0_, bf16[80,768]{1,0:T(8,128)(2,1)} %copy-done.20, bf16[80,768]{1,0:T(8,128)(2,1)} %copy-done.21, bf16[80,768]{1,0:T(8,128)(2,1)} %copy-done.22, f32[80,768]{1,0:T(8,128)} %get-tuple-element.173.refs_4_), custom_call_target="tpu_custom_call" | custom-call | bytes 2457600 | tf_op jit(solution)/shard_map/assemble/pallas_call | solution.py:129
  256.7 3.7 %collective-permute-done.24.refs_2_ = bf16[104,768]{1,0:T(8,128)(2,1)S(1)} collective-permute-done((bf16[104,768]{1,0:T(8,128)(2,1)}, bf16[104,768]{1,0:T(8,128)(2,1)S(1)}, u32[]{:S(2)}, u32[]{:S(2)}) %collective-permute-start.24) | collective-permute-done | bytes 159776 | tf_op jit(solution)/shard_map/ppermute | solution.py:1017
  (130 shorter events, 43.7 us)
Async XLA Ops:
  10.4 16.6 %collective-permute-start = (bf16[80,768]{1,0:T(8,128)(2,1)}, bf16[80,768]{1,0:T(8,128)(2,1)S(1)}, u32[]{:S(2)}, u32[]{:S(2)}) collective-permute-start(bf16[80,768]{1,0:T(8,128)(2,1)} %get-tuple-element.113), channel_id=1, source_target_pairs={{0,8},{8,0},{16,24},{24,16},{1,9},{9,1},{17,25},{25,17},{2,10},{10... | collective-permute-start | bytes 368648 | tf_op jit(solution)/shard_map/ppermute | solution.py:1017
  13.4 13.6 %collective-permute-start.1 = (bf16[80,768]{1,0:T(8,128)(2,1)}, bf16[80,768]{1,0:T(8,128)(2,1)S(1)}, u32[]{:S(2)}, u32[]{:S(2)}) collective-permute-start(bf16[80,768]{1,0:T(8,128)(2,1)} %get-tuple-element.114), channel_id=1, source_target_pairs={{0,16},{8,24},{16,0},{24,8},{1,17},{9,25},{17,1},{25,9},{2,18},{10... | collective-permute-start | bytes 368648 | tf_op jit(solution)/shard_map/ppermute | solution.py:1017
  16.0 11.0 %collective-permute-start.2 = (bf16[80,768]{1,0:T(8,128)(2,1)}, bf16[80,768]{1,0:T(8,128)(2,1)S(1)}, u32[]{:S(2)}, u32[]{:S(2)}) collective-permute-start(bf16[80,768]{1,0:T(8,128)(2,1)} %get-tuple-element.115), channel_id=1, source_target_pairs={{0,24},{8,16},{16,8},{24,0},{1,25},{9,17},{17,9},{25,1},{2,26},{10... | collective-permute-start | bytes 368648 | tf_op jit(solution)/shard_map/ppermute | solution.py:1017
  19.9 21.0 %all-to-all-start = ((bf16[16,40,384]{2,1,0:T(8,128)(2,1)}), bf16[16,40,384]{2,1,0:T(8,128)(2,1)S(1)}, u32[]{:S(2)}, u32[]{:S(2)}) async-start(bf16[16,40,384]{2,1,0:T(8,128)(2,1)} %get-tuple-element.118), calls=%async_computation | async-start | bytes 983040 | tf_op jit(solution)/shard_map/all_to_all | solution.py:1027
  30.6 30.6 %collective-permute-start.8 = (bf16[320,768]{1,0:T(8,128)(2,1)}, bf16[320,768]{1,0:T(8,128)(2,1)S(1)}, u32[]{:S(2)}, u32[]{:S(2)}) collective-permute-start(bf16[320,768]{1,0:T(8,128)(2,1)} %ln_one.1.refs_0_.x_ref.n0.refs_3_), channel_id=1, source_target_pairs={{0,6},{2,4},{4,2},{6,0},{1,7},{3,5},{5,3},{7,1},{8,14},{10,12},{12... | collective-permute-start | bytes 1474568 | tf_op jit(solution)/shard_map/ppermute | solution.py:1017
  33.4 27.9 %collective-permute-start.7 = (bf16[320,768]{1,0:T(8,128)(2,1)}, bf16[320,768]{1,0:T(8,128)(2,1)S(1)}, u32[]{:S(2)}, u32[]{:S(2)}) collective-permute-start(bf16[320,768]{1,0:T(8,128)(2,1)} %ln_one.1.refs_0_.x_ref.n0.refs_3_), channel_id=1, source_target_pairs={{0,4},{2,6},{4,0},{6,2},{1,5},{3,7},{5,1},{7,3},{8,12},{10,14},{12... | collective-permute-start | bytes 1474568 | tf_op jit(solution)/shard_map/ppermute | solution.py:1017
  34.0 27.3 %collective-permute-start.6 = (bf16[320,768]{1,0:T(8,128)(2,1)}, bf16[320,768]{1,0:T(8,128)(2,1)S(1)}, u32[]{:S(2)}, u32[]{:S(2)}) collective-permute-start(bf16[320,768]{1,0:T(8,128)(2,1)} %ln_one.1.refs_0_.x_ref.n0.refs_3_), channel_id=1, source_target_pairs={{0,2},{2,0},{4,6},{6,4},{1,3},{3,1},{5,7},{7,5},{8,10},{10,8},{12,... | collective-permute-start | bytes 1474568 | tf_op jit(solution)/shard_map/ppermute | solution.py:1017
  49.5 34.8 %all-to-all-start.1 = ((bf16[16,40,128]{2,1,0:T(8,128)(2,1)}), bf16[16,40,128]{2,1,0:T(8,128)(2,1)S(1)}, u32[]{:S(2)}, u32[]{:S(2)}) async-start(bf16[16,40,128]{2,1,0:T(8,128)(2,1)} %bitcast.16), calls=%async_computation.1 | async-start | bytes 327680 | tf_op jit(solution)/shard_map/all_to_all | solution.py:1027
  54.2 150.9 %reduce-scatter.2.cloned.1.call-start = ((), (), s32[]{:S(2)}) async-start(), calls=%async_computation.7 | async-start | bytes 10616832 | tf_op jit(solution)/shard_map/reduce_scatter | solution.py:1093
  56.9 27.3 %collective-permute-start.3 = (bf16[80,768]{1,0:T(8,128)(2,1)}, bf16[80,768]{1,0:T(8,128)(2,1)S(1)}, u32[]{:S(2)}, u32[]{:S(2)}) collective-permute-start(bf16[80,768]{1,0:T(8,128)(2,1)} %get-tuple-element.129), channel_id=1, source_target_pairs={{0,8},{8,0},{16,24},{24,16},{1,9},{9,1},{17,25},{25,17},{2,10},{10... | collective-permute-start | bytes 368648 | tf_op jit(solution)/shard_map/ppermute | solution.py:1017
  58.9 25.4 %collective-permute-start.4 = (bf16[80,768]{1,0:T(8,128)(2,1)}, bf16[80,768]{1,0:T(8,128)(2,1)S(1)}, u32[]{:S(2)}, u32[]{:S(2)}) collective-permute-start(bf16[80,768]{1,0:T(8,128)(2,1)} %get-tuple-element.130), channel_id=1, source_target_pairs={{0,16},{8,24},{16,0},{24,8},{1,17},{9,25},{17,1},{25,9},{2,18},{10... | collective-permute-start | bytes 368648 | tf_op jit(solution)/shard_map/ppermute | solution.py:1017
  61.2 23.1 %collective-permute-start.5 = (bf16[80,768]{1,0:T(8,128)(2,1)}, bf16[80,768]{1,0:T(8,128)(2,1)S(1)}, u32[]{:S(2)}, u32[]{:S(2)}) collective-permute-start(bf16[80,768]{1,0:T(8,128)(2,1)} %get-tuple-element.131), channel_id=1, source_target_pairs={{0,24},{8,16},{16,8},{24,0},{1,25},{9,17},{17,9},{25,1},{2,26},{10... | collective-permute-start | bytes 368648 | tf_op jit(solution)/shard_map/ppermute | solution.py:1017
  108.0 23.3 %all-to-all-start.2 = ((bf16[16,40,128]{2,1,0:T(8,128)(2,1)}), bf16[16,40,128]{2,1,0:T(8,128)(2,1)S(1)}, u32[]{:S(2)}, u32[]{:S(2)}) async-start(bf16[16,40,128]{2,1,0:T(8,128)(2,1)} %get-tuple-element.139), calls=%async_computation.2 | async-start | bytes 327680 | tf_op jit(solution)/shard_map/all_to_all | solution.py:1027
  115.0 16.3 %collective-permute-start.9 = (bf16[4,4,24,768]{3,2,1,0:T(8,128)(2,1)S(1)}, bf16[4,4,24,768]{3,2,1,0:T(8,128)(2,1)S(1)}, u32[]{:S(2)}, u32[]{:S(2)}) collective-permute-start(bf16[4,4,24,768]{3,2,1,0:T(8,128)(2,1)S(1)} %copy-done.26), channel_id=1, source_target_pairs={{0,1},{1,0},{2,3},{3,2},{4,5},{5,4},{6,7},{7,6},{8,9},{9,8},{10,11... | collective-permute-start | bytes 1769480 | tf_op jit(solution)/shard_map/ppermute | solution.py:1012
  139.8 21.8 %all-to-all-start.3 = ((bf16[16,40,384]{2,1,0:T(8,128)(2,1)}), bf16[16,40,384]{2,1,0:T(8,128)(2,1)S(1)}, u32[]{:S(2)}, u32[]{:S(2)}) async-start(bf16[16,40,384]{2,1,0:T(8,128)(2,1)} %bitcast.14), calls=%async_computation.3 | async-start | bytes 983040 | tf_op jit(solution)/shard_map/all_to_all | solution.py:1027
  157.4 22.8 %collective-permute-start.10 = (bf16[320,768]{1,0:T(8,128)(2,1)}, bf16[320,768]{1,0:T(8,128)(2,1)S(1)}, u32[]{:S(2)}, u32[]{:S(2)}) collective-permute-start(bf16[320,768]{1,0:T(8,128)(2,1)} %get-tuple-element.156), channel_id=1, source_target_pairs={{0,2},{2,0},{4,6},{6,4},{1,3},{3,1},{5,7},{7,5},{8,10},{10,8},{12,... | collective-permute-start | bytes 1474568 | tf_op jit(solution)/shard_map/ppermute | solution.py:1017
  159.3 20.9 %collective-permute-start.11 = (bf16[320,768]{1,0:T(8,128)(2,1)}, bf16[320,768]{1,0:T(8,128)(2,1)S(1)}, u32[]{:S(2)}, u32[]{:S(2)}) collective-permute-start(bf16[320,768]{1,0:T(8,128)(2,1)} %get-tuple-element.157), channel_id=1, source_target_pairs={{0,4},{2,6},{4,0},{6,2},{1,5},{3,7},{5,1},{7,3},{8,12},{10,14},{12... | collective-permute-start | bytes 1474568 | tf_op jit(solution)/shard_map/ppermute | solution.py:1017
  160.6 34.2 %collective-permute-start.12 = (bf16[320,768]{1,0:T(8,128)(2,1)}, bf16[320,768]{1,0:T(8,128)(2,1)S(1)}, u32[]{:S(2)}, u32[]{:S(2)}) collective-permute-start(bf16[320,768]{1,0:T(8,128)(2,1)} %get-tuple-element.158), channel_id=1, source_target_pairs={{0,6},{2,4},{4,2},{6,0},{1,7},{3,5},{5,3},{7,1},{8,14},{10,12},{12... | collective-permute-start | bytes 1474568 | tf_op jit(solution)/shard_map/ppermute | solution.py:1017
  175.9 23.9 %collective-permute-start.16 = (bf16[4,4,32,768]{3,2,1,0:T(8,128)(2,1)}, bf16[4,4,32,768]{3,2,1,0:T(8,128)(2,1)S(1)}, u32[]{:S(2)}, u32[]{:S(2)}) collective-permute-start(bf16[4,4,32,768]{3,2,1,0:T(8,128)(2,1)} %get-tuple-element.175), channel_id=1, source_target_pairs={{0,1},{1,0},{2,3},{3,2},{4,5},{5,4},{6,7},{7,6},{8,9},{9,8},{10,11... | collective-permute-start | bytes 2359304 | tf_op jit(solution)/shard_map/ppermute | solution.py:1012
  175.9 29.1 %all-to-all-start.4 = ((bf16[4,80,768]{2,1,0:T(8,128)(2,1)}), bf16[4,80,768]{2,1,0:T(8,128)(2,1)S(1)}, u32[]{:S(2)}, u32[]{:S(2)}) async-start(bf16[4,80,768]{2,1,0:T(8,128)(2,1)} %get-tuple-element.151), calls=%async_computation.4 | async-start | bytes 983040 | tf_op jit(solution)/shard_map/all_to_all | solution.py:1027
  195.6 4.2 %collective-permute-start.18 = (bf16[4,4,24,768]{3,2,1,0:T(8,128)(2,1)}, bf16[4,4,24,768]{3,2,1,0:T(8,128)(2,1)S(1)}, u32[]{:S(2)}, u32[]{:S(2)}) collective-permute-start(bf16[4,4,24,768]{3,2,1,0:T(8,128)(2,1)} %get-tuple-element.180), channel_id=1, source_target_pairs={{0,1},{1,0},{2,3},{3,2},{4,5},{5,4},{6,7},{7,6},{8,9},{9,8},{10,11... | collective-permute-start | bytes 1769480 | tf_op jit(solution)/shard_map/ppermute | solution.py:1012
  205.1 58.0 %all-to-all-start.5 = ((bf16[4,192,768]{2,1,0:T(8,128)(2,1)}), bf16[4,192,768]{2,1,0:T(8,128)(2,1)S(1)}, u32[]{:S(2)}, u32[]{:S(2)}) async-start(bf16[4,192,768]{2,1,0:T(8,128)(2,1)} %bitcast.11), calls=%async_computation.6 | async-start | bytes 2359296 | tf_op jit(solution)/shard_map/all_to_all | solution.py:1027
  209.8 16.3 %collective-permute-start.20 = (bf16[2,2,104,768]{3,2,1,0:T(8,128)(2,1)}, bf16[2,2,104,768]{3,2,1,0:T(8,128)(2,1)S(1)}, u32[]{:S(2)}, u32[]{:S(2)}) collective-permute-start(bf16[2,2,104,768]{3,2,1,0:T(8,128)(2,1)} %get-tuple-element.186), channel_id=1, source_target_pairs={{0,4},{2,6},{4,0},{6,2},{1,5},{3,7},{5,1},{7,3},{8,12},{10,14},{12... | collective-permute-start | bytes 1916936 | tf_op jit(solution)/shard_map/ppermute | solution.py:940
  210.5 15.9 %collective-permute-start.19 = (bf16[2,2,104,768]{3,2,1,0:T(8,128)(2,1)}, bf16[2,2,104,768]{3,2,1,0:T(8,128)(2,1)S(1)}, u32[]{:S(2)}, u32[]{:S(2)}) collective-permute-start(bf16[2,2,104,768]{3,2,1,0:T(8,128)(2,1)} %get-tuple-element.183), channel_id=1, source_target_pairs={{0,2},{2,0},{4,6},{6,4},{1,3},{3,1},{5,7},{7,5},{8,10},{10,8},{12,... | collective-permute-start | bytes 1916936 | tf_op jit(solution)/shard_map/ppermute | solution.py:940
  229.4 8.4 %collective-permute-start.21 = (bf16[2,104,768]{2,1,0:T(8,128)(2,1)}, bf16[2,104,768]{2,1,0:T(8,128)(2,1)S(1)}, u32[]{:S(2)}, u32[]{:S(2)}) collective-permute-start(bf16[2,104,768]{2,1,0:T(8,128)(2,1)} %get-tuple-element.187), channel_id=1, source_target_pairs={{0,4},{2,6},{4,0},{6,2},{1,5},{3,7},{5,1},{7,3},{8,12},{10,14},{12... | collective-permute-start | bytes 958472 | tf_op jit(solution)/shard_map/ppermute | solution.py:940
  230.9 7.9 %collective-permute-start.22 = (bf16[2,104,768]{2,1,0:T(8,128)(2,1)}, bf16[2,104,768]{2,1,0:T(8,128)(2,1)S(1)}, u32[]{:S(2)}, u32[]{:S(2)}) collective-permute-start(bf16[2,104,768]{2,1,0:T(8,128)(2,1)} %get-tuple-element.189), channel_id=1, source_target_pairs={{0,2},{2,0},{4,6},{6,4},{1,3},{3,1},{5,7},{7,5},{8,10},{10,8},{12,... | collective-permute-start | bytes 958472 | tf_op jit(solution)/shard_map/ppermute | solution.py:940
  231.5 15.1 %collective-permute-start.13 = (bf16[80,768]{1,0:T(8,128)(2,1)S(1)}, bf16[80,768]{1,0:T(8,128)(2,1)S(1)}, u32[]{:S(2)}, u32[]{:S(2)}) collective-permute-start(bf16[80,768]{1,0:T(8,128)(2,1)S(1)} %copy-done.32), channel_id=1, source_target_pairs={{0,8},{8,0},{16,24},{24,16},{1,9},{9,1},{17,25},{25,17},{2,10},{10... | collective-permute-start | bytes 368648 | tf_op jit(solution)/shard_map/ppermute | solution.py:1017
  233.1 17.8 %collective-permute-start.14 = (bf16[80,768]{1,0:T(8,128)(2,1)S(1)}, bf16[80,768]{1,0:T(8,128)(2,1)S(1)}, u32[]{:S(2)}, u32[]{:S(2)}) collective-permute-start(bf16[80,768]{1,0:T(8,128)(2,1)S(1)} %copy-done.31), channel_id=1, source_target_pairs={{0,16},{8,24},{16,0},{24,8},{1,17},{9,25},{17,1},{25,9},{2,18},{10... | collective-permute-start | bytes 368648 | tf_op jit(solution)/shard_map/ppermute | solution.py:1017
  235.5 15.5 %collective-permute-start.15 = (bf16[80,768]{1,0:T(8,128)(2,1)S(1)}, bf16[80,768]{1,0:T(8,128)(2,1)S(1)}, u32[]{:S(2)}, u32[]{:S(2)}) collective-permute-start(bf16[80,768]{1,0:T(8,128)(2,1)S(1)} %copy-done.30), channel_id=1, source_target_pairs={{0,24},{8,16},{16,8},{24,0},{1,25},{9,17},{17,9},{25,1},{2,26},{10... | collective-permute-start | bytes 368648 | tf_op jit(solution)/shard_map/ppermute | solution.py:1017
  242.8 13.9 %collective-permute-start.23 = (bf16[104,768]{1,0:T(8,128)(2,1)}, bf16[104,768]{1,0:T(8,128)(2,1)S(1)}, u32[]{:S(2)}, u32[]{:S(2)}) collective-permute-start(bf16[104,768]{1,0:T(8,128)(2,1)} %get-tuple-element.191), channel_id=1, source_target_pairs={{0,8},{8,0},{16,24},{24,16},{1,9},{9,1},{17,25},{25,17},{2,10},{10... | collective-permute-start | bytes 479240 | tf_op jit(solution)/shard_map/ppermute | solution.py:1017
  244.2 16.3 %collective-permute-start.24 = (bf16[104,768]{1,0:T(8,128)(2,1)}, bf16[104,768]{1,0:T(8,128)(2,1)S(1)}, u32[]{:S(2)}, u32[]{:S(2)}) collective-permute-start(bf16[104,768]{1,0:T(8,128)(2,1)} %get-tuple-element.192), channel_id=1, source_target_pairs={{0,16},{8,24},{16,0},{24,8},{1,17},{9,25},{17,1},{25,9},{2,18},{10... | collective-permute-start | bytes 479240 | tf_op jit(solution)/shard_map/ppermute | solution.py:1017
  246.5 13.9 %collective-permute-start.25 = (bf16[104,768]{1,0:T(8,128)(2,1)}, bf16[104,768]{1,0:T(8,128)(2,1)S(1)}, u32[]{:S(2)}, u32[]{:S(2)}) collective-permute-start(bf16[104,768]{1,0:T(8,128)(2,1)} %get-tuple-element.193), channel_id=1, source_target_pairs={{0,24},{8,16},{16,8},{24,0},{1,25},{9,17},{17,9},{25,1},{2,26},{10... | collective-permute-start | bytes 479240 | tf_op jit(solution)/shard_map/ppermute | solution.py:1017
  (37 other events, 151.8 us)
Sparse Core Ops, SparseCore 0:
  108.1 95.8 reduce-scatter.1

commit v4 on v3

--- a/solution.py
+++ b/solution.py
@@ -13,6 +13,7 @@
 F32 = jnp.float32
 ALL = ("freq", "tm", "grp")
 VMEM_LIMIT = 60 * 1024 * 1024
+SAFE = 50.0
 GAIN1, SHIFT1, BIAS_Q, BIAS_V, BIAS_OUT, GAIN2, SHIFT2, BIAS_DOWN, BIAS_UP = range(9)
 
 
@@ -84,10 +85,11 @@
     )
 
 
-def pick_kernel(nf, count, me_ref, x_ref, *refs):
-    vecs, outs = refs[:count], refs[count:]
+def pick_kernel(nf, count, me_ref, x_ref, c_ref, *refs):
+    vecs, outs, cots = refs[:count], refs[count : -nf], refs[-nf:]
     for k in range(nf):
         outs[k][...] = x_ref[me_ref[0] ^ k]
+        cots[k][...] = c_ref[me_ref[0] ^ k]
     if count:
         width = x_ref.shape[2]
         for i in range(count - 1):
@@ -98,7 +100,7 @@
             outs[nf][at : at + 1, :] = last[i * width : (i + 1) * width].reshape(1, width)
 
 
-def pick_call(nf, me, x, vecs=()):
+def pick_call(nf, me, x, c, vecs):
     _, rows, width = x.shape
     count = 8 + -(-sum(v.shape[0] for v in vecs) // width) // 8 * 8
     more = [(count, width)] if vecs else []
@@ -107,15 +109,18 @@
         grid_spec=pltpu.PrefetchScalarGridSpec(
             num_scalar_prefetch=1,
             grid=(1,),
-            in_specs=[full(x.shape)] + [full(v.shape) for v in vecs],
-            out_specs=[full((rows, width))] * nf + [full(y) for y in more],
+            in_specs=[full(x.shape)] * 2 + [full(v.shape) for v in vecs],
+            out_specs=[full((rows, width))] * nf
+            + [full(y) for y in more]
+            + [full((rows, width))] * nf,
         ),
         out_shape=[jax.ShapeDtypeStruct((rows, width), BF)] * nf
-        + [jax.ShapeDtypeStruct(y, F32) for y in more],
+        + [jax.ShapeDtypeStruct(y, F32) for y in more]
+        + [jax.ShapeDtypeStruct((rows, width), BF)] * nf,
         compiler_params=params(),
-        cost_estimate=cost(0, 4 * x.size),
+        cost_estimate=cost(0, 8 * x.size),
         name="pick",
-    )(me, x, *vecs)
+    )(me, x, c, *vecs)
 
 
 def assemble_kernel(nf, me_ref, *refs):
@@ -159,7 +164,7 @@
         out_specs=full((len(xs) * rows, width)),
         out_shape=jax.ShapeDtypeStruct((len(xs) * rows, width), BF),
         compiler_params=pltpu.CompilerParams(vmem_limit_bytes=VMEM_LIMIT),
-        cost_estimate=cost(len(xs) * rows * width * 10, len(xs) * rows * width * 4, 100),
+        cost_estimate=cost(len(xs) * rows * width * 10, len(xs) * rows * width * 4, 10000),
         name="ln_one",
     )(*xs, vecs)
 
@@ -223,6 +228,13 @@
     return jnp.concatenate([jnp.where(low, x, zero), jnp.where(low, zero, x)], axis=0)
 
 
+def plain_block(q, k, v):
+    e = jnp.exp(nt_dot(q, k))
+    rinv = 1.0 / jnp.sum(e, axis=-1, keepdims=True)
+    e = e.astype(BF)
+    return e, nn(e, v) * rinv, rinv
+
+
 def softmax_block(q, k, v):
     s = nt_dot(q, k)
     m = jnp.max(s, axis=-1, keepdims=True)
@@ -263,9 +275,9 @@
     shape = jax.ShapeDtypeStruct
     return pl.pallas_call(
         attn5_fwd_kernel,
-        grid=(4,),
+        grid=(2,),
         in_specs=[full(x.shape)],
-        out_specs=[full((rows, 2 * HD))] * 3 + [pl.BlockSpec((toks // 4, toks), lambda j: (j, 0))],
+        out_specs=[full((rows, 2 * HD))] * 3 + [pl.BlockSpec((toks // 2, toks), lambda j: (j, 0))],
         out_shape=(
             shape((rows, 2 * HD), F32),
             shape((rows, 2 * HD), F32),
@@ -329,133 +341,137 @@
     )(x, ga, o, r, e)
 
 
-def kv_kernel(count, first_v, *refs):
-    xs, (w_ref, vec_ref, kv_ref) = refs[:count], refs[count:]
-    rows = xs[0].shape[0]
-    shift = jnp.where(pl.program_id(0) >= first_v, row_of(vec_ref, BIAS_V), 0.0)
-    for c in range(count):
-        part = nn(xs[c][...], w_ref[...]) + shift
-        kv_ref[c * rows : (c + 1) * rows, :] = part.astype(BF)
-
-
-def kv_call(xs, w, vecs, weight):
-    rows, width = xs[0].shape
-    blk = width // 2
-    steps = width // blk
-    return pl.pallas_call(
-        functools.partial(kv_kernel, len(xs), steps),
-        grid=(2 * steps,),
-        in_specs=[full((rows, width))] * len(xs)
-        + [
-            pl.BlockSpec((width, blk), lambda j: (0, steps + j)),
-            pl.BlockSpec((8, blk), lambda j: (0, j % steps)),
-        ],
-        out_specs=pl.BlockSpec((len(xs) * rows, blk), lambda j: (0, j)),
-        out_shape=jax.ShapeDtypeStruct((len(xs) * rows, 2 * width), BF),
-        compiler_params=params(),
-        cost_estimate=cost(4 * len(xs) * rows * width * width, 6 << 20, weight),
-        name="kv",
-    )(*xs, w, vecs)
-
-
-def attn_fwd_kernel(x_ref, wq_ref, vec_ref, k0, k1, v0, v1, att_ref, o_ref, r_ref, q_ref, e_ref, kc, vc):
-    rows = x_ref.shape[0]
-    kc[0:rows, :] = k0[...]
-    kc[rows:, :] = k1[...]
-    vc[0:rows, :] = v0[...]
-    vc[rows:, :] = v1[...]
-    q = ((nn(x_ref[...], wq_ref[...]) + row_of(vec_ref, BIAS_Q)) * (HD**-0.5)).astype(BF)
+def attn_fwd_kernel(nt, *refs):
+    ns, (wq, wk, wv, vec_ref, att_ref, o_ref, r_ref, q_ref, kv_ref, e_ref, x_all, w_kv, qs, os, rs) = refs[:nt], refs[nt:]
+    rows = ns[0].shape[0]
+
+    @pl.when(pl.program_id(0) == 0)
+    def _():
+        for c in range(nt):
+            x_all[c * rows : (c + 1) * rows, :] = ns[c][...]
+
+    lanes = 2 * HD
+    w_kv[:, 0:lanes] = wk[...]
+    w_kv[:, lanes:] = wv[...]
+    kv = nn(x_all[...], w_kv[...])
+    kv_ref[0] = kv[:, 0:lanes].astype(BF)
+    kv_ref[1] = (kv[:, lanes:] + row_of(vec_ref, BIAS_V)).astype(BF)
+    q = ((nn(x_all[0:rows, :], wq[...]) + row_of(vec_ref, BIAS_Q)) * (HD**-0.5)).astype(BF)
     q_ref[...] = q
     low = low_lanes(rows)
-    zero = jnp.zeros_like(q)
-    k, v = kc[...], vc[...]
-    e0, o0, r0 = softmax_block(jnp.where(low, q, zero), k, v)
-    e_ref[0] = e0
-    e1, o1, r1 = softmax_block(jnp.where(low, zero, q), k, v)
-    e_ref[1] = e1
-    o = jnp.where(low, o0, o1)
-    o_ref[...] = o
-    att_ref[...] = o.astype(BF)
-    r_ref[...] = jnp.where(
-        low, jnp.broadcast_to(r0, (rows, 2 * HD)), jnp.broadcast_to(r1, (rows, 2 * HD))
-    )
-
-
-def kv_specs(kv0, kv1, pairs):
-    one = lambda x, at: pl.BlockSpec((x.shape[0], 2 * HD), lambda j, at=at: (0, j + at))
-    return [one(kv0, 0), one(kv1, 0), one(kv0, pairs), one(kv1, pairs)]
-
-
-def attn_fwd_call(x, w, vecs, kv0, kv1):
-    rows, width = x.shape
-    toks = rows + kv1.shape[0]
+    weight = jnp.abs(q.astype(F32)) * jnp.max(jnp.abs(kv_ref[0].astype(F32)), axis=0, keepdims=True)
+    left = jnp.sum(jnp.where(low, weight, 0.0), axis=-1, keepdims=True)
+    right = jnp.sum(jnp.where(low, 0.0, weight), axis=-1, keepdims=True)
+    small = jnp.max(jnp.maximum(left, right)) < SAFE
+
+    def put(o, r0, r1):
+        o_ref[...] = o
+        att_ref[...] = o.astype(BF)
+        r_ref[...] = jnp.where(
+            low, jnp.broadcast_to(r0, (rows, lanes)), jnp.broadcast_to(r1, (rows, lanes))
+        )
+
+    @pl.when(small)
+    def _():
+        zero = jnp.zeros_like(q)
+        k, v = kv_ref[0], kv_ref[1]
+        e0, o0, r0 = plain_block(jnp.where(low, q, zero), k, v)
+        e_ref[0] = e0
+        e1, o1, r1 = plain_block(jnp.where(low, zero, q), k, v)
+        e_ref[1] = e1
+        put(jnp.where(low, o0, o1), r0, r1)
+
+    @pl.when(jnp.logical_not(small))
+    def _():
+        qs[...] = stack_heads(q)
+        part = 32
+
+        def body(i, carry):
+            at = pl.ds(pl.multiple_of(i * part, part), part)
+            e, o, rinv = softmax_block(qs[at, :], kv_ref[0], kv_ref[1])
+            side = i // (rows // part)
+            e_ref[side, pl.ds(pl.multiple_of((i - side * (rows // part)) * part, part), part), :] = e
+            os[at, :] = o
+            rs[at, :] = rinv
+            return carry
+
+        lax.fori_loop(0, 2 * rows // part, body, 0)
+        put(jnp.where(low, os[0:rows, :], os[rows:, :]), rs[0:rows, :], rs[rows:, :])
+
+
+def attn_fwd_call(ns, w, vecs):
+    rows, width = ns[0].shape
+    nt = len(ns)
+    toks = nt * rows
     blk = 2 * HD
     pairs = width // blk
     row = pl.BlockSpec((rows, blk), lambda j: (0, j))
     shape = jax.ShapeDtypeStruct
     return pl.pallas_call(
-        attn_fwd_kernel,
+        functools.partial(attn_fwd_kernel, nt),
         grid=(pairs,),
-        in_specs=[full(x.shape), pl.BlockSpec((width, blk), lambda j: (0, j))]
-        + [pl.BlockSpec((8, blk), lambda j: (0, j))]
-        + kv_specs(kv0, kv1, pairs),
-        out_specs=[row] * 4 + [pl.BlockSpec((2, rows, toks), lambda j: (j, 0, 0))],
+        in_specs=[full((rows, width))] * nt
+        + [pl.BlockSpec((width, blk), lambda j, p=p: (0, p * pairs + j)) for p in range(3)]
+        + [pl.BlockSpec((8, blk), lambda j: (0, j))],
+        out_specs=[row] * 4
+        + [pl.BlockSpec((2, toks, blk), lambda j: (0, 0, j))]
+        + [pl.BlockSpec((2, rows, toks), lambda j: (j, 0, 0))],
         out_shape=(
             shape((rows, width), BF),
             shape((rows, width), F32),
             shape((rows, width), F32),
             shape((rows, width), BF),
+            shape((2, toks, width), BF),
             shape((width // HD, rows, toks), BF),
         ),
-        scratch_shapes=[pltpu.VMEM((toks, blk), BF)] * 2,
+        scratch_shapes=[
+            pltpu.VMEM((toks, width), BF),
+            pltpu.VMEM((width, 2 * blk), BF),
+            pltpu.VMEM((2 * rows, blk), BF),
+            pltpu.VMEM((2 * rows, blk), F32),
+            pltpu.VMEM((2 * rows, 1), F32),
+        ],
         compiler_params=params(),
         cost_estimate=cost(16 * rows * toks * width, 20 << 20, 0.01),
         name="attn_fwd",
-    )(x, w, vecs, kv0, kv1, kv0, kv1)
-
-
-def attn_bwd_kernel(ga_ref, q_ref, k0, k1, v0, v1, o_ref, r_ref, e_ref, gq_ref, gkv_ref, kc, vc):
+    )(*ns, w, w, w, vecs)
+
+
+def attn_bwd_kernel(ga_ref, q_ref, kv_ref, o_ref, r_ref, e_ref, gq_ref, gkv_ref):
     rows = q_ref.shape[0]
-    kc[0:rows, :] = k0[...]
-    kc[rows:, :] = k1[...]
-    vc[0:rows, :] = v0[...]
-    vc[rows:, :] = v1[...]
     low = low_lanes(rows)
     stack = stack_heads
     g = ga_ref[...].astype(F32) * r_ref[...]
     inner = jnp.sum(stack(g * o_ref[...]), axis=-1, keepdims=True)
     gs, qs = stack(g.astype(BF)), stack(q_ref[...])
     e = e_ref[...].reshape(2 * rows, e_ref.shape[2])
-    dp = nt_dot(gs, vc[...])
+    dp = nt_dot(gs, kv_ref[1])
     ds = (e.astype(F32) * (dp - inner)).astype(BF)
-    dq = nn(ds, kc[...])
+    dq = nn(ds, kv_ref[0])
     gq_ref[...] = (jnp.where(low, dq[:rows], dq[rows:]) * (HD**-0.5)).astype(BF)
     gkv_ref[0] = tn_dot(ds, qs).astype(BF)
     gkv_ref[1] = tn_dot(e, gs).astype(BF)
 
 
-def attn_bwd_call(ga, q, kv0, kv1, o, r, e):
+def attn_bwd_call(ga, q, kv, o, r, e):
     rows, width = q.shape
     toks = e.shape[2]
     blk = 2 * HD
-    steps = width // blk
     row = pl.BlockSpec((rows, blk), lambda j: (0, j))
+    both = pl.BlockSpec((2, toks, blk), lambda j: (0, 0, j))
     return pl.pallas_call(
         attn_bwd_kernel,
-        grid=(steps,),
-        in_specs=[row, row]
-        + kv_specs(kv0, kv1, steps)
-        + [row, row, pl.BlockSpec((2, rows, toks), lambda j: (j, 0, 0))],
-        out_specs=[row, pl.BlockSpec((2, toks, blk), lambda j: (0, 0, j))],
+        grid=(width // blk,),
+        in_specs=[row, row, both, row, row, pl.BlockSpec((2, rows, toks), lambda j: (j, 0, 0))],
+        out_specs=[row, both],
         out_shape=[
-            jax.ShapeDtypeStruct((rows, steps * blk), BF),
-            jax.ShapeDtypeStruct((2, toks, steps * blk), BF),
+            jax.ShapeDtypeStruct((rows, width), BF),
+            jax.ShapeDtypeStruct((2, toks, width), BF),
         ],
-        scratch_shapes=[pltpu.VMEM((toks, blk), BF)] * 2,
         compiler_params=params(),
-        cost_estimate=cost(32 * rows * toks * blk * steps, steps * (4 << 20)),
+        cost_estimate=cost(32 * rows * toks * width, 24 << 20),
         name="attn_bwd",
-    )(ga, q, kv0, kv1, kv0, kv1, o, r, e)
+    )(ga, q, kv, o, r, e)
 
 
 def put_pieces(me_ref, src, keep_ref, send_ref, index):
@@ -981,10 +997,10 @@
 
 
 def last_sum_kernel(nf, places, first_vec, per, *refs):
-    parts, outs = refs[:nf], refs[nf:]
-    if len(parts[0].shape) == 3:
-        parts = [parts[0].at[i] for i in range(parts[0].shape[0])]
-    for at, rows, out, col in places:
+    parts, stacked, outs = refs[:nf], refs[nf], refs[nf + 1 :]
+    for at, rows, out, col, source in places:
+        if source:
+            parts = [stacked.at[i] for i in range(stacked.shape[0])]
         lanes = parts[0].shape[1]
         total = parts[0][at : at + rows, :].astype(F32)
         for part in parts[1:]:
@@ -997,7 +1013,7 @@
             outs[out][:, col : col + lanes] = total
 
 
-def last_sum(parts, places, shapes, first_vec=None, per=None):
+def last_sum(parts, stacked, places, shapes, first_vec, per):
     nf = len(parts)
     return pl.pallas_call(
         functools.partial(last_sum_kernel, nf, places, first_vec, per),
@@ -1005,7 +1021,7 @@
         compiler_params=pltpu.CompilerParams(vmem_limit_bytes=VMEM_LIMIT),
         cost_estimate=cost(nf * parts[0].size, 2 * nf * parts[0].size, 1),
         name="last_sum",
-    )(*parts)
+    )(*parts, stacked)
 
 
 def swap_cores(x):
@@ -1054,23 +1070,23 @@
     fast = ng == 2 and per % 8 == 0 and ff // nf == width
     me = jnp.stack([lax.axis_index(a) for a in ALL]).astype(jnp.int32)
     both = ("freq", "tm")
-    *picked, vecs = pick_call(
+    got = pick_call(
         nf,
         me,
         inputs,
+        cotangent,
         (gain_one, shift_one, bias_query, bias_value, bias_out, gain_two, shift_two, bias_down, bias_up),
     )
+    picked, vecs, cs = got[:nf], got[nf], got[nf + 1 :]
     xs = exchange("freq", picked)
     n5, pack5 = q5_call(nf, nt, tie(inputs, picked[0]), vecs, w_qkv)
     got5 = over(both, pack5).reshape(-1, 6 * HD)
     nm = ln_call(tie(xs, pack5), vecs)
     ns = exchange("tm", [nm] * nt)
-    kv0 = kv_call([nm], w_qkv, vecs, 100)
-    o5, r5, ob5, e5 = attn5_fwd_call(tie(got5, kv0))
+    o5, r5, ob5, e5 = attn5_fwd_call(got5)
     att5 = over(both, ob5.reshape(nf * nt, r // 2, 2 * HD))
-    cs = exchange("freq", tie(pick_call(nf, me, tie(cotangent, pack5)), nm))
-    kv1 = kv_call(tie(ns[1:], ob5), w_qkv, vecs, 0.01)
-    att, o, rr, q, e = attn_fwd_call(nm, w_qkv, vecs, kv0, kv1)
+    cs = exchange("freq", tie(cs, ob5))
+    att, o, rr, q, kv, e = attn_fwd_call(tie(ns, ob5), w_qkv, vecs)
     outs, out5, gm, ga, ga5, *dws, vec, gbu = mid_call(
         nf,
         nt,
@@ -1098,7 +1114,7 @@
         )
         keep_o, got_o = pieces(dws[1]), pieces(swap_cores(dws[2]))
     got_ga5 = over(both, ga5).reshape(-1, 2 * HD)
-    gq, gkv = attn_bwd_call(ga, q, kv0, kv1, o, rr, e)
+    gq, gkv = attn_bwd_call(ga, q, kv, o, rr, e)
     g5 = attn5_bwd_call(got5, tie(got_ga5, gq, *([got_o] if fast else [])), o5, r5, e5).reshape(nf * nt, r // 2, 6 * HD)
     *dxs, vec_m = dx_call(tie(gq, g5), gkv, ns, w_qkv)
     dxs = exchange("tm", dxs)
@@ -1120,12 +1136,11 @@
         rdq, ruq = along("tm", 2, sdq), along("tm", 1, suq)
         dff = over("freq", tie(dff, dxq).reshape(nf, -1, width))
         sums_q = exchange("freq", tm_sum(nf, me, d0q, gxq, rdq, u0q, gyq, ruq))
-        places = [(0, pd, 0, 0)] + [(pd + i * per, per, 1, i * width) for i in range(nf)]
-        dwd, dwu = last_sum([dff], places, [(pd, width), (per, ff)])
-        places = [(0, per, 0, 0), (per, 8, None, 0), (per + 8, per, 0, width)]
-        places += [(2 * per + 8, per, 0, 2 * width), (3 * per + 8, per, 1, 0)]
-        shapes = [(per, 3 * width), (per, width)] + [(per,)] * 8 + [(pd,)]
-        dwqkv, dwo, *small, gbu = last_sum(sums_q, places, shapes, 2, per)
+        places = [(0, per, 0, 0, 0), (per, 8, None, 0, 0), (per + 8, per, 0, width, 0)]
+        places += [(2 * per + 8, per, 0, 2 * width, 0), (3 * per + 8, per, 1, 0, 0)]
+        places += [(0, pd, 2, 0, 1)] + [(pd + i * per, per, 3, i * width, 1) for i in range(nf)]
+        shapes = [(per, 3 * width), (per, width), (pd, width), (per, ff)] + [(per,)] * 8 + [(pd,)]
+        dwqkv, dwo, dwd, dwu, *small, gbu = last_sum(sums_q, dff, places, shapes, 4, per)
         piece = lambda i: small[i]
     else:
         dwd, dwu, dwo, dwqkv = (

time: 275 us -> 264 us (0.960)
  Pallas kernels: 136 us -> 123 us
  waiting for transfers between devices: 43.5 us -> 48.8 us
    pallas_call x5 -> x3, Pallas kernels: 49.8 us -> 40.4 us  [the longest x1 17.2 us: attn_fwd_call(): pl.pallas_call(functools.partial(attn_fwd_kernel, nt), grid=(pairs,), in_...]
    all_to_all x6, waiting for transfers between devices: 3 us -> 7.57 us  [over(): return lax.all_to_all(x, axes, 0, 0)]
    unnamed x72 -> x78, local copies, waits for them, and re-layouts: 12.8 us -> 11.5 us
  transfers between devices with their start and end apart: 33 -> 33, of which waited for: 9 -> 10; matrix products, arithmetic and copies ran while one was open for 0% -> 0% of each run, Pallas kernels for 40% -> 36%
where the time goes in v4:
time: 264 us; the launch traced here: 263 us
  Pallas kernels  123 us (47%)
  starting transfers between devices  63.6 us (24%)
  waiting for transfers between devices  48.8 us (18%)
  between operations  14.4 us (5%)
  local copies, waits for them, and re-layouts  11.5 us (4%)
    all_to_all x6, starting transfers between devices, over(): return lax.all_to_all(x, axes, 0, 0)  33.6 us
    ppermute x18, starting transfers between devices, exchange(): lax.ppermute(parts[k], axis, pairs(k))  25.9 us
    ppermute x18, waiting for transfers between devices, exchange(): lax.ppermute(parts[k], axis, pairs(k))  23 us
    pallas_call x1, Pallas kernels, mid_call(): pl.pallas_call(functools.partial(mid_kernel, nf, nt, fast), grid_spec=plt...  22.9 us
    ppermute x4, waiting for transfers between devices, along(): return lax.ppermute(x, axis, [(i, i ^ k) for i in range(4)])  18.3 us
    pallas_call x1, Pallas kernels, attn_fwd_call(): pl.pallas_call(functools.partial(attn_fwd_kernel, nt), grid=(pairs,), in_...  17.2 us
    pallas_call x1, Pallas kernels, attn_bwd_call(): pl.pallas_call(attn_bwd_kernel, grid=(width // blk,), in_specs=[row, row,...  15.7 us
    pallas_call x1, Pallas kernels, tail5_call(): pl.pallas_call(functools.partial(tail5_kernel, nf, nt, fast), grid_spec=p...  13.5 us
  transfers between devices with their start and end apart: 33, of which 10 were waited for; matrix products, arithmetic and copies ran while one was open for 0% of the time, Pallas kernels for 36%

profile of v4, /device:TPU:0, one launch (start us, length us, event | category | flops | bytes accessed | tf_op | source)
XLA Modules:
  0.0 263.2 jit_solution(2946089357355612228)
XLA Ops:
  7.8 3.0 %pick.1 = (bf16[80,768]{1,0:T(8,128)(2,1)}, bf16[80,768]{1,0:T(8,128)(2,1)}, bf16[80,768]{1,0:T(8,128)(2,1)}, bf16[80,768]{1,0:T(8,128)(2,1)}, f32[16,768]{1,0:T...) custom-call(s32[3]{0:T(128)} %pad_add_fusion.me_ref.refs_0_, ...), custom_call_target="tpu_custom_call" | custom-call | bytes 2457600 | tf_op jit(solution)/shard_map/pick/pallas_call | solution.py:107
  10.8 3.0 %collective-permute-start = (bf16[80,768]{1,0:T(8,128)(2,1)}, bf16[80,768]{1,0:T(8,128)(2,1)S(1)}, u32[]{:S(2)}, u32[]{:S(2)}) collective-permute-start(bf16[80,768]{1,0:T(8,128)(2,1)} %get-tuple-element.113), channel_id=1, source_target_pairs={{0,8},{8,0},{16,24},{24,16},{1,9},{9,1},{17,25},{25,17},{2,10},{10... | collective-permute-start | bytes 368648 | tf_op jit(solution)/shard_map/ppermute | solution.py:1033
  13.8 2.6 collective-permute-start.1
  16.4 3.9 %q_shared.1 = (bf16[80,768]{1,0:T(8,128)(2,1)}, bf16[16,40,384]{2,1,0:T(8,128)(2,1)}) custom-call(bf16[5,80,768]{2,1,0:T(8,128)(2,1)} %refs_9_.1, f32[16,768]{1,0:T(8,128)} %get-tuple-element.121.vec_ref.refs_4_.refs_7_.refs_13_.refs_9_.refs_12_, bf16[768,2304]{1,0:T(8,128)(2,1)} %refs_11_.3), custom_call_target="tpu_custom_call" | custom-call | flops 283115520 | bytes 3538944 | tf_op jit(solution)/shard_map/q_shared/pallas_call | solution.py:198
  20.3 7.1 %all-to-all-start = ((bf16[16,40,384]{2,1,0:T(8,128)(2,1)}), bf16[16,40,384]{2,1,0:T(8,128)(2,1)S(1)}, u32[]{:S(2)}, u32[]{:S(2)}) async-start(bf16[16,40,384]{2,1,0:T(8,128)(2,1)} %get-tuple-element.122), calls=%async_computation | async-start | bytes 983040 | tf_op jit(solution)/shard_map/all_to_all | solution.py:1043
  28.8 2.2 ln_one.1.refs_0_.n0.refs_3_
  31.0 2.8 %collective-permute-start.8 = (bf16[320,768]{1,0:T(8,128)(2,1)}, bf16[320,768]{1,0:T(8,128)(2,1)S(1)}, u32[]{:S(2)}, u32[]{:S(2)}) collective-permute-start(bf16[320,768]{1,0:T(8,128)(2,1)} %ln_one.1.refs_0_.n0.refs_3_), channel_id=1, source_target_pairs={{0,6},{2,4},{4,2},{6,0},{1,7},{3,5},{5,3},{7,1},{8,14},{10,12},{12... | collective-permute-start | bytes 1474568 | tf_op jit(solution)/shard_map/ppermute | solution.py:1033
  34.5 6.8 %all-to-all-done = bf16[16,40,384]{2,1,0:T(8,128)(2,1)S(1)} async-done(((bf16[16,40,384]{2,1,0:T(8,128)(2,1)}), bf16[16,40,384]{2,1,0:T(8,128)(2,1)S(1)}, u32[]{:S(2)}, u32[]{:S(2)}) %all-to-all-start) | async-done | bytes 491552 | tf_op jit(solution)/shard_map/all_to_all | solution.py:1043
  42.1 7.5 %attn_shared_fwd.1 = (f32[640,128]{1,0:T(8,128)}, f32[640,128]{1,0:T(8,128)}, bf16[640,128]{1,0:T(8,128)(2,1)}, bf16[1280,1280]{1,0:T(8,128)(2,1)}) custom-call(bf16[640,384]{1,0:T(8,128)(2,1)} %bitcast.12), custom_call_target="tpu_custom_call" | custom-call | flops 3355443200 | bytes 3276800 | tf_op jit(solution)/shard_map/attn_shared_fwd/pallas_call | solution.py:276
  49.6 3.6 %all-to-all-start.1 = ((bf16[16,40,128]{2,1,0:T(8,128)(2,1)}), bf16[16,40,128]{2,1,0:T(8,128)(2,1)S(1)}, u32[]{:S(2)}, u32[]{:S(2)}) async-start(bf16[16,40,128]{2,1,0:T(8,128)(2,1)} %bitcast.16), calls=%async_computation.1 | async-start | bytes 327680 | tf_op jit(solution)/shard_map/all_to_all | solution.py:1043
  55.4 2.4 collective-permute-start.4
  59.6 17.2 %attn_fwd.1 = (bf16[320,768]{1,0:T(8,128)(2,1)}, f32[320,768]{1,0:T(8,128)}, f32[320,768]{1,0:T(8,128)}, bf16[320,768]{1,0:T(8,128)(2,1)}, bf16[2,1280,768]{2,1,...) custom-call(bf16[320,768]{1,0:T(8,128)(2,1)} %ln_one.1.refs_0_.n0.refs_3_, bf16[320,768]{1,0:T(8,128)(2,1)} %copy-done.9, ...), custom_call_target="tpu_custom_call" | custom-call | flops 50331648 | bytes 209715 | tf_op jit(solution)/shard_map/attn_fwd/pallas_call | solution.py:410
  77.6 22.9 %mid.1 = (bf16[4,80,768]{2,1,0:T(8,128)(2,1)}, f32[80,768]{1,0:T(8,128)}, f32[400,768]{1,0:T(8,128)}, bf16[320,768]{1,0:T(8,128)(2,1)}, bf16[16,40,128]{2,1,0:T(...) custom-call(s32[3]{0:T(128)} %pad_add_fusion.me_ref.refs_0_, ...), custom_call_target="tpu_custom_call" | custom-call | flops 12740198400 | bytes 25165824 | tf_op jit(solution)/shard_map/mid/pallas_call | solution.py:687
  100.6 7.0 %all-to-all-start.2 = ((bf16[16,40,128]{2,1,0:T(8,128)(2,1)}), bf16[16,40,128]{2,1,0:T(8,128)(2,1)S(1)}, u32[]{:S(2)}, u32[]{:S(2)}) async-start(bf16[16,40,128]{2,1,0:T(8,128)(2,1)} %get-tuple-element.138), calls=%async_computation.2 | async-start | bytes 327680 | tf_op jit(solution)/shard_map/all_to_all | solution.py:1043
  107.7 15.7 %attn_bwd.1 = (bf16[320,768]{1,0:T(8,128)(2,1)}, bf16[2,1280,768]{2,1,0:T(8,128)(2,1)}) custom-call(bf16[320,768]{1,0:T(8,128)(2,1)} %get-tuple-element.139.ga_ref, bf16[320,768]{1,0:T(8,128)(2,1)} %get-tuple-element.140.q_ref, bf16[2,1280,768]{2,1,0:T(8,128)(2,1)} %get-tuple-element.141.kv_ref, f32[320,768]{1,0:T(8,128)} %get-tuple-element.142.o_ref, ...), custom_call_target="tpu_custom_call" | custom-call | flops 10066329600 | bytes 25165824 | tf_op jit(solution)/shard_map/attn_bwd/pallas_call | solution.py:462
  124.1 8.0 %attn_shared_bwd.1 = bf16[640,384]{1,0:T(8,128)(2,1)} custom-call(bf16[640,384]{1,0:T(8,128)(2,1)} %bitcast.13, bf16[640,128]{1,0:T(8,128)(2,1)} %bitcast.17, f32[640,128]{1,0:T(8,128)} %get-tuple-element.148.o_ref, f32[640,128]{1,0:T(8,128)} %get-tuple-element.149.r_ref, bf16[1280,1280]{1,0:T(8,128)(2,1)} %get-tuple-element.150.e_ref), custom_call_target="tpu_custom_call" | custom-call | flops 6710886400 | bytes 3276800 | tf_op jit(solution)/shard_map/attn_shared_bwd/pallas_call | solution.py:328
  132.1 6.9 %all-to-all-start.3 = ((bf16[16,40,384]{2,1,0:T(8,128)(2,1)}), bf16[16,40,384]{2,1,0:T(8,128)(2,1)S(1)}, u32[]{:S(2)}, u32[]{:S(2)}) async-start(bf16[16,40,384]{2,1,0:T(8,128)(2,1)} %bitcast.14), calls=%async_computation.3 | async-start | bytes 983040 | tf_op jit(solution)/shard_map/all_to_all | solution.py:1043
  139.0 10.7 %dx.1 = (f32[320,768]{1,0:T(8,128)}, bf16[320,768]{1,0:T(8,128)(2,1)}, bf16[320,768]{1,0:T(8,128)(2,1)}, bf16[320,768]{1,0:T(8,128)(2,1)}, f32[2,768]{1,0:T(2,128)}) custom-call(bf16[320,768]{1,0:T(8,128)(2,1)} %get-tuple-element.169.gq_ref.refs_1_, bf16[2,1280,768]{2,1,0:T(8,128)(2,1)} %get-tuple-element.154.gkv_ref.refs_2_, ...), custom_call_target="tpu_custom_call" | custom-call | flops 3019898880 | bytes 12582912 | tf_op jit(solution)/shard_map/dx/pallas_call | solution.py:531
  154.7 13.5 %tail_shared.1 = (bf16[4,4,32,768]{3,2,1,0:T(8,128)(2,1)}, bf16[4,4,32,768]{3,2,1,0:T(8,128)(2,1)}, bf16[4,4,24,768]{3,2,1,0:T(8,128)(2,1)}, bf16[4,4,24,768]{3,...) custom-call(s32[3]{0:T(128)} %pad_add_fusion.me_ref.refs_0_, ...), custom_call_target="tpu_custom_call" | custom-call | flops 3586129920 | bytes 16777216 | tf_op jit(solution)/shard_map/tail_shared/pallas_call | solution.py:830
  168.2 4.3 %all-to-all-start.4 = ((bf16[4,80,768]{2,1,0:T(8,128)(2,1)}), bf16[4,80,768]{2,1,0:T(8,128)(2,1)S(1)}, u32[]{:S(2)}, u32[]{:S(2)}) async-start(bf16[4,80,768]{2,1,0:T(8,128)(2,1)} %get-tuple-element.151), calls=%async_computation.4 | async-start | bytes 983040 | tf_op jit(solution)/shard_map/all_to_all | solution.py:1043
  172.5 14.6 %collective-permute-done.12.refs_3_ = bf16[320,768]{1,0:T(8,128)(2,1)S(1)} collective-permute-done((bf16[320,768]{1,0:T(8,128)(2,1)}, bf16[320,768]{1,0:T(8,128)(2,1)S(1)}, u32[]{:S(2)}, u32[]{:S(2)}) %collective-permute-start.12) | collective-permute-done | bytes 491552 | tf_op jit(solution)/shard_map/ppermute | solution.py:1033
  188.4 3.6 %tail.1 = (bf16[80,768]{1,0:T(8,128)(2,1)}, bf16[80,768]{1,0:T(8,128)(2,1)}, bf16[80,768]{1,0:T(8,128)(2,1)}, bf16[80,768]{1,0:T(8,128)(2,1)}) custom-call(f32[320,768]{1,0:T(8,128)} %get-tuple-element.159.refs_0_, bf16[320,768]{1,0:T(8,128)(2,1)} %copy-done.24, bf16[320,768]{1,0:T(8,128)(2,1)} %copy-done.25, bf16[320,768]{1,0:T(8,128)(2,1)} %copy-done.26, ...), custom_call_target="tpu_custom_call" | custom-call | flops 7372800000 | bytes 6291456000 | tf_op jit(solution)/shard_map/tail/pallas_call | solution.py:878
  193.3 3.9 %pair_sum.1 = (bf16[2,2,104,768]{3,2,1,0:T(8,128)(2,1)}, bf16[2,104,768]{2,1,0:T(8,128)(2,1)}, bf16[2,104,768]{2,1,0:T(8,128)(2,1)}, bf16[2,2,104,768]{3,2,1,0:T...) custom-call(bf16[4,4,32,768]{3,2,1,0:T(8,128)(2,1)} %get-tuple-element.174.refs_0_.refs_8_, ...), custom_call_target="tpu_custom_call" | custom-call | flops 1048576 | bytes 8388608 | tf_op jit(solution)/shard_map/pair_sum/pallas_call | solution.py:919
  197.3 4.7 %all-to-all-start.5 = ((bf16[4,192,768]{2,1,0:T(8,128)(2,1)}), bf16[4,192,768]{2,1,0:T(8,128)(2,1)S(1)}, u32[]{:S(2)}, u32[]{:S(2)}) async-start(bf16[4,192,768]{2,1,0:T(8,128)(2,1)} %bitcast.11), calls=%async_computation.6 | async-start | bytes 2359296 | tf_op jit(solution)/shard_map/all_to_all | solution.py:1043
  203.2 15.1 %collective-permute-done.20.gy.refs_4_ = bf16[2,2,104,768]{3,2,1,0:T(8,128)(2,1)S(1)} collective-permute-done((bf16[2,2,104,768]{3,2,1,0:T(8,128)(2,1)}, bf16[2,2,104,768]{3,2,1,0:T(8,128)(2,1)S(1)}, u32[]{:S(2)}, u32[]{:S(2)}) %collective-permute-start.20) | collective-permute-done | bytes 639008 | tf_op jit(solution)/shard_map/ppermute | solution.py:956
  225.4 2.4 collective-permute-start.14
  231.7 3.3 %tm_sum.1 = (bf16[104,768]{1,0:T(8,128)(2,1)}, bf16[104,768]{1,0:T(8,128)(2,1)}, bf16[104,768]{1,0:T(8,128)(2,1)}, bf16[104,768]{1,0:T(8,128)(2,1)}) custom-call(s32[3]{0:T(128)} %pad_add_fusion.me_ref.refs_0_, bf16[2,104,768]{2,1,0:T(8,128)(2,1)} %get-tuple-element.182.refs_0_, bf16[2,2,104,768]{3,2,1,0:T(8,128)(2,1)} %copy-done.3, ...), custom_call_target="tpu_custom_call" | custom-call | flops 1048576 | bytes 5242880 | tf_op jit(solution)/shard_map/tm_sum/pallas_call | solution.py:983
  236.4 2.4 collective-permute-start.24
  239.4 3.8 %collective-permute-done.14.refs_2_ = bf16[80,768]{1,0:T(8,128)(2,1)S(1)} collective-permute-done((bf16[80,768]{1,0:T(8,128)(2,1)S(1)}, bf16[80,768]{1,0:T(8,128)(2,1)S(1)}, u32[]{:S(2)}, u32[]{:S(2)}) %collective-permute-start.14) | collective-permute-done | bytes 122912 | tf_op jit(solution)/shard_map/ppermute | solution.py:1033
  243.9 3.0 %assemble.1 = f32[5,80,768]{2,1,0:T(8,128)} custom-call(s32[3]{0:T(128)} %pad_add_fusion.me_ref.refs_0_, bf16[80,768]{1,0:T(8,128)(2,1)} %get-tuple-element.164.refs_0_, bf16[80,768]{1,0:T(8,128)(2,1)} %copy-done.20, bf16[80,768]{1,0:T(8,128)(2,1)} %copy-done.21, bf16[80,768]{1,0:T(8,128)(2,1)} %copy-done.22, f32[80,768]{1,0:T(8,128)} %get-tuple-element.173.refs_4_), custom_call_target="tpu_custom_call" | custom-call | bytes 2457600 | tf_op jit(solution)/shard_map/assemble/pallas_call | solution.py:134
  248.9 3.7 %collective-permute-done.24.refs_2_ = bf16[104,768]{1,0:T(8,128)(2,1)S(1)} collective-permute-done((bf16[104,768]{1,0:T(8,128)(2,1)}, bf16[104,768]{1,0:T(8,128)(2,1)S(1)}, u32[]{:S(2)}, u32[]{:S(2)}) %collective-permute-start.24) | collective-permute-done | bytes 159776 | tf_op jit(solution)/shard_map/ppermute | solution.py:1033
  253.8 2.6 last_sum.1
  (132 shorter events, 34.6 us)
Async XLA Ops:
  10.8 16.6 %collective-permute-start = (bf16[80,768]{1,0:T(8,128)(2,1)}, bf16[80,768]{1,0:T(8,128)(2,1)S(1)}, u32[]{:S(2)}, u32[]{:S(2)}) collective-permute-start(bf16[80,768]{1,0:T(8,128)(2,1)} %get-tuple-element.113), channel_id=1, source_target_pairs={{0,8},{8,0},{16,24},{24,16},{1,9},{9,1},{17,25},{25,17},{2,10},{10... | collective-permute-start | bytes 368648 | tf_op jit(solution)/shard_map/ppermute | solution.py:1033
  13.8 13.6 %collective-permute-start.1 = (bf16[80,768]{1,0:T(8,128)(2,1)}, bf16[80,768]{1,0:T(8,128)(2,1)S(1)}, u32[]{:S(2)}, u32[]{:S(2)}) collective-permute-start(bf16[80,768]{1,0:T(8,128)(2,1)} %get-tuple-element.114), channel_id=1, source_target_pairs={{0,16},{8,24},{16,0},{24,8},{1,17},{9,25},{17,1},{25,9},{2,18},{10... | collective-permute-start | bytes 368648 | tf_op jit(solution)/shard_map/ppermute | solution.py:1033
  16.4 11.0 %collective-permute-start.2 = (bf16[80,768]{1,0:T(8,128)(2,1)}, bf16[80,768]{1,0:T(8,128)(2,1)S(1)}, u32[]{:S(2)}, u32[]{:S(2)}) collective-permute-start(bf16[80,768]{1,0:T(8,128)(2,1)} %get-tuple-element.115), channel_id=1, source_target_pairs={{0,24},{8,16},{16,8},{24,0},{1,25},{9,17},{17,9},{25,1},{2,26},{10... | collective-permute-start | bytes 368648 | tf_op jit(solution)/shard_map/ppermute | solution.py:1033
  20.3 21.0 %all-to-all-start = ((bf16[16,40,384]{2,1,0:T(8,128)(2,1)}), bf16[16,40,384]{2,1,0:T(8,128)(2,1)S(1)}, u32[]{:S(2)}, u32[]{:S(2)}) async-start(bf16[16,40,384]{2,1,0:T(8,128)(2,1)} %get-tuple-element.122), calls=%async_computation | async-start | bytes 983040 | tf_op jit(solution)/shard_map/all_to_all | solution.py:1043
  31.0 26.8 %collective-permute-start.8 = (bf16[320,768]{1,0:T(8,128)(2,1)}, bf16[320,768]{1,0:T(8,128)(2,1)S(1)}, u32[]{:S(2)}, u32[]{:S(2)}) collective-permute-start(bf16[320,768]{1,0:T(8,128)(2,1)} %ln_one.1.refs_0_.n0.refs_3_), channel_id=1, source_target_pairs={{0,6},{2,4},{4,2},{6,0},{1,7},{3,5},{5,3},{7,1},{8,14},{10,12},{12... | collective-permute-start | bytes 1474568 | tf_op jit(solution)/shard_map/ppermute | solution.py:1033
  33.9 24.1 %collective-permute-start.7 = (bf16[320,768]{1,0:T(8,128)(2,1)}, bf16[320,768]{1,0:T(8,128)(2,1)S(1)}, u32[]{:S(2)}, u32[]{:S(2)}) collective-permute-start(bf16[320,768]{1,0:T(8,128)(2,1)} %ln_one.1.refs_0_.n0.refs_3_), channel_id=1, source_target_pairs={{0,4},{2,6},{4,0},{6,2},{1,5},{3,7},{5,1},{7,3},{8,12},{10,14},{12... | collective-permute-start | bytes 1474568 | tf_op jit(solution)/shard_map/ppermute | solution.py:1033
  34.4 24.3 %collective-permute-start.6 = (bf16[320,768]{1,0:T(8,128)(2,1)}, bf16[320,768]{1,0:T(8,128)(2,1)S(1)}, u32[]{:S(2)}, u32[]{:S(2)}) collective-permute-start(bf16[320,768]{1,0:T(8,128)(2,1)} %ln_one.1.refs_0_.n0.refs_3_), channel_id=1, source_target_pairs={{0,2},{2,0},{4,6},{6,4},{1,3},{3,1},{5,7},{7,5},{8,10},{10,8},{12,... | collective-permute-start | bytes 1474568 | tf_op jit(solution)/shard_map/ppermute | solution.py:1033
  49.6 27.3 %all-to-all-start.1 = ((bf16[16,40,128]{2,1,0:T(8,128)(2,1)}), bf16[16,40,128]{2,1,0:T(8,128)(2,1)S(1)}, u32[]{:S(2)}, u32[]{:S(2)}) async-start(bf16[16,40,128]{2,1,0:T(8,128)(2,1)} %bitcast.16), calls=%async_computation.1 | async-start | bytes 327680 | tf_op jit(solution)/shard_map/all_to_all | solution.py:1043
  53.2 144.1 %reduce-scatter.2.cloned.1.call-start = ((), (), s32[]{:S(2)}) async-start(), calls=%async_computation.7 | async-start | bytes 10616832 | tf_op jit(solution)/shard_map/reduce_scatter | solution.py:1109
  53.5 23.4 %collective-permute-start.3 = (bf16[80,768]{1,0:T(8,128)(2,1)S(1)}, bf16[80,768]{1,0:T(8,128)(2,1)S(1)}, u32[]{:S(2)}, u32[]{:S(2)}) collective-permute-start(bf16[80,768]{1,0:T(8,128)(2,1)S(1)} %copy-done.35), channel_id=1, source_target_pairs={{0,8},{8,0},{16,24},{24,16},{1,9},{9,1},{17,25},{25,17},{2,10},{10... | collective-permute-start | bytes 368648 | tf_op jit(solution)/shard_map/ppermute | solution.py:1033
  55.4 21.4 %collective-permute-start.4 = (bf16[80,768]{1,0:T(8,128)(2,1)S(1)}, bf16[80,768]{1,0:T(8,128)(2,1)S(1)}, u32[]{:S(2)}, u32[]{:S(2)}) collective-permute-start(bf16[80,768]{1,0:T(8,128)(2,1)S(1)} %copy-done.34), channel_id=1, source_target_pairs={{0,16},{8,24},{16,0},{24,8},{1,17},{9,25},{17,1},{25,9},{2,18},{10... | collective-permute-start | bytes 368648 | tf_op jit(solution)/shard_map/ppermute | solution.py:1033
  57.8 19.0 %collective-permute-start.5 = (bf16[80,768]{1,0:T(8,128)(2,1)S(1)}, bf16[80,768]{1,0:T(8,128)(2,1)S(1)}, u32[]{:S(2)}, u32[]{:S(2)}) collective-permute-start(bf16[80,768]{1,0:T(8,128)(2,1)S(1)} %copy-done.33), channel_id=1, source_target_pairs={{0,24},{8,16},{16,8},{24,0},{1,25},{9,17},{17,9},{25,1},{2,26},{10... | collective-permute-start | bytes 368648 | tf_op jit(solution)/shard_map/ppermute | solution.py:1033
  100.6 22.8 %all-to-all-start.2 = ((bf16[16,40,128]{2,1,0:T(8,128)(2,1)}), bf16[16,40,128]{2,1,0:T(8,128)(2,1)S(1)}, u32[]{:S(2)}, u32[]{:S(2)}) async-start(bf16[16,40,128]{2,1,0:T(8,128)(2,1)} %get-tuple-element.138), calls=%async_computation.2 | async-start | bytes 327680 | tf_op jit(solution)/shard_map/all_to_all | solution.py:1043
  107.7 15.8 %collective-permute-start.9 = (bf16[4,4,24,768]{3,2,1,0:T(8,128)(2,1)S(1)}, bf16[4,4,24,768]{3,2,1,0:T(8,128)(2,1)S(1)}, u32[]{:S(2)}, u32[]{:S(2)}) collective-permute-start(bf16[4,4,24,768]{3,2,1,0:T(8,128)(2,1)S(1)} %copy-done.23), channel_id=1, source_target_pairs={{0,1},{1,0},{2,3},{3,2},{4,5},{5,4},{6,7},{7,6},{8,9},{9,8},{10,11... | collective-permute-start | bytes 1769480 | tf_op jit(solution)/shard_map/ppermute | solution.py:1028
  132.1 21.8 %all-to-all-start.3 = ((bf16[16,40,384]{2,1,0:T(8,128)(2,1)}), bf16[16,40,384]{2,1,0:T(8,128)(2,1)S(1)}, u32[]{:S(2)}, u32[]{:S(2)}) async-start(bf16[16,40,384]{2,1,0:T(8,128)(2,1)} %bitcast.14), calls=%async_computation.3 | async-start | bytes 983040 | tf_op jit(solution)/shard_map/all_to_all | solution.py:1043
  149.6 22.9 %collective-permute-start.10 = (bf16[320,768]{1,0:T(8,128)(2,1)}, bf16[320,768]{1,0:T(8,128)(2,1)S(1)}, u32[]{:S(2)}, u32[]{:S(2)}) collective-permute-start(bf16[320,768]{1,0:T(8,128)(2,1)} %get-tuple-element.156), channel_id=1, source_target_pairs={{0,2},{2,0},{4,6},{6,4},{1,3},{3,1},{5,7},{7,5},{8,10},{10,8},{12,... | collective-permute-start | bytes 1474568 | tf_op jit(solution)/shard_map/ppermute | solution.py:1033
  151.5 20.9 %collective-permute-start.11 = (bf16[320,768]{1,0:T(8,128)(2,1)}, bf16[320,768]{1,0:T(8,128)(2,1)S(1)}, u32[]{:S(2)}, u32[]{:S(2)}) collective-permute-start(bf16[320,768]{1,0:T(8,128)(2,1)} %get-tuple-element.157), channel_id=1, source_target_pairs={{0,4},{2,6},{4,0},{6,2},{1,5},{3,7},{5,1},{7,3},{8,12},{10,14},{12... | collective-permute-start | bytes 1474568 | tf_op jit(solution)/shard_map/ppermute | solution.py:1033
  153.0 34.1 %collective-permute-start.12 = (bf16[320,768]{1,0:T(8,128)(2,1)}, bf16[320,768]{1,0:T(8,128)(2,1)S(1)}, u32[]{:S(2)}, u32[]{:S(2)}) collective-permute-start(bf16[320,768]{1,0:T(8,128)(2,1)} %get-tuple-element.158), channel_id=1, source_target_pairs={{0,6},{2,4},{4,2},{6,0},{1,7},{3,5},{5,3},{7,1},{8,14},{10,12},{12... | collective-permute-start | bytes 1474568 | tf_op jit(solution)/shard_map/ppermute | solution.py:1033
  168.1 23.9 %collective-permute-start.16 = (bf16[4,4,32,768]{3,2,1,0:T(8,128)(2,1)}, bf16[4,4,32,768]{3,2,1,0:T(8,128)(2,1)S(1)}, u32[]{:S(2)}, u32[]{:S(2)}) collective-permute-start(bf16[4,4,32,768]{3,2,1,0:T(8,128)(2,1)} %get-tuple-element.175), channel_id=1, source_target_pairs={{0,1},{1,0},{2,3},{3,2},{4,5},{5,4},{6,7},{7,6},{8,9},{9,8},{10,11... | collective-permute-start | bytes 2359304 | tf_op jit(solution)/shard_map/ppermute | solution.py:1028
  168.2 29.1 %all-to-all-start.4 = ((bf16[4,80,768]{2,1,0:T(8,128)(2,1)}), bf16[4,80,768]{2,1,0:T(8,128)(2,1)S(1)}, u32[]{:S(2)}, u32[]{:S(2)}) async-start(bf16[4,80,768]{2,1,0:T(8,128)(2,1)} %get-tuple-element.151), calls=%async_computation.4 | async-start | bytes 983040 | tf_op jit(solution)/shard_map/all_to_all | solution.py:1043
  187.9 4.2 %collective-permute-start.18 = (bf16[4,4,24,768]{3,2,1,0:T(8,128)(2,1)}, bf16[4,4,24,768]{3,2,1,0:T(8,128)(2,1)S(1)}, u32[]{:S(2)}, u32[]{:S(2)}) collective-permute-start(bf16[4,4,24,768]{3,2,1,0:T(8,128)(2,1)} %get-tuple-element.180), channel_id=1, source_target_pairs={{0,1},{1,0},{2,3},{3,2},{4,5},{5,4},{6,7},{7,6},{8,9},{9,8},{10,11... | collective-permute-start | bytes 1769480 | tf_op jit(solution)/shard_map/ppermute | solution.py:1028
  197.3 55.4 %all-to-all-start.5 = ((bf16[4,192,768]{2,1,0:T(8,128)(2,1)}), bf16[4,192,768]{2,1,0:T(8,128)(2,1)S(1)}, u32[]{:S(2)}, u32[]{:S(2)}) async-start(bf16[4,192,768]{2,1,0:T(8,128)(2,1)} %bitcast.11), calls=%async_computation.6 | async-start | bytes 2359296 | tf_op jit(solution)/shard_map/all_to_all | solution.py:1043
  202.1 16.3 %collective-permute-start.20 = (bf16[2,2,104,768]{3,2,1,0:T(8,128)(2,1)}, bf16[2,2,104,768]{3,2,1,0:T(8,128)(2,1)S(1)}, u32[]{:S(2)}, u32[]{:S(2)}) collective-permute-start(bf16[2,2,104,768]{3,2,1,0:T(8,128)(2,1)} %get-tuple-element.186), channel_id=1, source_target_pairs={{0,4},{2,6},{4,0},{6,2},{1,5},{3,7},{5,1},{7,3},{8,12},{10,14},{12... | collective-permute-start | bytes 1916936 | tf_op jit(solution)/shard_map/ppermute | solution.py:956
  202.7 15.9 %collective-permute-start.19 = (bf16[2,2,104,768]{3,2,1,0:T(8,128)(2,1)}, bf16[2,2,104,768]{3,2,1,0:T(8,128)(2,1)S(1)}, u32[]{:S(2)}, u32[]{:S(2)}) collective-permute-start(bf16[2,2,104,768]{3,2,1,0:T(8,128)(2,1)} %get-tuple-element.183), channel_id=1, source_target_pairs={{0,2},{2,0},{4,6},{6,4},{1,3},{3,1},{5,7},{7,5},{8,10},{10,8},{12,... | collective-permute-start | bytes 1916936 | tf_op jit(solution)/shard_map/ppermute | solution.py:956
  221.6 8.4 %collective-permute-start.21 = (bf16[2,104,768]{2,1,0:T(8,128)(2,1)}, bf16[2,104,768]{2,1,0:T(8,128)(2,1)S(1)}, u32[]{:S(2)}, u32[]{:S(2)}) collective-permute-start(bf16[2,104,768]{2,1,0:T(8,128)(2,1)} %get-tuple-element.187), channel_id=1, source_target_pairs={{0,4},{2,6},{4,0},{6,2},{1,5},{3,7},{5,1},{7,3},{8,12},{10,14},{12... | collective-permute-start | bytes 958472 | tf_op jit(solution)/shard_map/ppermute | solution.py:956
  223.1 7.9 %collective-permute-start.22 = (bf16[2,104,768]{2,1,0:T(8,128)(2,1)}, bf16[2,104,768]{2,1,0:T(8,128)(2,1)S(1)}, u32[]{:S(2)}, u32[]{:S(2)}) collective-permute-start(bf16[2,104,768]{2,1,0:T(8,128)(2,1)} %get-tuple-element.189), channel_id=1, source_target_pairs={{0,2},{2,0},{4,6},{6,4},{1,3},{3,1},{5,7},{7,5},{8,10},{10,8},{12,... | collective-permute-start | bytes 958472 | tf_op jit(solution)/shard_map/ppermute | solution.py:956
  223.7 15.1 %collective-permute-start.13 = (bf16[80,768]{1,0:T(8,128)(2,1)S(1)}, bf16[80,768]{1,0:T(8,128)(2,1)S(1)}, u32[]{:S(2)}, u32[]{:S(2)}) collective-permute-start(bf16[80,768]{1,0:T(8,128)(2,1)S(1)} %copy-done.32), channel_id=1, source_target_pairs={{0,8},{8,0},{16,24},{24,16},{1,9},{9,1},{17,25},{25,17},{2,10},{10... | collective-permute-start | bytes 368648 | tf_op jit(solution)/shard_map/ppermute | solution.py:1033
  225.4 17.8 %collective-permute-start.14 = (bf16[80,768]{1,0:T(8,128)(2,1)S(1)}, bf16[80,768]{1,0:T(8,128)(2,1)S(1)}, u32[]{:S(2)}, u32[]{:S(2)}) collective-permute-start(bf16[80,768]{1,0:T(8,128)(2,1)S(1)} %copy-done.31), channel_id=1, source_target_pairs={{0,16},{8,24},{16,0},{24,8},{1,17},{9,25},{17,1},{25,9},{2,18},{10... | collective-permute-start | bytes 368648 | tf_op jit(solution)/shard_map/ppermute | solution.py:1033
  227.7 15.4 %collective-permute-start.15 = (bf16[80,768]{1,0:T(8,128)(2,1)S(1)}, bf16[80,768]{1,0:T(8,128)(2,1)S(1)}, u32[]{:S(2)}, u32[]{:S(2)}) collective-permute-start(bf16[80,768]{1,0:T(8,128)(2,1)S(1)} %copy-done.30), channel_id=1, source_target_pairs={{0,24},{8,16},{16,8},{24,0},{1,25},{9,17},{17,9},{25,1},{2,26},{10... | collective-permute-start | bytes 368648 | tf_op jit(solution)/shard_map/ppermute | solution.py:1033
  235.0 13.9 %collective-permute-start.23 = (bf16[104,768]{1,0:T(8,128)(2,1)}, bf16[104,768]{1,0:T(8,128)(2,1)S(1)}, u32[]{:S(2)}, u32[]{:S(2)}) collective-permute-start(bf16[104,768]{1,0:T(8,128)(2,1)} %get-tuple-element.191), channel_id=1, source_target_pairs={{0,8},{8,0},{16,24},{24,16},{1,9},{9,1},{17,25},{25,17},{2,10},{10... | collective-permute-start | bytes 479240 | tf_op jit(solution)/shard_map/ppermute | solution.py:1033
  236.4 16.3 %collective-permute-start.24 = (bf16[104,768]{1,0:T(8,128)(2,1)}, bf16[104,768]{1,0:T(8,128)(2,1)S(1)}, u32[]{:S(2)}, u32[]{:S(2)}) collective-permute-start(bf16[104,768]{1,0:T(8,128)(2,1)} %get-tuple-element.192), channel_id=1, source_target_pairs={{0,16},{8,24},{16,0},{24,8},{1,17},{9,25},{17,1},{25,9},{2,18},{10... | collective-permute-start | bytes 479240 | tf_op jit(solution)/shard_map/ppermute | solution.py:1033
  238.7 13.9 %collective-permute-start.25 = (bf16[104,768]{1,0:T(8,128)(2,1)}, bf16[104,768]{1,0:T(8,128)(2,1)S(1)}, u32[]{:S(2)}, u32[]{:S(2)}) collective-permute-start(bf16[104,768]{1,0:T(8,128)(2,1)} %get-tuple-element.193), channel_id=1, source_target_pairs={{0,24},{8,16},{16,8},{24,0},{1,25},{9,17},{17,9},{25,1},{2,26},{10... | collective-permute-start | bytes 479240 | tf_op jit(solution)/shard_map/ppermute | solution.py:1033
  (40 other events, 192.6 us)
Sparse Core Ops, SparseCore 0:
  100.7 95.8 reduce-scatter.1

commit v5 on v4

--- a/solution.py
+++ b/solution.py
@@ -256,10 +256,31 @@
 
     rows = e_ref.shape[0]
     at = pl.ds(pl.multiple_of(step * rows, rows), rows)
-    e, o, rinv = softmax_block(qf[at, :], kf[...], vf[...])
-    e_ref[...] = e
-    of[at, :] = o
-    rf[at, :] = jnp.where(low_lanes(rows), jnp.broadcast_to(rinv, (rows, 2 * HD)), 0.0)
+    peak = jnp.max(jnp.abs(kf[...].astype(F32)), axis=0, keepdims=True)
+    bound = jnp.sum(jnp.abs(qf[at, :].astype(F32)) * peak, axis=-1, keepdims=True)
+    small = jnp.max(bound) < SAFE
+
+    @pl.when(small)
+    def _():
+        e, o, rinv = plain_block(qf[at, :], kf[...], vf[...])
+        e_ref[...] = e
+        of[at, :] = o
+        rf[at, :] = jnp.where(low_lanes(rows), jnp.broadcast_to(rinv, (rows, 2 * HD)), 0.0)
+
+    @pl.when(jnp.logical_not(small))
+    def _():
+        part = 32
+
+        def body(i, carry):
+            here = pl.ds(pl.multiple_of(i * part, part), part)
+            there = pl.ds(pl.multiple_of(step * rows + i * part, part), part)
+            e, o, rinv = softmax_block(qf[there, :], kf[...], vf[...])
+            e_ref[here, :] = e
+            of[there, :] = o
+            rf[there, :] = jnp.where(low_lanes(part), jnp.broadcast_to(rinv, (part, 2 * HD)), 0.0)
+            return carry
+
+        lax.fori_loop(0, rows // part, body, 0)
 
     @pl.when(step == pl.num_programs(0) - 1)
     def _():

time: 264 us -> 263 us (level)
  transfers between devices with their start and end apart: 33 -> 33, of which waited for: 10 -> 11; matrix products, arithmetic and copies ran while one was open for 0% -> 0% of each run, Pallas kernels for 36% -> 35%
where the time goes in v5:
time: 263 us; the launch traced here: 262 us
  Pallas kernels  121 us (46%)
  starting transfers between devices  62.3 us (24%)
  waiting for transfers between devices  50.9 us (19%)
  between operations  14.4 us (5%)
  local copies, waits for them, and re-layouts  11.4 us (4%)
    all_to_all x6, starting transfers between devices, over(): return lax.all_to_all(x, axes, 0, 0)  32.3 us
    ppermute x18, starting transfers between devices, exchange(): lax.ppermute(parts[k], axis, pairs(k))  25.9 us
    ppermute x18, waiting for transfers between devices, exchange(): lax.ppermute(parts[k], axis, pairs(k))  25.1 us
    pallas_call x1, Pallas kernels, mid_call(): pl.pallas_call(functools.partial(mid_kernel, nf, nt, fast), grid_spec=plt...  22.9 us
    ppermute x4, waiting for transfers between devices, along(): return lax.ppermute(x, axis, [(i, i ^ k) for i in range(4)])  18.3 us
    pallas_call x1, Pallas kernels, attn_fwd_call(): pl.pallas_call(functools.partial(attn_fwd_kernel, nt), grid=(pairs,), in_...  17.2 us
    pallas_call x1, Pallas kernels, attn_bwd_call(): pl.pallas_call(attn_bwd_kernel, grid=(width // blk,), in_specs=[row, row,...  15.7 us
    pallas_call x1, Pallas kernels, tail5_call(): pl.pallas_call(functools.partial(tail5_kernel, nf, nt, fast), grid_spec=p...  13.5 us
  transfers between devices with their start and end apart: 33, of which 11 were waited for; matrix products, arithmetic and copies ran while one was open for 0% of the time, Pallas kernels for 35%

profile of v5, /device:TPU:0, one launch (start us, length us, event | category | flops | bytes accessed | tf_op | source)
XLA Modules:
  0.0 262.3 jit_solution(14250787956339218603)
XLA Ops:
  7.8 3.0 %pick.1 = (bf16[80,768]{1,0:T(8,128)(2,1)}, bf16[80,768]{1,0:T(8,128)(2,1)}, bf16[80,768]{1,0:T(8,128)(2,1)}, bf16[80,768]{1,0:T(8,128)(2,1)}, f32[16,768]{1,0:T...) custom-call(s32[3]{0:T(128)} %pad_add_fusion.me_ref.refs_0_, ...), custom_call_target="tpu_custom_call" | custom-call | bytes 2457600 | tf_op jit(solution)/shard_map/pick/pallas_call | solution.py:107
  10.8 3.0 %collective-permute-start = (bf16[80,768]{1,0:T(8,128)(2,1)}, bf16[80,768]{1,0:T(8,128)(2,1)S(1)}, u32[]{:S(2)}, u32[]{:S(2)}) collective-permute-start(bf16[80,768]{1,0:T(8,128)(2,1)} %get-tuple-element.113), channel_id=1, source_target_pairs={{0,8},{8,0},{16,24},{24,16},{1,9},{9,1},{17,25},{25,17},{2,10},{10... | collective-permute-start | bytes 368648 | tf_op jit(solution)/shard_map/ppermute | solution.py:1054
  13.8 2.6 collective-permute-start.1
  16.4 3.9 %q_shared.1 = (bf16[80,768]{1,0:T(8,128)(2,1)}, bf16[16,40,384]{2,1,0:T(8,128)(2,1)}) custom-call(bf16[5,80,768]{2,1,0:T(8,128)(2,1)} %refs_9_.1, f32[16,768]{1,0:T(8,128)} %get-tuple-element.121.vec_ref.refs_4_.refs_7_.refs_13_.refs_9_.refs_12_, bf16[768,2304]{1,0:T(8,128)(2,1)} %refs_11_.3), custom_call_target="tpu_custom_call" | custom-call | flops 283115520 | bytes 3538944 | tf_op jit(solution)/shard_map/q_shared/pallas_call | solution.py:198
  20.3 7.1 %all-to-all-start = ((bf16[16,40,384]{2,1,0:T(8,128)(2,1)}), bf16[16,40,384]{2,1,0:T(8,128)(2,1)S(1)}, u32[]{:S(2)}, u32[]{:S(2)}) async-start(bf16[16,40,384]{2,1,0:T(8,128)(2,1)} %get-tuple-element.122), calls=%async_computation | async-start | bytes 983040 | tf_op jit(solution)/shard_map/all_to_all | solution.py:1064
  28.8 2.2 ln_one.1.refs_0_.n0.refs_3_
  31.0 2.8 %collective-permute-start.8 = (bf16[320,768]{1,0:T(8,128)(2,1)}, bf16[320,768]{1,0:T(8,128)(2,1)S(1)}, u32[]{:S(2)}, u32[]{:S(2)}) collective-permute-start(bf16[320,768]{1,0:T(8,128)(2,1)} %ln_one.1.refs_0_.n0.refs_3_), channel_id=1, source_target_pairs={{0,6},{2,4},{4,2},{6,0},{1,7},{3,5},{5,3},{7,1},{8,14},{10,12},{12... | collective-permute-start | bytes 1474568 | tf_op jit(solution)/shard_map/ppermute | solution.py:1054
  34.5 6.8 %all-to-all-done = bf16[16,40,384]{2,1,0:T(8,128)(2,1)S(1)} async-done(((bf16[16,40,384]{2,1,0:T(8,128)(2,1)}), bf16[16,40,384]{2,1,0:T(8,128)(2,1)S(1)}, u32[]{:S(2)}, u32[]{:S(2)}) %all-to-all-start) | async-done | bytes 491552 | tf_op jit(solution)/shard_map/all_to_all | solution.py:1064
  42.1 5.8 %attn_shared_fwd.1 = (f32[640,128]{1,0:T(8,128)}, f32[640,128]{1,0:T(8,128)}, bf16[640,128]{1,0:T(8,128)(2,1)}, bf16[1280,1280]{1,0:T(8,128)(2,1)}) custom-call(bf16[640,384]{1,0:T(8,128)(2,1)} %bitcast.12), custom_call_target="tpu_custom_call" | custom-call | flops 3355443200 | bytes 3276800 | tf_op jit(solution)/shard_map/attn_shared_fwd/pallas_call | solution.py:297
  47.9 3.6 %all-to-all-start.1 = ((bf16[16,40,128]{2,1,0:T(8,128)(2,1)}), bf16[16,40,128]{2,1,0:T(8,128)(2,1)S(1)}, u32[]{:S(2)}, u32[]{:S(2)}) async-start(bf16[16,40,128]{2,1,0:T(8,128)(2,1)} %bitcast.16), calls=%async_computation.1 | async-start | bytes 327680 | tf_op jit(solution)/shard_map/all_to_all | solution.py:1064
  53.7 2.4 collective-permute-start.4
  59.9 17.2 %attn_fwd.1 = (bf16[320,768]{1,0:T(8,128)(2,1)}, f32[320,768]{1,0:T(8,128)}, f32[320,768]{1,0:T(8,128)}, bf16[320,768]{1,0:T(8,128)(2,1)}, bf16[2,1280,768]{2,1,...) custom-call(bf16[320,768]{1,0:T(8,128)(2,1)} %ln_one.1.refs_0_.n0.refs_3_, bf16[320,768]{1,0:T(8,128)(2,1)} %copy-done.9, ...), custom_call_target="tpu_custom_call" | custom-call | flops 50331648 | bytes 209715 | tf_op jit(solution)/shard_map/attn_fwd/pallas_call | solution.py:431
  77.9 22.9 %mid.1 = (bf16[4,80,768]{2,1,0:T(8,128)(2,1)}, f32[80,768]{1,0:T(8,128)}, f32[400,768]{1,0:T(8,128)}, bf16[320,768]{1,0:T(8,128)(2,1)}, bf16[16,40,128]{2,1,0:T(...) custom-call(s32[3]{0:T(128)} %pad_add_fusion.me_ref.refs_0_, ...), custom_call_target="tpu_custom_call" | custom-call | flops 12740198400 | bytes 25165824 | tf_op jit(solution)/shard_map/mid/pallas_call | solution.py:708
  100.9 5.8 %all-to-all-start.2 = ((bf16[16,40,128]{2,1,0:T(8,128)(2,1)}), bf16[16,40,128]{2,1,0:T(8,128)(2,1)S(1)}, u32[]{:S(2)}, u32[]{:S(2)}) async-start(bf16[16,40,128]{2,1,0:T(8,128)(2,1)} %get-tuple-element.138), calls=%async_computation.2 | async-start | bytes 327680 | tf_op jit(solution)/shard_map/all_to_all | solution.py:1064
  106.8 15.7 %attn_bwd.1 = (bf16[320,768]{1,0:T(8,128)(2,1)}, bf16[2,1280,768]{2,1,0:T(8,128)(2,1)}) custom-call(bf16[320,768]{1,0:T(8,128)(2,1)} %get-tuple-element.139.ga_ref, bf16[320,768]{1,0:T(8,128)(2,1)} %get-tuple-element.140.q_ref, bf16[2,1280,768]{2,1,0:T(8,128)(2,1)} %get-tuple-element.141.kv_ref, f32[320,768]{1,0:T(8,128)} %get-tuple-element.142.o_ref, ...), custom_call_target="tpu_custom_call" | custom-call | flops 10066329600 | bytes 25165824 | tf_op jit(solution)/shard_map/attn_bwd/pallas_call | solution.py:483
  123.1 8.0 %attn_shared_bwd.1 = bf16[640,384]{1,0:T(8,128)(2,1)} custom-call(bf16[640,384]{1,0:T(8,128)(2,1)} %bitcast.13, bf16[640,128]{1,0:T(8,128)(2,1)} %bitcast.17, f32[640,128]{1,0:T(8,128)} %get-tuple-element.148.o_ref, f32[640,128]{1,0:T(8,128)} %get-tuple-element.149.r_ref, bf16[1280,1280]{1,0:T(8,128)(2,1)} %get-tuple-element.150.e_ref), custom_call_target="tpu_custom_call" | custom-call | flops 6710886400 | bytes 3276800 | tf_op jit(solution)/shard_map/attn_shared_bwd/pallas_call | solution.py:349
  131.1 6.9 %all-to-all-start.3 = ((bf16[16,40,384]{2,1,0:T(8,128)(2,1)}), bf16[16,40,384]{2,1,0:T(8,128)(2,1)S(1)}, u32[]{:S(2)}, u32[]{:S(2)}) async-start(bf16[16,40,384]{2,1,0:T(8,128)(2,1)} %bitcast.14), calls=%async_computation.3 | async-start | bytes 983040 | tf_op jit(solution)/shard_map/all_to_all | solution.py:1064
  138.0 10.7 %dx.1 = (f32[320,768]{1,0:T(8,128)}, bf16[320,768]{1,0:T(8,128)(2,1)}, bf16[320,768]{1,0:T(8,128)(2,1)}, bf16[320,768]{1,0:T(8,128)(2,1)}, f32[2,768]{1,0:T(2,128)}) custom-call(bf16[320,768]{1,0:T(8,128)(2,1)} %get-tuple-element.169.gq_ref.refs_1_, bf16[2,1280,768]{2,1,0:T(8,128)(2,1)} %get-tuple-element.154.gkv_ref.refs_2_, ...), custom_call_target="tpu_custom_call" | custom-call | flops 3019898880 | bytes 12582912 | tf_op jit(solution)/shard_map/dx/pallas_call | solution.py:552
  153.7 13.5 %tail_shared.1 = (bf16[4,4,32,768]{3,2,1,0:T(8,128)(2,1)}, bf16[4,4,32,768]{3,2,1,0:T(8,128)(2,1)}, bf16[4,4,24,768]{3,2,1,0:T(8,128)(2,1)}, bf16[4,4,24,768]{3,...) custom-call(s32[3]{0:T(128)} %pad_add_fusion.me_ref.refs_0_, ...), custom_call_target="tpu_custom_call" | custom-call | flops 3586129920 | bytes 16777216 | tf_op jit(solution)/shard_map/tail_shared/pallas_call | solution.py:851
  167.2 4.3 %all-to-all-start.4 = ((bf16[4,80,768]{2,1,0:T(8,128)(2,1)}), bf16[4,80,768]{2,1,0:T(8,128)(2,1)S(1)}, u32[]{:S(2)}, u32[]{:S(2)}) async-start(bf16[4,80,768]{2,1,0:T(8,128)(2,1)} %get-tuple-element.151), calls=%async_computation.4 | async-start | bytes 983040 | tf_op jit(solution)/shard_map/all_to_all | solution.py:1064
  171.5 14.6 %collective-permute-done.12.refs_3_ = bf16[320,768]{1,0:T(8,128)(2,1)S(1)} collective-permute-done((bf16[320,768]{1,0:T(8,128)(2,1)}, bf16[320,768]{1,0:T(8,128)(2,1)S(1)}, u32[]{:S(2)}, u32[]{:S(2)}) %collective-permute-start.12) | collective-permute-done | bytes 491552 | tf_op jit(solution)/shard_map/ppermute | solution.py:1054
  187.5 3.6 %tail.1 = (bf16[80,768]{1,0:T(8,128)(2,1)}, bf16[80,768]{1,0:T(8,128)(2,1)}, bf16[80,768]{1,0:T(8,128)(2,1)}, bf16[80,768]{1,0:T(8,128)(2,1)}) custom-call(f32[320,768]{1,0:T(8,128)} %get-tuple-element.159.refs_0_, bf16[320,768]{1,0:T(8,128)(2,1)} %copy-done.24, bf16[320,768]{1,0:T(8,128)(2,1)} %copy-done.25, bf16[320,768]{1,0:T(8,128)(2,1)} %copy-done.26, ...), custom_call_target="tpu_custom_call" | custom-call | flops 7372800000 | bytes 6291456000 | tf_op jit(solution)/shard_map/tail/pallas_call | solution.py:899
  192.4 3.9 %pair_sum.1 = (bf16[2,2,104,768]{3,2,1,0:T(8,128)(2,1)}, bf16[2,104,768]{2,1,0:T(8,128)(2,1)}, bf16[2,104,768]{2,1,0:T(8,128)(2,1)}, bf16[2,2,104,768]{3,2,1,0:T...) custom-call(bf16[4,4,32,768]{3,2,1,0:T(8,128)(2,1)} %get-tuple-element.174.refs_0_.refs_8_, ...), custom_call_target="tpu_custom_call" | custom-call | flops 1048576 | bytes 8388608 | tf_op jit(solution)/shard_map/pair_sum/pallas_call | solution.py:940
  196.4 4.7 %all-to-all-start.5 = ((bf16[4,192,768]{2,1,0:T(8,128)(2,1)}), bf16[4,192,768]{2,1,0:T(8,128)(2,1)S(1)}, u32[]{:S(2)}, u32[]{:S(2)}) async-start(bf16[4,192,768]{2,1,0:T(8,128)(2,1)} %bitcast.11), calls=%async_computation.6 | async-start | bytes 2359296 | tf_op jit(solution)/shard_map/all_to_all | solution.py:1064
  202.3 15.1 %collective-permute-done.20.gy.refs_4_ = bf16[2,2,104,768]{3,2,1,0:T(8,128)(2,1)S(1)} collective-permute-done((bf16[2,2,104,768]{3,2,1,0:T(8,128)(2,1)}, bf16[2,2,104,768]{3,2,1,0:T(8,128)(2,1)S(1)}, u32[]{:S(2)}, u32[]{:S(2)}) %collective-permute-start.20) | collective-permute-done | bytes 639008 | tf_op jit(solution)/shard_map/ppermute | solution.py:977
  224.4 2.4 collective-permute-start.14
  230.7 3.3 %tm_sum.1 = (bf16[104,768]{1,0:T(8,128)(2,1)}, bf16[104,768]{1,0:T(8,128)(2,1)}, bf16[104,768]{1,0:T(8,128)(2,1)}, bf16[104,768]{1,0:T(8,128)(2,1)}) custom-call(s32[3]{0:T(128)} %pad_add_fusion.me_ref.refs_0_, bf16[2,104,768]{2,1,0:T(8,128)(2,1)} %get-tuple-element.182.refs_0_, bf16[2,2,104,768]{3,2,1,0:T(8,128)(2,1)} %copy-done.3, ...), custom_call_target="tpu_custom_call" | custom-call | flops 1048576 | bytes 5242880 | tf_op jit(solution)/shard_map/tm_sum/pallas_call | solution.py:1004
  235.4 2.4 collective-permute-start.24
  238.4 3.8 %collective-permute-done.14.refs_2_ = bf16[80,768]{1,0:T(8,128)(2,1)S(1)} collective-permute-done((bf16[80,768]{1,0:T(8,128)(2,1)S(1)}, bf16[80,768]{1,0:T(8,128)(2,1)S(1)}, u32[]{:S(2)}, u32[]{:S(2)}) %collective-permute-start.14) | collective-permute-done | bytes 122912 | tf_op jit(solution)/shard_map/ppermute | solution.py:1054
  242.9 3.0 %assemble.1 = f32[5,80,768]{2,1,0:T(8,128)} custom-call(s32[3]{0:T(128)} %pad_add_fusion.me_ref.refs_0_, bf16[80,768]{1,0:T(8,128)(2,1)} %get-tuple-element.164.refs_0_, bf16[80,768]{1,0:T(8,128)(2,1)} %copy-done.20, bf16[80,768]{1,0:T(8,128)(2,1)} %copy-done.21, bf16[80,768]{1,0:T(8,128)(2,1)} %copy-done.22, f32[80,768]{1,0:T(8,128)} %get-tuple-element.173.refs_4_), custom_call_target="tpu_custom_call" | custom-call | bytes 2457600 | tf_op jit(solution)/shard_map/assemble/pallas_call | solution.py:134
  248.0 3.7 %collective-permute-done.24.refs_2_ = bf16[104,768]{1,0:T(8,128)(2,1)S(1)} collective-permute-done((bf16[104,768]{1,0:T(8,128)(2,1)}, bf16[104,768]{1,0:T(8,128)(2,1)S(1)}, u32[]{:S(2)}, u32[]{:S(2)}) %collective-permute-start.24) | collective-permute-done | bytes 159776 | tf_op jit(solution)/shard_map/ppermute | solution.py:1054
  252.8 2.6 last_sum.1
  (132 shorter events, 36.6 us)
Async XLA Ops:
  10.8 16.6 %collective-permute-start = (bf16[80,768]{1,0:T(8,128)(2,1)}, bf16[80,768]{1,0:T(8,128)(2,1)S(1)}, u32[]{:S(2)}, u32[]{:S(2)}) collective-permute-start(bf16[80,768]{1,0:T(8,128)(2,1)} %get-tuple-element.113), channel_id=1, source_target_pairs={{0,8},{8,0},{16,24},{24,16},{1,9},{9,1},{17,25},{25,17},{2,10},{10... | collective-permute-start | bytes 368648 | tf_op jit(solution)/shard_map/ppermute | solution.py:1054
  13.8 13.6 %collective-permute-start.1 = (bf16[80,768]{1,0:T(8,128)(2,1)}, bf16[80,768]{1,0:T(8,128)(2,1)S(1)}, u32[]{:S(2)}, u32[]{:S(2)}) collective-permute-start(bf16[80,768]{1,0:T(8,128)(2,1)} %get-tuple-element.114), channel_id=1, source_target_pairs={{0,16},{8,24},{16,0},{24,8},{1,17},{9,25},{17,1},{25,9},{2,18},{10... | collective-permute-start | bytes 368648 | tf_op jit(solution)/shard_map/ppermute | solution.py:1054
  16.4 11.0 %collective-permute-start.2 = (bf16[80,768]{1,0:T(8,128)(2,1)}, bf16[80,768]{1,0:T(8,128)(2,1)S(1)}, u32[]{:S(2)}, u32[]{:S(2)}) collective-permute-start(bf16[80,768]{1,0:T(8,128)(2,1)} %get-tuple-element.115), channel_id=1, source_target_pairs={{0,24},{8,16},{16,8},{24,0},{1,25},{9,17},{17,9},{25,1},{2,26},{10... | collective-permute-start | bytes 368648 | tf_op jit(solution)/shard_map/ppermute | solution.py:1054
  20.3 21.0 %all-to-all-start = ((bf16[16,40,384]{2,1,0:T(8,128)(2,1)}), bf16[16,40,384]{2,1,0:T(8,128)(2,1)S(1)}, u32[]{:S(2)}, u32[]{:S(2)}) async-start(bf16[16,40,384]{2,1,0:T(8,128)(2,1)} %get-tuple-element.122), calls=%async_computation | async-start | bytes 983040 | tf_op jit(solution)/shard_map/all_to_all | solution.py:1064
  31.0 25.1 %collective-permute-start.8 = (bf16[320,768]{1,0:T(8,128)(2,1)}, bf16[320,768]{1,0:T(8,128)(2,1)S(1)}, u32[]{:S(2)}, u32[]{:S(2)}) collective-permute-start(bf16[320,768]{1,0:T(8,128)(2,1)} %ln_one.1.refs_0_.n0.refs_3_), channel_id=1, source_target_pairs={{0,6},{2,4},{4,2},{6,0},{1,7},{3,5},{5,3},{7,1},{8,14},{10,12},{12... | collective-permute-start | bytes 1474568 | tf_op jit(solution)/shard_map/ppermute | solution.py:1054
  33.9 24.4 %collective-permute-start.7 = (bf16[320,768]{1,0:T(8,128)(2,1)}, bf16[320,768]{1,0:T(8,128)(2,1)S(1)}, u32[]{:S(2)}, u32[]{:S(2)}) collective-permute-start(bf16[320,768]{1,0:T(8,128)(2,1)} %ln_one.1.refs_0_.n0.refs_3_), channel_id=1, source_target_pairs={{0,4},{2,6},{4,0},{6,2},{1,5},{3,7},{5,1},{7,3},{8,12},{10,14},{12... | collective-permute-start | bytes 1474568 | tf_op jit(solution)/shard_map/ppermute | solution.py:1054
  34.4 24.7 %collective-permute-start.6 = (bf16[320,768]{1,0:T(8,128)(2,1)}, bf16[320,768]{1,0:T(8,128)(2,1)S(1)}, u32[]{:S(2)}, u32[]{:S(2)}) collective-permute-start(bf16[320,768]{1,0:T(8,128)(2,1)} %ln_one.1.refs_0_.n0.refs_3_), channel_id=1, source_target_pairs={{0,2},{2,0},{4,6},{6,4},{1,3},{3,1},{5,7},{7,5},{8,10},{10,8},{12,... | collective-permute-start | bytes 1474568 | tf_op jit(solution)/shard_map/ppermute | solution.py:1054
  47.9 29.3 %all-to-all-start.1 = ((bf16[16,40,128]{2,1,0:T(8,128)(2,1)}), bf16[16,40,128]{2,1,0:T(8,128)(2,1)S(1)}, u32[]{:S(2)}, u32[]{:S(2)}) async-start(bf16[16,40,128]{2,1,0:T(8,128)(2,1)} %bitcast.16), calls=%async_computation.1 | async-start | bytes 327680 | tf_op jit(solution)/shard_map/all_to_all | solution.py:1064
  51.5 144.8 %reduce-scatter.2.cloned.1.call-start = ((), (), s32[]{:S(2)}) async-start(), calls=%async_computation.7 | async-start | bytes 10616832 | tf_op jit(solution)/shard_map/reduce_scatter | solution.py:1130
  51.7 25.4 %collective-permute-start.3 = (bf16[80,768]{1,0:T(8,128)(2,1)S(1)}, bf16[80,768]{1,0:T(8,128)(2,1)S(1)}, u32[]{:S(2)}, u32[]{:S(2)}) collective-permute-start(bf16[80,768]{1,0:T(8,128)(2,1)S(1)} %copy-done.35), channel_id=1, source_target_pairs={{0,8},{8,0},{16,24},{24,16},{1,9},{9,1},{17,25},{25,17},{2,10},{10... | collective-permute-start | bytes 368648 | tf_op jit(solution)/shard_map/ppermute | solution.py:1054
  53.7 23.4 %collective-permute-start.4 = (bf16[80,768]{1,0:T(8,128)(2,1)S(1)}, bf16[80,768]{1,0:T(8,128)(2,1)S(1)}, u32[]{:S(2)}, u32[]{:S(2)}) collective-permute-start(bf16[80,768]{1,0:T(8,128)(2,1)S(1)} %copy-done.34), channel_id=1, source_target_pairs={{0,16},{8,24},{16,0},{24,8},{1,17},{9,25},{17,1},{25,9},{2,18},{10... | collective-permute-start | bytes 368648 | tf_op jit(solution)/shard_map/ppermute | solution.py:1054
  56.1 21.1 %collective-permute-start.5 = (bf16[80,768]{1,0:T(8,128)(2,1)S(1)}, bf16[80,768]{1,0:T(8,128)(2,1)S(1)}, u32[]{:S(2)}, u32[]{:S(2)}) collective-permute-start(bf16[80,768]{1,0:T(8,128)(2,1)S(1)} %copy-done.33), channel_id=1, source_target_pairs={{0,24},{8,16},{16,8},{24,0},{1,25},{9,17},{17,9},{25,1},{2,26},{10... | collective-permute-start | bytes 368648 | tf_op jit(solution)/shard_map/ppermute | solution.py:1054
  100.9 21.5 %all-to-all-start.2 = ((bf16[16,40,128]{2,1,0:T(8,128)(2,1)}), bf16[16,40,128]{2,1,0:T(8,128)(2,1)S(1)}, u32[]{:S(2)}, u32[]{:S(2)}) async-start(bf16[16,40,128]{2,1,0:T(8,128)(2,1)} %get-tuple-element.138), calls=%async_computation.2 | async-start | bytes 327680 | tf_op jit(solution)/shard_map/all_to_all | solution.py:1064
  106.7 15.8 %collective-permute-start.9 = (bf16[4,4,24,768]{3,2,1,0:T(8,128)(2,1)S(1)}, bf16[4,4,24,768]{3,2,1,0:T(8,128)(2,1)S(1)}, u32[]{:S(2)}, u32[]{:S(2)}) collective-permute-start(bf16[4,4,24,768]{3,2,1,0:T(8,128)(2,1)S(1)} %copy-done.23), channel_id=1, source_target_pairs={{0,1},{1,0},{2,3},{3,2},{4,5},{5,4},{6,7},{7,6},{8,9},{9,8},{10,11... | collective-permute-start | bytes 1769480 | tf_op jit(solution)/shard_map/ppermute | solution.py:1049
  131.1 21.8 %all-to-all-start.3 = ((bf16[16,40,384]{2,1,0:T(8,128)(2,1)}), bf16[16,40,384]{2,1,0:T(8,128)(2,1)S(1)}, u32[]{:S(2)}, u32[]{:S(2)}) async-start(bf16[16,40,384]{2,1,0:T(8,128)(2,1)} %bitcast.14), calls=%async_computation.3 | async-start | bytes 983040 | tf_op jit(solution)/shard_map/all_to_all | solution.py:1064
  148.7 22.9 %collective-permute-start.10 = (bf16[320,768]{1,0:T(8,128)(2,1)}, bf16[320,768]{1,0:T(8,128)(2,1)S(1)}, u32[]{:S(2)}, u32[]{:S(2)}) collective-permute-start(bf16[320,768]{1,0:T(8,128)(2,1)} %get-tuple-element.156), channel_id=1, source_target_pairs={{0,2},{2,0},{4,6},{6,4},{1,3},{3,1},{5,7},{7,5},{8,10},{10,8},{12,... | collective-permute-start | bytes 1474568 | tf_op jit(solution)/shard_map/ppermute | solution.py:1054
  150.6 20.9 %collective-permute-start.11 = (bf16[320,768]{1,0:T(8,128)(2,1)}, bf16[320,768]{1,0:T(8,128)(2,1)S(1)}, u32[]{:S(2)}, u32[]{:S(2)}) collective-permute-start(bf16[320,768]{1,0:T(8,128)(2,1)} %get-tuple-element.157), channel_id=1, source_target_pairs={{0,4},{2,6},{4,0},{6,2},{1,5},{3,7},{5,1},{7,3},{8,12},{10,14},{12... | collective-permute-start | bytes 1474568 | tf_op jit(solution)/shard_map/ppermute | solution.py:1054
  152.0 34.1 %collective-permute-start.12 = (bf16[320,768]{1,0:T(8,128)(2,1)}, bf16[320,768]{1,0:T(8,128)(2,1)S(1)}, u32[]{:S(2)}, u32[]{:S(2)}) collective-permute-start(bf16[320,768]{1,0:T(8,128)(2,1)} %get-tuple-element.158), channel_id=1, source_target_pairs={{0,6},{2,4},{4,2},{6,0},{1,7},{3,5},{5,3},{7,1},{8,14},{10,12},{12... | collective-permute-start | bytes 1474568 | tf_op jit(solution)/shard_map/ppermute | solution.py:1054
  167.2 23.9 %collective-permute-start.16 = (bf16[4,4,32,768]{3,2,1,0:T(8,128)(2,1)}, bf16[4,4,32,768]{3,2,1,0:T(8,128)(2,1)S(1)}, u32[]{:S(2)}, u32[]{:S(2)}) collective-permute-start(bf16[4,4,32,768]{3,2,1,0:T(8,128)(2,1)} %get-tuple-element.175), channel_id=1, source_target_pairs={{0,1},{1,0},{2,3},{3,2},{4,5},{5,4},{6,7},{7,6},{8,9},{9,8},{10,11... | collective-permute-start | bytes 2359304 | tf_op jit(solution)/shard_map/ppermute | solution.py:1049
  167.2 29.1 %all-to-all-start.4 = ((bf16[4,80,768]{2,1,0:T(8,128)(2,1)}), bf16[4,80,768]{2,1,0:T(8,128)(2,1)S(1)}, u32[]{:S(2)}, u32[]{:S(2)}) async-start(bf16[4,80,768]{2,1,0:T(8,128)(2,1)} %get-tuple-element.151), calls=%async_computation.4 | async-start | bytes 983040 | tf_op jit(solution)/shard_map/all_to_all | solution.py:1064
  187.0 4.2 %collective-permute-start.18 = (bf16[4,4,24,768]{3,2,1,0:T(8,128)(2,1)}, bf16[4,4,24,768]{3,2,1,0:T(8,128)(2,1)S(1)}, u32[]{:S(2)}, u32[]{:S(2)}) collective-permute-start(bf16[4,4,24,768]{3,2,1,0:T(8,128)(2,1)} %get-tuple-element.180), channel_id=1, source_target_pairs={{0,1},{1,0},{2,3},{3,2},{4,5},{5,4},{6,7},{7,6},{8,9},{9,8},{10,11... | collective-permute-start | bytes 1769480 | tf_op jit(solution)/shard_map/ppermute | solution.py:1049
  196.4 55.4 %all-to-all-start.5 = ((bf16[4,192,768]{2,1,0:T(8,128)(2,1)}), bf16[4,192,768]{2,1,0:T(8,128)(2,1)S(1)}, u32[]{:S(2)}, u32[]{:S(2)}) async-start(bf16[4,192,768]{2,1,0:T(8,128)(2,1)} %bitcast.11), calls=%async_computation.6 | async-start | bytes 2359296 | tf_op jit(solution)/shard_map/all_to_all | solution.py:1064
  201.1 16.3 %collective-permute-start.20 = (bf16[2,2,104,768]{3,2,1,0:T(8,128)(2,1)}, bf16[2,2,104,768]{3,2,1,0:T(8,128)(2,1)S(1)}, u32[]{:S(2)}, u32[]{:S(2)}) collective-permute-start(bf16[2,2,104,768]{3,2,1,0:T(8,128)(2,1)} %get-tuple-element.186), channel_id=1, source_target_pairs={{0,4},{2,6},{4,0},{6,2},{1,5},{3,7},{5,1},{7,3},{8,12},{10,14},{12... | collective-permute-start | bytes 1916936 | tf_op jit(solution)/shard_map/ppermute | solution.py:977
  201.7 15.9 %collective-permute-start.19 = (bf16[2,2,104,768]{3,2,1,0:T(8,128)(2,1)}, bf16[2,2,104,768]{3,2,1,0:T(8,128)(2,1)S(1)}, u32[]{:S(2)}, u32[]{:S(2)}) collective-permute-start(bf16[2,2,104,768]{3,2,1,0:T(8,128)(2,1)} %get-tuple-element.183), channel_id=1, source_target_pairs={{0,2},{2,0},{4,6},{6,4},{1,3},{3,1},{5,7},{7,5},{8,10},{10,8},{12,... | collective-permute-start | bytes 1916936 | tf_op jit(solution)/shard_map/ppermute | solution.py:977
  220.6 8.4 %collective-permute-start.21 = (bf16[2,104,768]{2,1,0:T(8,128)(2,1)}, bf16[2,104,768]{2,1,0:T(8,128)(2,1)S(1)}, u32[]{:S(2)}, u32[]{:S(2)}) collective-permute-start(bf16[2,104,768]{2,1,0:T(8,128)(2,1)} %get-tuple-element.187), channel_id=1, source_target_pairs={{0,4},{2,6},{4,0},{6,2},{1,5},{3,7},{5,1},{7,3},{8,12},{10,14},{12... | collective-permute-start | bytes 958472 | tf_op jit(solution)/shard_map/ppermute | solution.py:977
  222.1 7.9 %collective-permute-start.22 = (bf16[2,104,768]{2,1,0:T(8,128)(2,1)}, bf16[2,104,768]{2,1,0:T(8,128)(2,1)S(1)}, u32[]{:S(2)}, u32[]{:S(2)}) collective-permute-start(bf16[2,104,768]{2,1,0:T(8,128)(2,1)} %get-tuple-element.189), channel_id=1, source_target_pairs={{0,2},{2,0},{4,6},{6,4},{1,3},{3,1},{5,7},{7,5},{8,10},{10,8},{12,... | collective-permute-start | bytes 958472 | tf_op jit(solution)/shard_map/ppermute | solution.py:977
  222.7 15.1 %collective-permute-start.13 = (bf16[80,768]{1,0:T(8,128)(2,1)S(1)}, bf16[80,768]{1,0:T(8,128)(2,1)S(1)}, u32[]{:S(2)}, u32[]{:S(2)}) collective-permute-start(bf16[80,768]{1,0:T(8,128)(2,1)S(1)} %copy-done.32), channel_id=1, source_target_pairs={{0,8},{8,0},{16,24},{24,16},{1,9},{9,1},{17,25},{25,17},{2,10},{10... | collective-permute-start | bytes 368648 | tf_op jit(solution)/shard_map/ppermute | solution.py:1054
  224.4 17.8 %collective-permute-start.14 = (bf16[80,768]{1,0:T(8,128)(2,1)S(1)}, bf16[80,768]{1,0:T(8,128)(2,1)S(1)}, u32[]{:S(2)}, u32[]{:S(2)}) collective-permute-start(bf16[80,768]{1,0:T(8,128)(2,1)S(1)} %copy-done.31), channel_id=1, source_target_pairs={{0,16},{8,24},{16,0},{24,8},{1,17},{9,25},{17,1},{25,9},{2,18},{10... | collective-permute-start | bytes 368648 | tf_op jit(solution)/shard_map/ppermute | solution.py:1054
  226.8 15.5 %collective-permute-start.15 = (bf16[80,768]{1,0:T(8,128)(2,1)S(1)}, bf16[80,768]{1,0:T(8,128)(2,1)S(1)}, u32[]{:S(2)}, u32[]{:S(2)}) collective-permute-start(bf16[80,768]{1,0:T(8,128)(2,1)S(1)} %copy-done.30), channel_id=1, source_target_pairs={{0,24},{8,16},{16,8},{24,0},{1,25},{9,17},{17,9},{25,1},{2,26},{10... | collective-permute-start | bytes 368648 | tf_op jit(solution)/shard_map/ppermute | solution.py:1054
  234.0 13.9 %collective-permute-start.23 = (bf16[104,768]{1,0:T(8,128)(2,1)}, bf16[104,768]{1,0:T(8,128)(2,1)S(1)}, u32[]{:S(2)}, u32[]{:S(2)}) collective-permute-start(bf16[104,768]{1,0:T(8,128)(2,1)} %get-tuple-element.191), channel_id=1, source_target_pairs={{0,8},{8,0},{16,24},{24,16},{1,9},{9,1},{17,25},{25,17},{2,10},{10... | collective-permute-start | bytes 479240 | tf_op jit(solution)/shard_map/ppermute | solution.py:1054
  235.4 16.3 %collective-permute-start.24 = (bf16[104,768]{1,0:T(8,128)(2,1)}, bf16[104,768]{1,0:T(8,128)(2,1)S(1)}, u32[]{:S(2)}, u32[]{:S(2)}) collective-permute-start(bf16[104,768]{1,0:T(8,128)(2,1)} %get-tuple-element.192), channel_id=1, source_target_pairs={{0,16},{8,24},{16,0},{24,8},{1,17},{9,25},{17,1},{25,9},{2,18},{10... | collective-permute-start | bytes 479240 | tf_op jit(solution)/shard_map/ppermute | solution.py:1054
  237.8 13.9 %collective-permute-start.25 = (bf16[104,768]{1,0:T(8,128)(2,1)}, bf16[104,768]{1,0:T(8,128)(2,1)S(1)}, u32[]{:S(2)}, u32[]{:S(2)}) collective-permute-start(bf16[104,768]{1,0:T(8,128)(2,1)} %get-tuple-element.193), channel_id=1, source_target_pairs={{0,24},{8,16},{16,8},{24,0},{1,25},{9,17},{17,9},{25,1},{2,26},{10... | collective-permute-start | bytes 479240 | tf_op jit(solution)/shard_map/ppermute | solution.py:1054
  (40 other events, 188.4 us)
Sparse Core Ops, SparseCore 0:
  101.0 94.6 reduce-scatter.1
